TPU v7x, 128 devices: a whole 4x4x4 slice. The times are simulated.
128 devices in a mesh: seq: 32 (over x, z, y_lo), head: 4 (over y_hi, core).
Axes of the slice: x: 4, y: 4 (y_hi: 2, y_lo: 2; y = y_hi * 2 + y_lo), z: 4, core: 2. Of those that a mesh axis runs over, the one named last changes fastest.
Arguments:
- query: bfloat16 [65536, 1024], P('seq', 'head'), may hold values from -9 to 9
- key: bfloat16 [65536, 1024], P('seq', 'head'), may hold values from -9 to 9
- value: bfloat16 [65536, 1024], P('seq', 'head'), may hold values from -6 to 6
- offsets: int32 [5, 16], P(None, 'head'), may hold values from 0 to 63, as said below
Outputs:
- attended: bfloat16 [65536, 1024], P('seq', 'head')
Inputs may be any that keep to these rules, and one draw needn't show every extreme that they name: offsets[0, h] is 0; offsets[l, h] lies below the rate of level l: 1, 4, 4, 16, 64; at every level some head takes the largest value.
All inputs are finite; a program needn't handle non-finite values.
Results may differ from a plain program's by a relative error of at most 0.0046.
Values may be sent and summed in bfloat16 or wider, within the bound.
No kernel may reach another device: no remote copies, remote signals or barrier semaphores. Data moves between devices by JAX's collectives and lax.ppermute only.
A program may use at most 320 MiB of HBM per device.

v0:
```python
import jax
import jax.numpy as jnp
from jax import lax
from jax.experimental import pallas as pl
from jax.experimental.pallas import tpu as pltpu
from jax.sharding import PartitionSpec as P

SEG = 512
RATE1 = 4
bf16 = jnp.bfloat16
f32 = jnp.float32
LANES = 128
HALF = 64
VMEM = pltpu.VMEM


def dot_nt(a, b):
    return lax.dot_general(a, b, (((1,), (1,)), ((), ())), preferred_element_type=f32)


def dot_nn(a, b):
    return lax.dot_general(a, b, (((1,), (0,)), ((), ())), preferred_element_type=f32)


def half_mask(rows, half):
    lane = lax.broadcasted_iota(jnp.int32, (rows, LANES), 1)
    return lax.div(lane, HALF) == half


def swap_halves(x):
    return pltpu.roll(x, HALF, 1)


def softmax_tile(q, keys, values, vl):
    scores = [dot_nt(q, k) for k in keys]
    top = scores[0].max(axis=1, keepdims=True)
    for s in scores[1:]:
        top = jnp.maximum(top, s.max(axis=1, keepdims=True))
    acc = None
    for s, v in zip(scores, values):
        part = dot_nn(jnp.exp(s - top).astype(bf16), v)
        acc = part if acc is None else acc + part
    return jnp.where(vl, acc / swap_halves(acc), top + jnp.log(acc))


def merge(vl, one, lse_one, two, lse_two):
    gap = lse_two - lse_one
    small = jnp.exp(-jnp.abs(gap))
    ahead = gap > 0.0
    big_out = jnp.where(ahead, two, one)
    small_out = jnp.where(ahead, one, two)
    weight = 1.0 + small
    out = (big_out + small * small_out) / weight
    return jnp.where(vl, out, jnp.maximum(lse_one, lse_two) + jnp.log(weight))


def spread_lse(tile, vl):
    return jnp.where(vl, swap_halves(tile), tile)


def encode(tile, vl, half):
    lane = lax.broadcasted_iota(jnp.int32, tile.shape, 1)
    spot = lax.rem(lane, HALF)
    first = tile.astype(bf16).astype(f32)
    rest = tile - first
    second = rest.astype(bf16).astype(f32)
    third = rest - second
    coded = jnp.where(spot == 0, first, jnp.where(spot == 1, second, third))
    return jnp.where(vl, tile, coded).astype(bf16)


def decode_lse(coded, half):
    row = lax.broadcasted_iota(jnp.int32, (LANES, LANES), 0)
    pick = jnp.logical_and(lax.div(row, HALF) != half, lax.rem(row, HALF) < 3)
    return dot_nn(coded, jnp.where(pick, 1.0, 0.0).astype(bf16))


def widen(src, dst):
    rows = src.shape[0]
    step = min(rows, 512)

    @pl.loop(0, rows // step)
    def _(i):
        part = pl.ds(pl.multiple_of(i * step, step), step)
        for p in range(src.shape[1] // LANES):
            dst[p, part, :] = src[part, p * LANES : (p + 1) * LANES].astype(f32)


def pack_kernel(levels, offs, q_ref, k_ref, v_ref, *rest):
    near_out, far_out, (qs, ks, vs) = rest[0:4], rest[4:8], rest[8:11]
    mine = lax.rem(lax.axis_index("seq"), 4)
    widen(q_ref, qs)
    widen(k_ref, ks)
    widen(v_ref, vs)
    for d in range(4):
        head = mine ^ d
        pair, half = lax.div(head, 2), lax.rem(head, 2)
        base = [0, 0]
        for what in ("kv", "q"):
            for index, (level, count, rate, near) in enumerate(levels):
                off = offs[level, head]
                ref = near_out[d] if near else far_out[d]
                at = base[near]
                if what == "kv":
                    vl = half_mask(count, half)
                    k = ks[pair, pl.ds(off, count, rate), :]
                    v = vs[pair, pl.ds(off, count, rate), :]
                    ref[at : at + count, :] = jnp.where(vl, v, swap_halves(k)).astype(bf16)
                    base[near] = at + count
                else:
                    few = count // 2
                    vl = half_mask(few, half)
                    q_one = qs[pair, pl.ds(off, few, rate), :]
                    q_two = qs[pair, pl.ds(off + few * rate, few, rate), :]
                    tile = jnp.where(vl, q_two, swap_halves(q_one))
                    ref[at : at + few, :] = (tile * 0.125).astype(bf16)
                    base[near] = at + few


def local_kernel(rate, offs, q_ref, k_ref, v_ref, t_ref, qs, ks, vs):
    rows = q_ref.shape[0]
    count = rows // rate
    zero, one = jnp.asarray(0, bf16), jnp.asarray(1, bf16)
    scale = jnp.asarray(0.125, bf16)

    @pl.loop(0, rows // SEG)
    def _(s):
        part = pl.ds(pl.multiple_of(s * SEG, SEG), SEG)
        for h in range(4):
            cols = slice(h // 2 * LANES, (h // 2 + 1) * LANES)
            vl = half_mask(SEG, h % 2)
            q = q_ref[part, cols] * scale
            k = jnp.where(vl, k_ref[part, cols], zero)
            v = jnp.where(vl, v_ref[part, cols], one)
            t_ref[h, part, :] = softmax_tile(q, [k], [v], vl)

    widen(q_ref, qs)
    widen(k_ref, ks)
    widen(v_ref, vs)
    for h in range(4):
        off = offs[1, h]
        vl = half_mask(count, h % 2)
        picked = pl.ds(off, count, rate)
        q = (qs[h // 2, picked, :] * 0.125).astype(bf16)
        k = jnp.where(vl, ks[h // 2, picked, :], 0.0).astype(bf16)
        v = jnp.where(vl, vs[h // 2, picked, :], 1.0).astype(bf16)
        new = softmax_tile(q, [k], [v], vl)
        old = t_ref[h, picked, :]
        t_ref[h, picked, :] = merge(vl, old, spread_lse(old, vl), new, spread_lse(new, vl))


def keys_values(tile, half):
    vl = half_mask(tile.shape[0], half)
    zero, one = jnp.asarray(0, bf16), jnp.asarray(1, bf16)
    return jnp.where(vl, zero, tile), jnp.where(vl, tile, one)


def near_kernel(count, *refs):
    ins, outs = refs[:4], refs[4:]
    half = lax.rem(lax.axis_index("seq"), 2)
    keys, values = zip(*[keys_values(r[:count, :], half) for r in ins])
    few = count // 2
    vl = half_mask(few, half)
    for d in range(4):
        tile = ins[d][count : count + few, :]
        for part in range(2):
            q = tile if part == 0 else swap_halves(tile.astype(f32)).astype(bf16)
            found = softmax_tile(q, keys, values, vl)
            outs[d][part * few : (part + 1) * few, :] = encode(found, vl, half)


def far_kernel(mid, top, *refs):
    far, gathered, outs = refs[:4], refs[4:8], refs[8:12]
    half = lax.rem(lax.axis_index("seq"), 2)
    base = mid + top
    blocks = (
        (0, 4 * mid, base, mid // 2, 0),
        (4 * mid, gathered[0].shape[0] - 4 * mid, base + mid // 2, top // 2, mid),
    )
    for key_at, key_count, q_at, few, out_at in blocks:
        keys, values = zip(
            *[keys_values(r[key_at : key_at + key_count, :], half) for r in gathered]
        )
        tile = jnp.concatenate([r[q_at : q_at + few, :].astype(f32) for r in far], axis=0)
        vl = half_mask(4 * few, half)
        for part in range(2):
            q = (tile if part == 0 else swap_halves(tile)).astype(bf16)
            found = encode(softmax_tile(q, keys, values, vl), vl, half).astype(f32)
            for d in range(4):
                at = out_at + part * few
                outs[d][at : at + few, :] = found[d * few : (d + 1) * few, :].astype(bf16)


def final_kernel(levels, offs, t_ref, *refs):
    near, far, out_ref, ts = refs[:4], refs[4:8], refs[8], refs[9]
    mine = lax.rem(lax.axis_index("seq"), 4)
    rows = out_ref.shape[0]
    ts[...] = t_ref[...]
    for d in range(4):
        head = mine ^ d
        half = lax.rem(head, 2)
        at = 0
        for level, count, rate, is_near in levels:
            off = offs[level, head]
            if is_near:
                coded = near[d][...]
            else:
                coded = far[d][at : at + count, :]
                at += count
            vl = half_mask(count, half)
            picked = pl.ds(off, count, rate)
            old = ts[head, picked, :]
            ts[head, picked, :] = merge(
                vl, old, spread_lse(old, vl), coded.astype(f32), decode_lse(coded, half)
            )
    vl = half_mask(rows, 0)
    for p in range(2):
        out_ref[:, p * LANES : (p + 1) * LANES] = jnp.where(
            vl, ts[2 * p, :, :], ts[2 * p + 1, :, :]
        ).astype(bf16)


def call(body, name, outs, n_in, scratch=(), smem=True, flops=0, bytes_moved=0, exps=0):
    whole = pl.BlockSpec(memory_space=VMEM)
    first = [pl.BlockSpec(memory_space=pltpu.SMEM)] if smem else []
    return pl.pallas_call(
        body,
        name=name,
        out_shape=outs,
        in_specs=first + [whole] * n_in,
        out_specs=jax.tree.map(lambda _: whole, outs),
        scratch_shapes=list(scratch),
        compiler_params=pltpu.CompilerParams(vmem_limit_bytes=56 << 20),
        cost_estimate=pl.CostEstimate(flops=flops, bytes_accessed=bytes_moved, transcendentals=exps),
    )


def swapped(shard, bits):
    return lax.ppermute(shard, "seq", [(i, i ^ bits) for i in range(lax.axis_size("seq"))])


def per_device(query, key, value, offsets):
    rows, width = query.shape
    places = lax.axis_size("seq")
    rate_three = RATE1 * places // 8
    rate_four = 4 * rate_three
    near_count, mid, top = rows // RATE1, rows // rate_three, rows // rate_four
    levels = (
        (2, near_count, RATE1, True),
        (3, mid, rate_three, False),
        (4, top, rate_four, False),
    )
    near_rows = near_count * 3 // 2
    far_rows = (mid + top) * 3 // 2
    wide = VMEM((2, rows, LANES), f32)

    def tile(n, kind=bf16):
        return jax.ShapeDtypeStruct((n, LANES), kind)

    def packed(*args):
        return call(
            lambda *refs: pack_kernel(levels, *refs),
            "pack",
            [tile(near_rows)] * 4 + [tile(far_rows)] * 4,
            3,
            (wide, wide, wide),
            bytes_moved=5 << 20,
        )(*args)

    parts = packed(offsets, query, key, value)
    near_sent, far_sent = parts[:4], parts[4:]
    far_held = [far_sent[0]] + [swapped(far_sent[d], d) for d in (1, 2, 3)]
    near_held = [near_sent[0]] + [swapped(near_sent[d], d) for d in (1, 2, 3)]

    state = call(
        lambda *refs: local_kernel(RATE1, *refs),
        "local",
        jax.ShapeDtypeStruct((4, rows, LANES), f32),
        3,
        (wide, wide, wide),
        flops=6 << 30,
        bytes_moved=7 << 20,
        exps=5 << 20,
    )(offsets, query, key, value)

    own_mid = jnp.concatenate([r[:mid] for r in far_held], axis=0)
    own_top = jnp.concatenate([r[mid : mid + top] for r in far_held], axis=0)
    other_top = swapped(own_top, 16)
    held = jnp.concatenate([own_mid, own_top, other_top], axis=0)
    gathered = [held] + [swapped(held, b) for b in (4, 8, 12)]

    near_found = call(
        lambda *refs: near_kernel(near_count, *refs),
        "near",
        [tile(near_count)] * 4,
        4,
        smem=False,
        flops=6 << 30,
        bytes_moved=2 << 20,
        exps=4 << 20,
    )(*near_held)
    near_back = [near_found[0]] + [swapped(near_found[d], d) for d in (1, 2, 3)]

    far_found = call(
        lambda *refs: far_kernel(mid, top, *refs),
        "far",
        [tile(mid + top)] * 4,
        8,
        smem=False,
        flops=2 << 30,
        bytes_moved=2 << 20,
        exps=1 << 20,
    )(*far_held, *gathered)
    far_back = [far_found[0]] + [swapped(far_found[d], d) for d in (1, 2, 3)]

    return call(
        lambda *refs: final_kernel(levels, *refs),
        "final",
        jax.ShapeDtypeStruct((rows, width), bf16),
        9,
        (VMEM((4, rows, LANES), f32),),
        bytes_moved=6 << 20,
    )(offsets, state, *near_back, *far_back)


def solution(mesh):
    return jax.shard_map(
        per_device,
        mesh=mesh,
        in_specs=(P("seq", "head"), P("seq", "head"), P("seq", "head"), P(None, "head")),
        out_specs=P("seq", "head"),
        check_vma=False,
    )
```

profile of v0, /device:TPU:0, one launch (start us, length us, event | category | flops | bytes accessed | tf_op | source)
XLA Modules:
  0.0 70.2 jit_solution(10272240173423515677)
XLA Ops:
  0.0 1.4 %copy.7.refs_0_ = s32[5,4]{1,0:T(8,128)} copy(s32[5,4]{0,1:T(4,128)} %param.7) | data formatting | bytes 160 | tf_op args[3]
  1.4 4.2 %pack.1 = (bf16[768,128]{1,0:T(8,128)(2,1)}, bf16[768,128]{1,0:T(8,128)(2,1)}, bf16[768,128]{1,0:T(8,128)(2,1)}, bf16[768,128]{1,0:T(8,128)(2,1)}, bf16[240,128]...) custom-call(s32[5,4]{1,0:T(8,128)} %copy.7.refs_0_, ...), custom_call_target="tpu_custom_call" | custom-call | bytes 5242880 | tf_op jit(solution)/shard_map/pack/pallas_call | solution.py:261
  5.6 1.7 %collective-permute-start.6 = (bf16[240,128]{1,0:T(8,128)(2,1)}, bf16[240,128]{1,0:T(8,128)(2,1)S(1)}, u32[]{:S(2)}, u32[]{:S(2)}) collective-permute-start(bf16[240,128]{1,0:T(8,128)(2,1)} %get-tuple-element.30), channel_id=1, source_target_pairs={{0,4},{4,0},{8,12},{12,8},{16,20},{20,16},{24,28},{28,24},{32,36},... | collective-permute-start | bytes 184328 | tf_op jit(solution)/shard_map/ppermute | solution.py:239
  7.3 1.9 %collective-permute-start.7 = (bf16[240,128]{1,0:T(8,128)(2,1)}, bf16[240,128]{1,0:T(8,128)(2,1)S(1)}, u32[]{:S(2)}, u32[]{:S(2)}) collective-permute-start(bf16[240,128]{1,0:T(8,128)(2,1)} %get-tuple-element.31), channel_id=1, source_target_pairs={{0,8},{4,12},{8,0},{12,4},{16,24},{20,28},{24,16},{28,20},{32,40},... | collective-permute-start | bytes 184328 | tf_op jit(solution)/shard_map/ppermute | solution.py:239
  9.2 1.6 %collective-permute-start = (bf16[768,128]{1,0:T(8,128)(2,1)}, bf16[768,128]{1,0:T(8,128)(2,1)S(1)}, u32[]{:S(2)}, u32[]{:S(2)}) collective-permute-start(bf16[768,128]{1,0:T(8,128)(2,1)} %get-tuple-element.22), channel_id=1, source_target_pairs={{0,4},{4,0},{8,12},{12,8},{16,20},{20,16},{24,28},{28,24},{32,36},... | collective-permute-start | bytes 589832 | tf_op jit(solution)/shard_map/ppermute | solution.py:239
  10.8 1.9 %collective-permute-start.1 = (bf16[768,128]{1,0:T(8,128)(2,1)}, bf16[768,128]{1,0:T(8,128)(2,1)S(1)}, u32[]{:S(2)}, u32[]{:S(2)}) collective-permute-start(bf16[768,128]{1,0:T(8,128)(2,1)} %get-tuple-element.23), channel_id=1, source_target_pairs={{0,8},{4,12},{8,0},{12,4},{16,24},{20,28},{24,16},{28,20},{32,40},... | collective-permute-start | bytes 589832 | tf_op jit(solution)/shard_map/ppermute | solution.py:239
  12.7 0.8 %slice_dynamic-update-slice_fusion.3 = bf16[768,128]{1,0:T(8,128)(2,1)S(1)} fusion(bf16[240,128]{1,0:T(8,128)(2,1)} %get-tuple-element.29.refs_0_), kind=kLoop, calls=%fused_computation.4 | loop fusion | bytes 65536
  13.6 1.6 %collective-permute-done.8.refs_3_ = bf16[240,128]{1,0:T(8,128)(2,1)S(1)} collective-permute-done((bf16[240,128]{1,0:T(8,128)(2,1)}, bf16[240,128]{1,0:T(8,128)(2,1)S(1)}, u32[]{:S(2)}, u32[]{:S(2)}) %collective-permute-start.8) | collective-permute-done | bytes 61472 | tf_op jit(solution)/shard_map/ppermute | solution.py:239
  15.2 0.7 %fusion = (bf16[32,128]{1,0:T(8,128)(2,1)S(1)}, bf16[768,128]{1,0:T(8,128)(2,1)S(1)}) fusion(bf16[240,128]{1,0:T(8,128)(2,1)} %get-tuple-element.29.refs_0_, bf16[768,128]{1,0:T(8,128)(2,1)S(1)} %slice_dynamic-update-slice_fusion), kind=kLoop, calls=%fused_computation.10 | loop fusion | bytes 24576 | tf_op jit(solution)/shard_map/slice | solution.py:287
  16.0 3.1 %collective-permute-start.9 = (bf16[128,128]{1,0:T(8,128)(2,1)S(1)}, bf16[128,128]{1,0:T(8,128)(2,1)S(1)}, u32[]{:S(2)}, u32[]{:S(2)}) collective-permute-start(bf16[128,128]{1,0:T(8,128)(2,1)S(1)} %pad_maximum_fusion), channel_id=1, source_target_pairs={{0,64},{4,68},{8,72},{12,76},{16,80},{20,84},{24,88},{28,92},{32,9... | collective-permute-start | bytes 98312 | tf_op jit(solution)/shard_map/ppermute | solution.py:239
  19.1 2.4 %collective-permute-done.9 = bf16[128,128]{1,0:T(8,128)(2,1)S(1)} collective-permute-done((bf16[128,128]{1,0:T(8,128)(2,1)S(1)}, bf16[128,128]{1,0:T(8,128)(2,1)S(1)}, u32[]{:S(2)}, u32[]{:S(2)}) %collective-permute-start.9) | collective-permute-done | bytes 32800 | tf_op jit(solution)/shard_map/ppermute | solution.py:239
  21.5 4.9 %collective-permute-start.12 = (bf16[768,128]{1,0:T(8,128)(2,1)S(1)}, bf16[768,128]{1,0:T(8,128)(2,1)S(1)}, u32[]{:S(2)}, u32[]{:S(2)}) collective-permute-start(bf16[768,128]{1,0:T(8,128)(2,1)S(1)} %constant_dynamic-update-slice_fusion.refs_4_), channel_id=1, source_target_pairs={{0,48},{4,52},{8,56},{12,60},{16,32},{20,36},{24,40},{28,44},{32,1... | collective-permute-start | bytes 589832 | tf_op jit(solution)/shard_map/ppermute | solution.py:239
  26.6 0.5 collective-permute-start.10
  27.9 8.3 %near.1 = (bf16[512,128]{1,0:T(8,128)(2,1)}, bf16[512,128]{1,0:T(8,128)(2,1)}, bf16[512,128]{1,0:T(8,128)(2,1)}, bf16[512,128]{1,0:T(8,128)(2,1)}) custom-call(bf16[768,128]{1,0:T(8,128)(2,1)} %get-tuple-element.21.refs_0_, bf16[768,128]{1,0:T(8,128)(2,1)} %copy-done.10, bf16[768,128]{1,0:T(8,128)(2,1)} %copy-done.11, bf16[768,128]{1,0:T(8,128)(2,1)} %copy-done.12), custom_call_target="tpu_custom_call" | custom-call | flops 6442450944 | bytes 2097152 | tf_op jit(solution)/shard_map/near/pallas_call | solution.py:292
  36.5 1.1 %collective-permute-start.4 = (bf16[512,128]{1,0:T(8,128)(2,1)}, bf16[512,128]{1,0:T(8,128)(2,1)S(1)}, u32[]{:S(2)}, u32[]{:S(2)}) collective-permute-start(bf16[512,128]{1,0:T(8,128)(2,1)} %get-tuple-element.27), channel_id=1, source_target_pairs={{0,8},{4,12},{8,0},{12,4},{16,24},{20,28},{24,16},{28,20},{32,40},... | collective-permute-start | bytes 393224 | tf_op jit(solution)/shard_map/ppermute | solution.py:239
  37.6 2.2 %collective-permute-start.5 = (bf16[512,128]{1,0:T(8,128)(2,1)}, bf16[512,128]{1,0:T(8,128)(2,1)S(1)}, u32[]{:S(2)}, u32[]{:S(2)}) collective-permute-start(bf16[512,128]{1,0:T(8,128)(2,1)} %get-tuple-element.28), channel_id=1, source_target_pairs={{0,12},{4,8},{8,4},{12,0},{16,28},{20,24},{24,20},{28,16},{32,44},... | collective-permute-start | bytes 393224 | tf_op jit(solution)/shard_map/ppermute | solution.py:239
  39.8 0.7 copy-done.14
  40.5 0.7 copy-done.15
  41.2 4.4 %far.1 = (bf16[160,128]{1,0:T(8,128)(2,1)}, bf16[160,128]{1,0:T(8,128)(2,1)}, bf16[160,128]{1,0:T(8,128)(2,1)}, bf16[160,128]{1,0:T(8,128)(2,1)}) custom-call(bf16[240,128]{1,0:T(8,128)(2,1)} %get-tuple-element.29.refs_0_, bf16[240,128]{1,0:T(8,128)(2,1)} %copy-done.6, bf16[240,128]{1,0:T(8,128)(2,1)} %copy-done.7, bf16[240,128]{1,0:T(8,128)(2,1)} %copy-done.8, ...), custom_call_target="tpu_custom_call" | custom-call | flops 2147483648 | bytes 2097152 | tf_op jit(solution)/shard_map/far/pallas_call | solution.py:304
  45.7 1.1 %collective-permute-start.14 = (bf16[160,128]{1,0:T(8,128)(2,1)}, bf16[160,128]{1,0:T(8,128)(2,1)S(1)}, u32[]{:S(2)}, u32[]{:S(2)}) collective-permute-start(bf16[160,128]{1,0:T(8,128)(2,1)} %get-tuple-element.35), channel_id=1, source_target_pairs={{0,8},{4,12},{8,0},{12,4},{16,24},{20,28},{24,16},{28,20},{32,40},... | collective-permute-start | bytes 122888 | tf_op jit(solution)/shard_map/ppermute | solution.py:239
  46.8 2.2 %collective-permute-start.15 = (bf16[160,128]{1,0:T(8,128)(2,1)}, bf16[160,128]{1,0:T(8,128)(2,1)S(1)}, u32[]{:S(2)}, u32[]{:S(2)}) collective-permute-start(bf16[160,128]{1,0:T(8,128)(2,1)} %get-tuple-element.36), channel_id=1, source_target_pairs={{0,12},{4,8},{8,4},{12,0},{16,28},{20,24},{24,20},{28,16},{32,44},... | collective-permute-start | bytes 122888 | tf_op jit(solution)/shard_map/ppermute | solution.py:239
  49.0 14.4 %local.1.refs_1_ = f32[4,2048,128]{2,1,0:T(8,128)} custom-call(s32[5,4]{1,0:T(8,128)} %copy.7.refs_0_, bf16[2048,256]{1,0:T(8,128)(2,1)} %refs_1_.3, bf16[2048,256]{1,0:T(8,128)(2,1)} %refs_2_.3, bf16[2048,256]{1,0:T(8,128)(2,1)} %refs_3_.3), custom_call_target="tpu_custom_call" | custom-call | flops 6442450944 | bytes 7340032 | tf_op jit(solution)/shard_map/local/pallas_call | solution.py:275
  63.5 0.6 copy-done.1
  64.2 6.1 %final.1 = bf16[2048,256]{1,0:T(8,128)(2,1)} custom-call(s32[5,4]{1,0:T(8,128)} %copy.7.refs_0_, f32[4,2048,128]{2,1,0:T(8,128)} %local.1.refs_1_, bf16[512,128]{1,0:T(8,128)(2,1)} %get-tuple-element.25.refs_2_, bf16[512,128]{1,0:T(8,128)(2,1)} %copy-done, bf16[512,128]{1,0:T(8,128)(2,1)} %copy-done.1, bf16[512,128]{1,0:T(8,128)(2,1)} %copy-done.2, ...), custom_call_target="tpu_custom_call" | custom-call | bytes 6291456 | tf_op jit(solution)/shard_map/final/pallas_call | solution.py:316
  (56 shorter events, 1.7 us)
Async XLA Ops:
  5.6 7.9 %collective-permute-start.6 = (bf16[240,128]{1,0:T(8,128)(2,1)}, bf16[240,128]{1,0:T(8,128)(2,1)S(1)}, u32[]{:S(2)}, u32[]{:S(2)}) collective-permute-start(bf16[240,128]{1,0:T(8,128)(2,1)} %get-tuple-element.30), channel_id=1, source_target_pairs={{0,4},{4,0},{8,12},{12,8},{16,20},{20,16},{24,28},{28,24},{32,36},... | collective-permute-start | bytes 184328 | tf_op jit(solution)/shard_map/ppermute | solution.py:239
  7.3 6.2 %collective-permute-start.7 = (bf16[240,128]{1,0:T(8,128)(2,1)}, bf16[240,128]{1,0:T(8,128)(2,1)S(1)}, u32[]{:S(2)}, u32[]{:S(2)}) collective-permute-start(bf16[240,128]{1,0:T(8,128)(2,1)} %get-tuple-element.31), channel_id=1, source_target_pairs={{0,8},{4,12},{8,0},{12,4},{16,24},{20,28},{24,16},{28,20},{32,40},... | collective-permute-start | bytes 184328 | tf_op jit(solution)/shard_map/ppermute | solution.py:239
  9.2 6.0 %collective-permute-start.8 = (bf16[240,128]{1,0:T(8,128)(2,1)}, bf16[240,128]{1,0:T(8,128)(2,1)S(1)}, u32[]{:S(2)}, u32[]{:S(2)}) collective-permute-start(bf16[240,128]{1,0:T(8,128)(2,1)} %get-tuple-element.32), channel_id=1, source_target_pairs={{0,12},{4,8},{8,4},{12,0},{16,28},{20,24},{24,20},{28,16},{32,44},... | collective-permute-start | bytes 184328 | tf_op jit(solution)/shard_map/ppermute | solution.py:239
  9.2 17.4 %collective-permute-start = (bf16[768,128]{1,0:T(8,128)(2,1)}, bf16[768,128]{1,0:T(8,128)(2,1)S(1)}, u32[]{:S(2)}, u32[]{:S(2)}) collective-permute-start(bf16[768,128]{1,0:T(8,128)(2,1)} %get-tuple-element.22), channel_id=1, source_target_pairs={{0,4},{4,0},{8,12},{12,8},{16,20},{20,16},{24,28},{28,24},{32,36},... | collective-permute-start | bytes 589832 | tf_op jit(solution)/shard_map/ppermute | solution.py:239
  10.8 16.3 %collective-permute-start.1 = (bf16[768,128]{1,0:T(8,128)(2,1)}, bf16[768,128]{1,0:T(8,128)(2,1)S(1)}, u32[]{:S(2)}, u32[]{:S(2)}) collective-permute-start(bf16[768,128]{1,0:T(8,128)(2,1)} %get-tuple-element.23), channel_id=1, source_target_pairs={{0,8},{4,12},{8,0},{12,4},{16,24},{20,28},{24,16},{28,20},{32,40},... | collective-permute-start | bytes 589832 | tf_op jit(solution)/shard_map/ppermute | solution.py:239
  13.5 22.7 %copy-start.6 = (bf16[240,128]{1,0:T(8,128)(2,1)}, bf16[240,128]{1,0:T(8,128)(2,1)S(1)}, u32[]{:S(2)}) copy-start(bf16[240,128]{1,0:T(8,128)(2,1)S(1)} %collective-permute-done.6.refs_1_) | copy-start | bytes 184324
  13.5 13.6 %collective-permute-start.2 = (bf16[768,128]{1,0:T(8,128)(2,1)}, bf16[768,128]{1,0:T(8,128)(2,1)S(1)}, u32[]{:S(2)}, u32[]{:S(2)}) collective-permute-start(bf16[768,128]{1,0:T(8,128)(2,1)} %get-tuple-element.24), channel_id=1, source_target_pairs={{0,12},{4,8},{8,4},{12,0},{16,28},{20,24},{24,20},{28,16},{32,44},... | collective-permute-start | bytes 589832 | tf_op jit(solution)/shard_map/ppermute | solution.py:239
  13.5 22.7 %copy-start.7 = (bf16[240,128]{1,0:T(8,128)(2,1)}, bf16[240,128]{1,0:T(8,128)(2,1)S(1)}, u32[]{:S(2)}) copy-start(bf16[240,128]{1,0:T(8,128)(2,1)S(1)} %collective-permute-done.7.refs_2_) | copy-start | bytes 184324
  15.2 21.0 %copy-start.8 = (bf16[240,128]{1,0:T(8,128)(2,1)}, bf16[240,128]{1,0:T(8,128)(2,1)S(1)}, u32[]{:S(2)}) copy-start(bf16[240,128]{1,0:T(8,128)(2,1)S(1)} %collective-permute-done.8.refs_3_) | copy-start | bytes 184324
  16.0 5.5 %collective-permute-start.9 = (bf16[128,128]{1,0:T(8,128)(2,1)S(1)}, bf16[128,128]{1,0:T(8,128)(2,1)S(1)}, u32[]{:S(2)}, u32[]{:S(2)}) collective-permute-start(bf16[128,128]{1,0:T(8,128)(2,1)S(1)} %pad_maximum_fusion), channel_id=1, source_target_pairs={{0,64},{4,68},{8,72},{12,76},{16,80},{20,84},{24,88},{28,92},{32,9... | collective-permute-start | bytes 98312 | tf_op jit(solution)/shard_map/ppermute | solution.py:239
  21.5 14.7 %copy-start.9 = (bf16[768,128]{1,0:T(8,128)(2,1)}, bf16[768,128]{1,0:T(8,128)(2,1)S(1)}, u32[]{:S(2)}) copy-start(bf16[768,128]{1,0:T(8,128)(2,1)S(1)} %constant_dynamic-update-slice_fusion.refs_4_) | copy-start | bytes 589828
  21.5 16.1 %collective-permute-start.12 = (bf16[768,128]{1,0:T(8,128)(2,1)S(1)}, bf16[768,128]{1,0:T(8,128)(2,1)S(1)}, u32[]{:S(2)}, u32[]{:S(2)}) collective-permute-start(bf16[768,128]{1,0:T(8,128)(2,1)S(1)} %constant_dynamic-update-slice_fusion.refs_4_), channel_id=1, source_target_pairs={{0,48},{4,52},{8,56},{12,60},{16,32},{20,36},{24,40},{28,44},{32,1... | collective-permute-start | bytes 589832 | tf_op jit(solution)/shard_map/ppermute | solution.py:239
  26.4 13.4 %collective-permute-start.11 = (bf16[768,128]{1,0:T(8,128)(2,1)S(1)}, bf16[768,128]{1,0:T(8,128)(2,1)S(1)}, u32[]{:S(2)}, u32[]{:S(2)}) collective-permute-start(bf16[768,128]{1,0:T(8,128)(2,1)S(1)} %constant_dynamic-update-slice_fusion.refs_4_), channel_id=1, source_target_pairs={{0,32},{4,36},{8,40},{12,44},{16,48},{20,52},{24,56},{28,60},{32,0... | collective-permute-start | bytes 589832 | tf_op jit(solution)/shard_map/ppermute | solution.py:239
  26.6 13.2 %collective-permute-start.10 = (bf16[768,128]{1,0:T(8,128)(2,1)S(1)}, bf16[768,128]{1,0:T(8,128)(2,1)S(1)}, u32[]{:S(2)}, u32[]{:S(2)}) collective-permute-start(bf16[768,128]{1,0:T(8,128)(2,1)S(1)} %constant_dynamic-update-slice_fusion.refs_4_), channel_id=1, source_target_pairs={{0,16},{4,20},{8,24},{12,28},{16,0},{20,4},{24,8},{28,12},{32,48},... | collective-permute-start | bytes 589832 | tf_op jit(solution)/shard_map/ppermute | solution.py:239
  27.1 0.8 %copy-start.12 = (bf16[768,128]{1,0:T(8,128)(2,1)}, bf16[768,128]{1,0:T(8,128)(2,1)S(1)}, u32[]{:S(2)}) copy-start(bf16[768,128]{1,0:T(8,128)(2,1)S(1)} %collective-permute-done.2.refs_3_) | copy-start | bytes 589828
  36.2 10.6 %collective-permute-start.3 = (bf16[512,128]{1,0:T(8,128)(2,1)}, bf16[512,128]{1,0:T(8,128)(2,1)S(1)}, u32[]{:S(2)}, u32[]{:S(2)}) collective-permute-start(bf16[512,128]{1,0:T(8,128)(2,1)} %get-tuple-element.26), channel_id=1, source_target_pairs={{0,4},{4,0},{8,12},{12,8},{16,20},{20,16},{24,28},{28,24},{32,36},... | collective-permute-start | bytes 393224 | tf_op jit(solution)/shard_map/ppermute | solution.py:239
  36.5 26.9 %collective-permute-start.4 = (bf16[512,128]{1,0:T(8,128)(2,1)}, bf16[512,128]{1,0:T(8,128)(2,1)S(1)}, u32[]{:S(2)}, u32[]{:S(2)}) collective-permute-start(bf16[512,128]{1,0:T(8,128)(2,1)} %get-tuple-element.27), channel_id=1, source_target_pairs={{0,8},{4,12},{8,0},{12,4},{16,24},{20,28},{24,16},{28,20},{32,40},... | collective-permute-start | bytes 393224 | tf_op jit(solution)/shard_map/ppermute | solution.py:239
  37.6 2.2 %copy-start.13 = (bf16[768,128]{1,0:T(8,128)(2,1)}, bf16[768,128]{1,0:T(8,128)(2,1)S(1)}, u32[]{:S(2)}) copy-start(bf16[768,128]{1,0:T(8,128)(2,1)S(1)} %collective-permute-done.12.refs_7_) | copy-start | bytes 589828
  37.6 25.8 %collective-permute-start.5 = (bf16[512,128]{1,0:T(8,128)(2,1)}, bf16[512,128]{1,0:T(8,128)(2,1)S(1)}, u32[]{:S(2)}, u32[]{:S(2)}) collective-permute-start(bf16[512,128]{1,0:T(8,128)(2,1)} %get-tuple-element.28), channel_id=1, source_target_pairs={{0,12},{4,8},{8,4},{12,0},{16,28},{20,24},{24,20},{28,16},{32,44},... | collective-permute-start | bytes 393224 | tf_op jit(solution)/shard_map/ppermute | solution.py:239
  45.5 17.9 %collective-permute-start.13 = (bf16[160,128]{1,0:T(8,128)(2,1)}, bf16[160,128]{1,0:T(8,128)(2,1)S(1)}, u32[]{:S(2)}, u32[]{:S(2)}) collective-permute-start(bf16[160,128]{1,0:T(8,128)(2,1)} %get-tuple-element.34), channel_id=1, source_target_pairs={{0,4},{4,0},{8,12},{12,8},{16,20},{20,16},{24,28},{28,24},{32,36},... | collective-permute-start | bytes 122888 | tf_op jit(solution)/shard_map/ppermute | solution.py:239
  45.7 17.7 %collective-permute-start.14 = (bf16[160,128]{1,0:T(8,128)(2,1)}, bf16[160,128]{1,0:T(8,128)(2,1)S(1)}, u32[]{:S(2)}, u32[]{:S(2)}) collective-permute-start(bf16[160,128]{1,0:T(8,128)(2,1)} %get-tuple-element.35), channel_id=1, source_target_pairs={{0,8},{4,12},{8,0},{12,4},{16,24},{20,28},{24,16},{28,20},{32,40},... | collective-permute-start | bytes 122888 | tf_op jit(solution)/shard_map/ppermute | solution.py:239
  46.8 16.6 %copy-start = (bf16[512,128]{1,0:T(8,128)(2,1)}, bf16[512,128]{1,0:T(8,128)(2,1)S(1)}, u32[]{:S(2)}) copy-start(bf16[512,128]{1,0:T(8,128)(2,1)S(1)} %collective-permute-done.3.refs_3_) | copy-start | bytes 393220
  46.8 16.6 %collective-permute-start.15 = (bf16[160,128]{1,0:T(8,128)(2,1)}, bf16[160,128]{1,0:T(8,128)(2,1)S(1)}, u32[]{:S(2)}, u32[]{:S(2)}) collective-permute-start(bf16[160,128]{1,0:T(8,128)(2,1)} %get-tuple-element.36), channel_id=1, source_target_pairs={{0,12},{4,8},{8,4},{12,0},{16,28},{20,24},{24,20},{28,16},{32,44},... | collective-permute-start | bytes 122888 | tf_op jit(solution)/shard_map/ppermute | solution.py:239
  63.4 0.7 %copy-start.2 = (bf16[512,128]{1,0:T(8,128)(2,1)}, bf16[512,128]{1,0:T(8,128)(2,1)S(1)}, u32[]{:S(2)}) copy-start(bf16[512,128]{1,0:T(8,128)(2,1)S(1)} %collective-permute-done.5.refs_5_) | copy-start | bytes 393220
  (8 other events, 5.5 us)
where the time goes:
time: 70.6 us; the launch traced here: 70.2 us
  Pallas kernels  37.4 us (53%)
  starting transfers between devices  22.9 us (32%)
  local copies, waits for them, and re-layouts  5.75 us (8%)
  waiting for transfers between devices  4.07 us (6%)
    ppermute x16, starting transfers between devices, swapped(): lax.ppermute(shard, 'seq', [(i, i ^ bits) for i in range(lax.axis_size('s...  22.9 us
    pallas_call x1, Pallas kernels, per_device(): call(lambda *refs: local_kernel(RATE1, *refs), 'local', jax.ShapeDtypeStr...  14.4 us
    pallas_call x1, Pallas kernels, per_device(): call(lambda *refs: near_kernel(near_count, *refs), 'near', [tile(near_cou...  8.33 us
    pallas_call x1, Pallas kernels, per_device(): call(lambda *refs: final_kernel(levels, *refs), 'final', jax.ShapeDtypeSt...  6.05 us
    unnamed x37, local copies, waits for them, and re-layouts  4.98 us
    pallas_call x1, Pallas kernels, per_device(): call(lambda *refs: far_kernel(mid, top, *refs), 'far', [tile(mid + top)]...  4.36 us
    pallas_call x1, Pallas kernels, packed(): call(lambda *refs: pack_kernel(levels, *refs), 'pack', [tile(near_rows)]...  4.25 us
    ppermute x16, waiting for transfers between devices, swapped(): lax.ppermute(shard, 'seq', [(i, i ^ bits) for i in range(lax.axis_size('s...  4.07 us
  transfers between devices with their start and end apart: 16, of which 2 were waited for; matrix products, arithmetic and copies ran while one was open for 2% of the time, Pallas kernels for 39%

commit v1 on v0

v1 whole, which is shorter than its diff:
```python
import jax
import jax.numpy as jnp
from jax import lax
from jax.experimental import pallas as pl
from jax.experimental.pallas import tpu as pltpu
from jax.sharding import PartitionSpec as P


SEG = 512
RATE1 = 4
bf16 = jnp.bfloat16
f32 = jnp.float32
LANES = 128
HALF = 64
VMEM = pltpu.VMEM


def dot_nt(a, b):
    return lax.dot_general(a, b, (((1,), (1,)), ((), ())), preferred_element_type=f32)


def dot_nn(a, b):
    return lax.dot_general(a, b, (((1,), (0,)), ((), ())), preferred_element_type=f32)


def half_mask(rows, half):
    lane = lax.broadcasted_iota(jnp.int32, (rows, LANES), 1)
    return lax.div(lane, HALF) == half


def swap_halves(x):
    return pltpu.roll(x, HALF, 1)


def softmax_tile(q, keys, values, vl):
    scores = [dot_nt(q, k) for k in keys]
    top = scores[0].max(axis=1, keepdims=True)
    for s in scores[1:]:
        top = jnp.maximum(top, s.max(axis=1, keepdims=True))
    acc = None
    for s, v in zip(scores, values):
        part = dot_nn(jnp.exp(s - top).astype(bf16), v)
        acc = part if acc is None else acc + part
    return jnp.where(vl, acc / swap_halves(acc), top + jnp.log(acc))


def merge(vl, one, lse_one, two, lse_two):
    gap = lse_two - lse_one
    small = jnp.exp(-jnp.abs(gap))
    ahead = gap > 0.0
    big_out = jnp.where(ahead, two, one)
    small_out = jnp.where(ahead, one, two)
    weight = 1.0 + small
    out = (big_out + small * small_out) / weight
    return jnp.where(vl, out, jnp.maximum(lse_one, lse_two) + jnp.log(weight))


def spread_lse(tile, vl):
    return jnp.where(vl, swap_halves(tile), tile)


def encode(tile, vl):
    lane = lax.broadcasted_iota(jnp.int32, tile.shape, 1)
    spot = lax.rem(lane, HALF)
    first = tile.astype(bf16).astype(f32)
    rest = tile - first
    second = rest.astype(bf16).astype(f32)
    third = rest - second
    coded = jnp.where(spot == 0, first, jnp.where(spot == 1, second, third))
    return jnp.where(vl, tile, coded).astype(bf16)


def decode_lse(coded, half):
    row = lax.broadcasted_iota(jnp.int32, (LANES, LANES), 0)
    pick = jnp.logical_and(lax.div(row, HALF) != half, lax.rem(row, HALF) < 3)
    return dot_nn(coded, jnp.where(pick, 1.0, 0.0).astype(bf16))


def widen(src, dst):
    rows = src.shape[0]
    step = min(rows, 512)

    @pl.loop(0, rows // step)
    def _(i):
        part = pl.ds(pl.multiple_of(i * step, step), step)
        for p in range(src.shape[1] // LANES):
            dst[p, part, :] = src[part, p * LANES : (p + 1) * LANES].astype(f32)


def fetch(offs_any, offs, sem):
    copy = pltpu.make_async_copy(offs_any, offs, sem)
    copy.start()
    return copy


def pack_kernel(levels, offs_any, q_any, k_any, v_any, *rest):
    near_out, far_out, (qs, ks, vs, qb, kb, vb, offs, sems) = rest[0:4], rest[4:8], rest[8:]
    mine = lax.rem(lax.axis_index("seq"), 4)
    copies = [fetch(k_any, kb, sems.at[0]), fetch(v_any, vb, sems.at[1])]
    copies += [fetch(q_any, qb, sems.at[2]), fetch(offs_any, offs, sems.at[3])]
    for copy, narrow, wide in zip(copies, (kb, vb, qb), (ks, vs, qs)):
        copy.wait()
        widen(narrow, wide)
    copies[3].wait()
    for d in range(4):
        head = mine ^ d
        pair, half = lax.div(head, 2), lax.rem(head, 2)
        base = [0, 0]
        for what in ("kv", "q"):
            for level, count, rate, near in levels:
                off = offs[level, head]
                ref = near_out[d] if near else far_out[d]
                at = base[near]
                if what == "kv":
                    vl = half_mask(count, half)
                    k = ks[pair, pl.ds(off, count, rate), :]
                    v = vs[pair, pl.ds(off, count, rate), :]
                    ref[at : at + count, :] = jnp.where(vl, v, swap_halves(k)).astype(bf16)
                    base[near] = at + count
                else:
                    few = count // 2
                    vl = half_mask(few, half)
                    q_one = qs[pair, pl.ds(off, few, rate), :]
                    q_two = qs[pair, pl.ds(off + few * rate, few, rate), :]
                    tile = jnp.where(vl, q_two, swap_halves(q_one))
                    ref[at : at + few, :] = (tile * 0.125).astype(bf16)
                    base[near] = at + few


def first_kernel(q_ref, k_ref, v_ref, t_ref):
    zero, one = jnp.asarray(0, bf16), jnp.asarray(1, bf16)
    scale = jnp.asarray(0.125, bf16)

    @pl.loop(0, q_ref.shape[0] // SEG)
    def _(s):
        part = pl.ds(pl.multiple_of(s * SEG, SEG), SEG)
        for h in range(4):
            cols = slice(h // 2 * LANES, (h // 2 + 1) * LANES)
            vl = half_mask(SEG, h % 2)
            q = q_ref[part, cols] * scale
            k = jnp.where(vl, k_ref[part, cols], zero)
            v = jnp.where(vl, v_ref[part, cols], one)
            t_ref[h, part, :] = softmax_tile(q, [k], [v], vl)


def second_kernel(rate, offs_any, q_ref, k_ref, v_ref, found_ref, qs, ks, vs, offs, sem):
    copy = fetch(offs_any, offs, sem)
    count = q_ref.shape[0] // rate
    widen(q_ref, qs)
    widen(k_ref, ks)
    widen(v_ref, vs)
    copy.wait()
    for h in range(4):
        vl = half_mask(count, h % 2)
        picked = pl.ds(offs[1, h], count, rate)
        q = (qs[h // 2, picked, :] * 0.125).astype(bf16)
        k = jnp.where(vl, ks[h // 2, picked, :], 0.0).astype(bf16)
        v = jnp.where(vl, vs[h // 2, picked, :], 1.0).astype(bf16)
        found_ref[h, :, :] = softmax_tile(q, [k], [v], vl)


def keys_values(tile, half):
    vl = half_mask(tile.shape[0], half)
    zero, one = jnp.asarray(0, bf16), jnp.asarray(1, bf16)
    return jnp.where(vl, zero, tile), jnp.where(vl, tile, one)


def near_kernel(count, *refs):
    ins, outs = refs[:4], refs[4:]
    half = lax.rem(lax.axis_index("seq"), 2)
    keys, values = zip(*[keys_values(r[:count, :], half) for r in ins])
    few = count // 2
    vl = half_mask(few, half)
    for d in range(4):
        tile = ins[d][count : count + few, :]
        for part in range(2):
            q = tile if part == 0 else swap_halves(tile.astype(f32)).astype(bf16)
            found = softmax_tile(q, keys, values, vl)
            outs[d][part * few : (part + 1) * few, :] = encode(found, vl)


def far_kernel(mid, top, *refs):
    far, gathered, tops, outs = refs[:4], refs[4:8], refs[8:12], refs[12:16]
    half = lax.rem(lax.axis_index("seq"), 2)
    base = mid + top
    blocks = (
        ([r[: 4 * mid, :] for r in gathered], base, mid // 2, 0),
        ([r[4 * mid :, :] for r in gathered] + [r[...] for r in tops], base + mid // 2, top // 2, mid),
    )
    for tiles, q_at, few, out_at in blocks:
        keys, values = zip(*[keys_values(t, half) for t in tiles])
        tile = jnp.concatenate([r[q_at : q_at + few, :].astype(f32) for r in far], axis=0)
        q = jnp.concatenate([tile, swap_halves(tile)], axis=0).astype(bf16)
        vl = half_mask(8 * few, half)
        found = encode(softmax_tile(q, keys, values, vl), vl).astype(f32)
        for part in range(2):
            for d in range(4):
                at, start = out_at + part * few, (part * 4 + d) * few
                outs[d][at : at + few, :] = found[start : start + few, :].astype(bf16)


def absorb(state, head, half, off, rate, coded):
    count = coded.shape[0]
    vl = half_mask(count, half)
    picked = pl.ds(off, count, rate)
    old = state[head, picked, :]
    state[head, picked, :] = merge(
        vl, old, spread_lse(old, vl), coded.astype(f32), decode_lse(coded, half)
    )


def blend_kernel(rate, offs_any, state_in, found_ref, *refs):
    near, state, offs, sem = refs[:4], refs[4], refs[5], refs[6]
    copy = fetch(offs_any, offs, sem)
    mine = lax.rem(lax.axis_index("seq"), 4)
    copy.wait()
    count = found_ref.shape[1]
    for h in range(4):
        vl = half_mask(count, h % 2)
        picked = pl.ds(offs[1, h], count, rate)
        old, new = state[h, picked, :], found_ref[h, :, :]
        state[h, picked, :] = merge(vl, old, spread_lse(old, vl), new, spread_lse(new, vl))
    for d in range(4):
        head = mine ^ d
        absorb(state, head, lax.rem(head, 2), offs[2, head], rate, near[d][...])


def final_kernel(levels, offs_any, state_in, *refs):
    far, state, out_ref, offs, sem = refs[:4], refs[4], refs[5], refs[6], refs[7]
    copy = fetch(offs_any, offs, sem)
    mine = lax.rem(lax.axis_index("seq"), 4)
    copy.wait()
    for d in range(4):
        head = mine ^ d
        at = 0
        for level, count, rate, near in levels:
            if not near:
                absorb(
                    state, head, lax.rem(head, 2), offs[level, head], rate, far[d][at : at + count, :]
                )
                at += count
    vl = half_mask(out_ref.shape[0], 0)
    for p in range(2):
        out_ref[:, p * LANES : (p + 1) * LANES] = jnp.where(
            vl, state[2 * p, :, :], state[2 * p + 1, :, :]
        ).astype(bf16)


def call(body, outs, spaces, scratch=(), flops=0, bytes_moved=0, exps=0, aliases=None):
    whole = pl.BlockSpec(memory_space=VMEM)
    place = {"v": whole, "a": pl.BlockSpec(memory_space=pltpu.HBM)}
    return pl.pallas_call(
        body,
        out_shape=outs,
        in_specs=[place[c] for c in spaces],
        out_specs=jax.tree.map(lambda _: whole, outs),
        scratch_shapes=list(scratch),
        input_output_aliases=aliases or {},
        compiler_params=pltpu.CompilerParams(vmem_limit_bytes=48 << 20),
        cost_estimate=pl.CostEstimate(flops=flops, bytes_accessed=bytes_moved, transcendentals=exps),
    )


def swapped(shard, bits):
    return lax.ppermute(
        shard, "seq", [(i, i ^ bits) for i in range(lax.axis_size("seq"))]
    )


def per_device(query, key, value, offsets):
    rows, width = query.shape
    places = lax.axis_size("seq")
    rate_three = RATE1 * places // 8
    rate_four = 4 * rate_three
    near_count, mid, top = rows // RATE1, rows // rate_three, rows // rate_four
    levels = (
        (2, near_count, RATE1, True),
        (3, mid, rate_three, False),
        (4, top, rate_four, False),
    )
    wide = VMEM((2, rows, LANES), f32)
    narrow = VMEM((rows, width), bf16)
    table = pltpu.SMEM(offsets.shape, jnp.int32)
    one_sem = pltpu.SemaphoreType.DMA

    def tile(n, kind=bf16):
        return jax.ShapeDtypeStruct((n, LANES), kind)

    state_shape = jax.ShapeDtypeStruct((4, rows, LANES), f32)
    parts = call(
        lambda *refs: pack_kernel(levels, *refs),
        [tile(near_count * 3 // 2)] * 4 + [tile((mid + top) * 3 // 2)] * 4,
        "aaaa",
        (wide, wide, wide, narrow, narrow, narrow, table, pltpu.SemaphoreType.DMA((4,))),
        bytes_moved=5 << 20,
    )(offsets, query, key, value)
    near_sent, far_sent = parts[:4], parts[4:]
    far_held = [far_sent[0]] + [swapped(far_sent[d], d) for d in (1, 2, 3)]
    near_held = [near_sent[0]] + [swapped(near_sent[d], d) for d in (1, 2, 3)]

    state = call(
        first_kernel, state_shape, "vvv", flops=4 << 30, bytes_moved=7 << 20, exps=4 << 20
    )(query, key, value)

    own_top = jnp.concatenate([r[mid : mid + top] for r in far_held], axis=0)
    held = jnp.concatenate([r[:mid] for r in far_held] + [own_top], axis=0)
    gathered = [held] + [swapped(held, b) for b in (12, 8, 4)]
    tops = [swapped(own_top, 16 + b) for b in (12, 8, 4, 0)]

    near_found = call(
        lambda *refs: near_kernel(near_count, *refs),
        [tile(near_count)] * 4,
        "vvvv",
        flops=6 << 30,
        bytes_moved=2 << 20,
        exps=4 << 20,
    )(*near_held)
    near_back = [near_found[0]] + [swapped(near_found[d], d) for d in (1, 2, 3)]

    found = call(
        lambda *refs: second_kernel(RATE1, *refs),
        jax.ShapeDtypeStruct((4, near_count, LANES), f32),
        "avvv",
        (wide, wide, wide, table, one_sem),
        flops=2 << 30,
        bytes_moved=4 << 20,
        exps=1 << 20,
    )(offsets, query, key, value)

    far_found = call(
        lambda *refs: far_kernel(mid, top, *refs),
        [tile(mid + top)] * 4,
        "v" * 12,
        flops=2 << 30,
        bytes_moved=2 << 20,
        exps=1 << 20,
    )(*far_held, *gathered, *tops)
    far_back = [far_found[0]] + [swapped(far_found[d], d) for d in (1, 2, 3)]

    state = call(
        lambda *refs: blend_kernel(RATE1, *refs),
        state_shape,
        "avvvvvv",
        (table, one_sem),
        bytes_moved=10 << 20,
        aliases={1: 0},
    )(offsets, state, found, *near_back)

    return call(
        lambda *refs: final_kernel(levels, *refs),
        [state_shape, jax.ShapeDtypeStruct((rows, width), bf16)],
        "avvvvv",
        (table, one_sem),
        bytes_moved=6 << 20,
        aliases={1: 0},
    )(offsets, state, *far_back)[1]


def solution(mesh):
    return jax.shard_map(
        per_device,
        mesh=mesh,
        in_specs=(P("seq", "head"), P("seq", "head"), P("seq", "head"), P(None, "head")),
        out_specs=P("seq", "head"),
        check_vma=False,
    )
```

time: 70.6 us -> 64.1 us (0.908)
  Pallas kernels: 37.4 us -> 28 us
  starting transfers between devices: 22.9 us -> 29.4 us
  waiting for transfers between devices: 4.07 us -> 1.7 us
  local copies, waits for them, and re-layouts: 5.75 us -> 4.52 us
    pallas_call x5 -> x7, Pallas kernels: 37.4 us -> 28 us  [the longest x1 9.01 us: per_device(): call(first_kernel, state_shape, 'vvv', flops=4 << 30, bytes_moved=7 << 20...]
    ppermute x16 -> x19, starting transfers between devices: 22.9 us -> 29.4 us  [swapped(): lax.ppermute(shard, 'seq', [(i, i ^ bits) for i in range(lax.axis_size('s...]
    ppermute x16 -> x19, waiting for transfers between devices: 4.07 us -> 1.7 us  [swapped(): lax.ppermute(shard, 'seq', [(i, i ^ bits) for i in range(lax.axis_size('s...]
    slice x4, local copies, waits for them, and re-layouts: 0.75 us -> 0.03 us  [per_device(): own_top = jnp.concatenate([r[mid:mid + top] for r in far_held], axis=0)]
    unnamed x37 -> x17, local copies, waits for them, and re-layouts: 4.98 us -> 4.49 us
  transfers between devices with their start and end apart: 16 -> 19, of which waited for: 2 -> 1; matrix products, arithmetic and copies ran while one was open for 2% -> 0% of each run, Pallas kernels for 39% -> 36%
where the time goes in v1:
time: 64.1 us; the launch traced here: 63.9 us
  starting transfers between devices  29.4 us (46%)
  Pallas kernels  28 us (44%)
  local copies, waits for them, and re-layouts  4.52 us (7%)
  waiting for transfers between devices  1.7 us (3%)
    ppermute x19, starting transfers between devices, swapped(): lax.ppermute(shard, 'seq', [(i, i ^ bits) for i in range(lax.axis_size('s...  29.4 us
    pallas_call x1, Pallas kernels, per_device(): call(first_kernel, state_shape, 'vvv', flops=4 << 30, bytes_moved=7 << 20...  9.01 us
    pallas_call x1, Pallas kernels, per_device(): call(lambda *refs: near_kernel(near_count, *refs), [tile(near_count)] * 4...  6.45 us
    unnamed x17, local copies, waits for them, and re-layouts  4.49 us
    pallas_call x1, Pallas kernels, per_device(): call(lambda *refs: final_kernel(levels, *refs), [state_shape, jax.ShapeDt...  2.96 us
    pallas_call x1, Pallas kernels, per_device(): call(lambda *refs: blend_kernel(RATE1, *refs), state_shape, 'avvvvvv', (t...  2.9 us
    pallas_call x1, Pallas kernels, per_device(): call(lambda *refs: far_kernel(mid, top, *refs), [tile(mid + top)] * 4, 'v...  2.45 us
    pallas_call x1, Pallas kernels, per_device(): call(lambda *refs: second_kernel(RATE1, *refs), jax.ShapeDtypeStruct((4,...  2.34 us
  transfers between devices with their start and end apart: 19, of which 1 were waited for; matrix products, arithmetic and copies ran while one was open for 0% of the time, Pallas kernels for 36%

profile of v1, /device:TPU:0, one launch (start us, length us, event | category | flops | bytes accessed | tf_op | source)
XLA Modules:
  0.0 63.9 jit_solution(10910500064246767667)
XLA Ops:
  0.0 0.8 %copy.10.refs_0_ = s32[5,4]{1,0:T(8,128)S(1)} copy(s32[5,4]{0,1:T(4,128)} %param.7) | data formatting | bytes 160 | tf_op args[3]
  0.8 1.2 %copy-done.1 = bf16[2048,256]{1,0:T(8,128)(2,1)S(1)} copy-done((bf16[2048,256]{1,0:T(8,128)(2,1)S(1)}, bf16[2048,256]{1,0:T(8,128)(2,1)}, u32[]{:S(2)}) %copy-start.1) | copy-done | bytes 1048600
  2.0 1.2 %copy-done.3 = bf16[2048,256]{1,0:T(8,128)(2,1)S(1)} copy-done((bf16[2048,256]{1,0:T(8,128)(2,1)S(1)}, bf16[2048,256]{1,0:T(8,128)(2,1)}, u32[]{:S(2)}) %copy-start.3) | copy-done | bytes 1048600
  3.2 1.2 %copy-done.5 = bf16[2048,256]{1,0:T(8,128)(2,1)S(1)} copy-done((bf16[2048,256]{1,0:T(8,128)(2,1)S(1)}, bf16[2048,256]{1,0:T(8,128)(2,1)}, u32[]{:S(2)}) %copy-start.5) | copy-done | bytes 1048600
  4.4 1.8 %shard_map.48 = (bf16[768,128]{1,0:T(8,128)(2,1)S(1)}, bf16[768,128]{1,0:T(8,128)(2,1)S(1)}, bf16[768,128]{1,0:T(8,128)(2,1)S(1)}, bf16[768,128]{1,0:T(8,128)(2,...) custom-call(s32[5,4]{1,0:T(8,128)S(1)} %copy.10.refs_0_, ...), custom_call_target="tpu_custom_call" | custom-call | bytes 5242880 | tf_op jit(solution)/shard_map/pallas_call | solution.py:290
  6.3 1.8 %collective-permute-start.6 = (bf16[240,128]{1,0:T(8,128)(2,1)S(1)}, bf16[240,128]{1,0:T(8,128)(2,1)S(1)}, u32[]{:S(2)}, u32[]{:S(2)}) collective-permute-start(bf16[240,128]{1,0:T(8,128)(2,1)S(1)} %get-tuple-element.31), channel_id=1, source_target_pairs={{0,4},{4,0},{8,12},{12,8},{16,20},{20,16},{24,28},{28,24},{32,36},... | collective-permute-start | bytes 184328 | tf_op jit(solution)/shard_map/ppermute | solution.py:265
  8.1 1.9 %collective-permute-start.7 = (bf16[240,128]{1,0:T(8,128)(2,1)S(1)}, bf16[240,128]{1,0:T(8,128)(2,1)S(1)}, u32[]{:S(2)}, u32[]{:S(2)}) collective-permute-start(bf16[240,128]{1,0:T(8,128)(2,1)S(1)} %get-tuple-element.32), channel_id=1, source_target_pairs={{0,8},{4,12},{8,0},{12,4},{16,24},{20,28},{24,16},{28,20},{32,40},... | collective-permute-start | bytes 184328 | tf_op jit(solution)/shard_map/ppermute | solution.py:265
  10.0 1.6 %collective-permute-start = (bf16[768,128]{1,0:T(8,128)(2,1)S(1)}, bf16[768,128]{1,0:T(8,128)(2,1)S(1)}, u32[]{:S(2)}, u32[]{:S(2)}) collective-permute-start(bf16[768,128]{1,0:T(8,128)(2,1)S(1)} %get-tuple-element.23), channel_id=1, source_target_pairs={{0,4},{4,0},{8,12},{12,8},{16,20},{20,16},{24,28},{28,24},{32,36},... | collective-permute-start | bytes 589832 | tf_op jit(solution)/shard_map/ppermute | solution.py:265
  11.6 1.9 %collective-permute-start.1 = (bf16[768,128]{1,0:T(8,128)(2,1)S(1)}, bf16[768,128]{1,0:T(8,128)(2,1)S(1)}, u32[]{:S(2)}, u32[]{:S(2)}) collective-permute-start(bf16[768,128]{1,0:T(8,128)(2,1)S(1)} %get-tuple-element.24), channel_id=1, source_target_pairs={{0,8},{4,12},{8,0},{12,4},{16,24},{20,28},{24,16},{28,20},{32,40},... | collective-permute-start | bytes 589832 | tf_op jit(solution)/shard_map/ppermute | solution.py:265
  13.5 0.6 collective-permute-start.2
  14.1 1.7 %collective-permute-done.8.refs_3_ = bf16[240,128]{1,0:T(8,128)(2,1)S(1)} collective-permute-done((bf16[240,128]{1,0:T(8,128)(2,1)S(1)}, bf16[240,128]{1,0:T(8,128)(2,1)S(1)}, u32[]{:S(2)}, u32[]{:S(2)}) %collective-permute-start.8) | collective-permute-done | bytes 61472 | tf_op jit(solution)/shard_map/ppermute | solution.py:265
  15.8 3.1 %collective-permute-start.15 = (bf16[128,128]{1,0:T(8,128)(2,1)S(1)}, bf16[128,128]{1,0:T(8,128)(2,1)S(1)}, u32[]{:S(2)}, u32[]{:S(2)}) collective-permute-start(bf16[128,128]{1,0:T(8,128)(2,1)S(1)} %pad_maximum_fusion), channel_id=1, source_target_pairs={{0,64},{4,68},{8,72},{12,76},{16,80},{20,84},{24,88},{28,92},{32,9... | collective-permute-start | bytes 98312 | tf_op jit(solution)/shard_map/ppermute | solution.py:265
  18.9 3.5 %collective-permute-start.14 = (bf16[128,128]{1,0:T(8,128)(2,1)S(1)}, bf16[128,128]{1,0:T(8,128)(2,1)S(1)}, u32[]{:S(2)}, u32[]{:S(2)}) collective-permute-start(bf16[128,128]{1,0:T(8,128)(2,1)S(1)} %pad_maximum_fusion), channel_id=1, source_target_pairs={{0,80},{4,84},{8,88},{12,92},{16,64},{20,68},{24,72},{28,76},{32,1... | collective-permute-start | bytes 98312 | tf_op jit(solution)/shard_map/ppermute | solution.py:265
  22.5 9.0 %shard_map.46.refs_1_ = f32[4,2048,128]{2,1,0:T(8,128)} custom-call(bf16[2048,256]{1,0:T(8,128)(2,1)S(1)} %copy-done.1, bf16[2048,256]{1,0:T(8,128)(2,1)S(1)} %copy-done.3, bf16[2048,256]{1,0:T(8,128)(2,1)S(1)} %copy-done.5), custom_call_target="tpu_custom_call" | custom-call | flops 4294967296 | bytes 7340032 | tf_op jit(solution)/shard_map/pallas_call | solution.py:301
  31.5 2.8 %collective-permute-start.13 = (bf16[128,128]{1,0:T(8,128)(2,1)S(1)}, bf16[128,128]{1,0:T(8,128)(2,1)S(1)}, u32[]{:S(2)}, u32[]{:S(2)}) collective-permute-start(bf16[128,128]{1,0:T(8,128)(2,1)S(1)} %pad_maximum_fusion), channel_id=1, source_target_pairs={{0,96},{4,100},{8,104},{12,108},{16,112},{20,116},{24,120},{28,124... | collective-permute-start | bytes 98312 | tf_op jit(solution)/shard_map/ppermute | solution.py:265
  34.2 3.4 %collective-permute-start.11 = (bf16[640,128]{1,0:T(8,128)(2,1)S(1)}, bf16[640,128]{1,0:T(8,128)(2,1)S(1)}, u32[]{:S(2)}, u32[]{:S(2)}) collective-permute-start(bf16[640,128]{1,0:T(8,128)(2,1)S(1)} %get-tuple-element.46.refs_4_), channel_id=1, source_target_pairs={{0,16},{4,20},{8,24},{12,28},{16,0},{20,4},{24,8},{28,12},{32,48},... | collective-permute-start | bytes 491528 | tf_op jit(solution)/shard_map/ppermute | solution.py:265
  38.0 1.4 %collective-permute-start.9 = (bf16[640,128]{1,0:T(8,128)(2,1)S(1)}, bf16[640,128]{1,0:T(8,128)(2,1)S(1)}, u32[]{:S(2)}, u32[]{:S(2)}) collective-permute-start(bf16[640,128]{1,0:T(8,128)(2,1)S(1)} %get-tuple-element.46.refs_4_), channel_id=1, source_target_pairs={{0,48},{4,52},{8,56},{12,60},{16,32},{20,36},{24,40},{28,44},{32,1... | collective-permute-start | bytes 491528 | tf_op jit(solution)/shard_map/ppermute | solution.py:265
  39.3 6.4 %shard_map.49 = (bf16[512,128]{1,0:T(8,128)(2,1)S(1)}, bf16[512,128]{1,0:T(8,128)(2,1)S(1)}, bf16[512,128]{1,0:T(8,128)(2,1)S(1)}, bf16[512,128]{1,0:T(8,128)(2,1)S(1)}) custom-call(bf16[768,128]{1,0:T(8,128)(2,1)S(1)} %get-tuple-element.22.refs_0_, bf16[768,128]{1,0:T(8,128)(2,1)S(1)} %collective-permute-done.refs_1_, ...), custom_call_target="tpu_custom_call" | custom-call | flops 6442450944 | bytes 2097152 | tf_op jit(solution)/shard_map/pallas_call | solution.py:310
  46.9 2.4 %collective-permute-start.5 = (bf16[512,128]{1,0:T(8,128)(2,1)S(1)}, bf16[512,128]{1,0:T(8,128)(2,1)S(1)}, u32[]{:S(2)}, u32[]{:S(2)}) collective-permute-start(bf16[512,128]{1,0:T(8,128)(2,1)S(1)} %get-tuple-element.29), channel_id=1, source_target_pairs={{0,12},{4,8},{8,4},{12,0},{16,28},{20,24},{24,20},{28,16},{32,44},... | collective-permute-start | bytes 393224 | tf_op jit(solution)/shard_map/ppermute | solution.py:265
  49.4 2.5 %shard_map.51 = (bf16[160,128]{1,0:T(8,128)(2,1)S(1)}, bf16[160,128]{1,0:T(8,128)(2,1)S(1)}, bf16[160,128]{1,0:T(8,128)(2,1)S(1)}, bf16[160,128]{1,0:T(8,128)(2,1)S(1)}) custom-call(bf16[240,128]{1,0:T(8,128)(2,1)S(1)} %get-tuple-element.30.refs_0_, bf16[240,128]{1,0:T(8,128)(2,1)S(1)} %collective-permute-done.6.refs_1_, ...), custom_call_target="tpu_custom_call" | custom-call | flops 2147483648 | bytes 2097152 | tf_op jit(solution)/shard_map/pallas_call | solution.py:330
  53.0 2.4 %collective-permute-start.18 = (bf16[160,128]{1,0:T(8,128)(2,1)S(1)}, bf16[160,128]{1,0:T(8,128)(2,1)S(1)}, u32[]{:S(2)}, u32[]{:S(2)}) collective-permute-start(bf16[160,128]{1,0:T(8,128)(2,1)S(1)} %get-tuple-element.37), channel_id=1, source_target_pairs={{0,12},{4,8},{8,4},{12,0},{16,28},{20,24},{24,20},{28,16},{32,44},... | collective-permute-start | bytes 122888 | tf_op jit(solution)/shard_map/ppermute | solution.py:265
  55.4 2.3 %shard_map.47.refs_2_ = f32[4,512,128]{2,1,0:T(8,128)S(1)} custom-call(s32[5,4]{1,0:T(8,128)S(1)} %copy.10.refs_0_, bf16[2048,256]{1,0:T(8,128)(2,1)S(1)} %copy-done.2, bf16[2048,256]{1,0:T(8,128)(2,1)S(1)} %copy-done.4, bf16[2048,256]{1,0:T(8,128)(2,1)S(1)} %copy-done.5), custom_call_target="tpu_custom_call" | custom-call | flops 2147483648 | bytes 4194304 | tf_op jit(solution)/shard_map/pallas_call | solution.py:320
  57.8 2.9 %shard_map.50.refs_1_ = f32[4,2048,128]{2,1,0:T(8,128)S(1)} custom-call(s32[5,4]{1,0:T(8,128)S(1)} %copy.10.refs_0_, f32[4,2048,128]{2,1,0:T(8,128)S(1)} %copy-done, f32[4,512,128]{2,1,0:T(8,128)S(1)} %shard_map.47.refs_2_, bf16[512,128]{1,0:T(8,128)(2,1)S(1)} %get-tuple-element.26.refs_3_, ...), custom_call_target="tpu_custom_call", output_to_operand_aliasing={{}: (1, {})} | custom-call | bytes 10485760 | tf_op jit(solution)/shard_map/pallas_call | solution.py:340
  60.8 3.0 %shard_map.52 = (f32[4,2048,128]{2,1,0:T(8,128)S(1)}, bf16[2048,256]{1,0:T(8,128)(2,1)}) custom-call(s32[5,4]{1,0:T(8,128)S(1)} %copy.10.refs_0_, f32[4,2048,128]{2,1,0:T(8,128)S(1)} %shard_map.50.refs_1_, bf16[160,128]{1,0:T(8,128)(2,1)S(1)} %get-tuple-element.34.refs_2_, ...), custom_call_target="tpu_custom_call", output_to_operand_aliasing={{0}: (1, {})} | custom-call | bytes 6291456 | tf_op jit(solution)/shard_map/pallas_call | solution.py:349
  (43 shorter events, 2.7 us)
Async XLA Ops:
  0.8 1.2 %copy-start.1 = (bf16[2048,256]{1,0:T(8,128)(2,1)S(1)}, bf16[2048,256]{1,0:T(8,128)(2,1)}, u32[]{:S(2)}) copy-start(bf16[2048,256]{1,0:T(8,128)(2,1)} %refs_1_.3) | copy-start | bytes 3145732
  3.2 1.2 %copy-start.5 = (bf16[2048,256]{1,0:T(8,128)(2,1)S(1)}, bf16[2048,256]{1,0:T(8,128)(2,1)}, u32[]{:S(2)}) copy-start(bf16[2048,256]{1,0:T(8,128)(2,1)} %refs_3_.3) | copy-start | bytes 3145732
  6.3 7.2 %collective-permute-start.6 = (bf16[240,128]{1,0:T(8,128)(2,1)S(1)}, bf16[240,128]{1,0:T(8,128)(2,1)S(1)}, u32[]{:S(2)}, u32[]{:S(2)}) collective-permute-start(bf16[240,128]{1,0:T(8,128)(2,1)S(1)} %get-tuple-element.31), channel_id=1, source_target_pairs={{0,4},{4,0},{8,12},{12,8},{16,20},{20,16},{24,28},{28,24},{32,36},... | collective-permute-start | bytes 184328 | tf_op jit(solution)/shard_map/ppermute | solution.py:265
  8.1 6.0 %collective-permute-start.7 = (bf16[240,128]{1,0:T(8,128)(2,1)S(1)}, bf16[240,128]{1,0:T(8,128)(2,1)S(1)}, u32[]{:S(2)}, u32[]{:S(2)}) collective-permute-start(bf16[240,128]{1,0:T(8,128)(2,1)S(1)} %get-tuple-element.32), channel_id=1, source_target_pairs={{0,8},{4,12},{8,0},{12,4},{16,24},{20,28},{24,16},{28,20},{32,40},... | collective-permute-start | bytes 184328 | tf_op jit(solution)/shard_map/ppermute | solution.py:265
  10.0 5.8 %collective-permute-start.8 = (bf16[240,128]{1,0:T(8,128)(2,1)S(1)}, bf16[240,128]{1,0:T(8,128)(2,1)S(1)}, u32[]{:S(2)}, u32[]{:S(2)}) collective-permute-start(bf16[240,128]{1,0:T(8,128)(2,1)S(1)} %get-tuple-element.33), channel_id=1, source_target_pairs={{0,12},{4,8},{8,4},{12,0},{16,28},{20,24},{24,20},{28,16},{32,44},... | collective-permute-start | bytes 184328 | tf_op jit(solution)/shard_map/ppermute | solution.py:265
  10.0 24.3 %collective-permute-start = (bf16[768,128]{1,0:T(8,128)(2,1)S(1)}, bf16[768,128]{1,0:T(8,128)(2,1)S(1)}, u32[]{:S(2)}, u32[]{:S(2)}) collective-permute-start(bf16[768,128]{1,0:T(8,128)(2,1)S(1)} %get-tuple-element.23), channel_id=1, source_target_pairs={{0,4},{4,0},{8,12},{12,8},{16,20},{20,16},{24,28},{28,24},{32,36},... | collective-permute-start | bytes 589832 | tf_op jit(solution)/shard_map/ppermute | solution.py:265
  11.6 26.1 %collective-permute-start.1 = (bf16[768,128]{1,0:T(8,128)(2,1)S(1)}, bf16[768,128]{1,0:T(8,128)(2,1)S(1)}, u32[]{:S(2)}, u32[]{:S(2)}) collective-permute-start(bf16[768,128]{1,0:T(8,128)(2,1)S(1)} %get-tuple-element.24), channel_id=1, source_target_pairs={{0,8},{4,12},{8,0},{12,4},{16,24},{20,28},{24,16},{28,20},{32,40},... | collective-permute-start | bytes 589832 | tf_op jit(solution)/shard_map/ppermute | solution.py:265
  13.5 24.5 %collective-permute-start.2 = (bf16[768,128]{1,0:T(8,128)(2,1)S(1)}, bf16[768,128]{1,0:T(8,128)(2,1)S(1)}, u32[]{:S(2)}, u32[]{:S(2)}) collective-permute-start(bf16[768,128]{1,0:T(8,128)(2,1)S(1)} %get-tuple-element.25), channel_id=1, source_target_pairs={{0,12},{4,8},{8,4},{12,0},{16,28},{20,24},{24,20},{28,16},{32,44},... | collective-permute-start | bytes 589832 | tf_op jit(solution)/shard_map/ppermute | solution.py:265
  15.8 15.6 %collective-permute-start.15 = (bf16[128,128]{1,0:T(8,128)(2,1)S(1)}, bf16[128,128]{1,0:T(8,128)(2,1)S(1)}, u32[]{:S(2)}, u32[]{:S(2)}) collective-permute-start(bf16[128,128]{1,0:T(8,128)(2,1)S(1)} %pad_maximum_fusion), channel_id=1, source_target_pairs={{0,64},{4,68},{8,72},{12,76},{16,80},{20,84},{24,88},{28,92},{32,9... | collective-permute-start | bytes 98312 | tf_op jit(solution)/shard_map/ppermute | solution.py:265
  18.9 15.3 %collective-permute-start.14 = (bf16[128,128]{1,0:T(8,128)(2,1)S(1)}, bf16[128,128]{1,0:T(8,128)(2,1)S(1)}, u32[]{:S(2)}, u32[]{:S(2)}) collective-permute-start(bf16[128,128]{1,0:T(8,128)(2,1)S(1)} %pad_maximum_fusion), channel_id=1, source_target_pairs={{0,80},{4,84},{8,88},{12,92},{16,64},{20,68},{24,72},{28,76},{32,1... | collective-permute-start | bytes 98312 | tf_op jit(solution)/shard_map/ppermute | solution.py:265
  31.5 14.3 %collective-permute-start.13 = (bf16[128,128]{1,0:T(8,128)(2,1)S(1)}, bf16[128,128]{1,0:T(8,128)(2,1)S(1)}, u32[]{:S(2)}, u32[]{:S(2)}) collective-permute-start(bf16[128,128]{1,0:T(8,128)(2,1)S(1)} %pad_maximum_fusion), channel_id=1, source_target_pairs={{0,96},{4,100},{8,104},{12,108},{16,112},{20,116},{24,120},{28,124... | collective-permute-start | bytes 98312 | tf_op jit(solution)/shard_map/ppermute | solution.py:265
  34.2 12.1 %collective-permute-start.12 = (bf16[128,128]{1,0:T(8,128)(2,1)S(1)}, bf16[128,128]{1,0:T(8,128)(2,1)S(1)}, u32[]{:S(2)}, u32[]{:S(2)}) collective-permute-start(bf16[128,128]{1,0:T(8,128)(2,1)S(1)} %pad_maximum_fusion), channel_id=1, source_target_pairs={{0,112},{4,116},{8,120},{12,124},{16,96},{20,100},{24,104},{28,108... | collective-permute-start | bytes 98312 | tf_op jit(solution)/shard_map/ppermute | solution.py:265
  34.2 12.7 %collective-permute-start.11 = (bf16[640,128]{1,0:T(8,128)(2,1)S(1)}, bf16[640,128]{1,0:T(8,128)(2,1)S(1)}, u32[]{:S(2)}, u32[]{:S(2)}) collective-permute-start(bf16[640,128]{1,0:T(8,128)(2,1)S(1)} %get-tuple-element.46.refs_4_), channel_id=1, source_target_pairs={{0,16},{4,20},{8,24},{12,28},{16,0},{20,4},{24,8},{28,12},{32,48},... | collective-permute-start | bytes 491528 | tf_op jit(solution)/shard_map/ppermute | solution.py:265
  37.7 11.7 %collective-permute-start.10 = (bf16[640,128]{1,0:T(8,128)(2,1)S(1)}, bf16[640,128]{1,0:T(8,128)(2,1)S(1)}, u32[]{:S(2)}, u32[]{:S(2)}) collective-permute-start(bf16[640,128]{1,0:T(8,128)(2,1)S(1)} %get-tuple-element.46.refs_4_), channel_id=1, source_target_pairs={{0,32},{4,36},{8,40},{12,44},{16,48},{20,52},{24,56},{28,60},{32,0... | collective-permute-start | bytes 491528 | tf_op jit(solution)/shard_map/ppermute | solution.py:265
  38.0 11.4 %collective-permute-start.9 = (bf16[640,128]{1,0:T(8,128)(2,1)S(1)}, bf16[640,128]{1,0:T(8,128)(2,1)S(1)}, u32[]{:S(2)}, u32[]{:S(2)}) collective-permute-start(bf16[640,128]{1,0:T(8,128)(2,1)S(1)} %get-tuple-element.46.refs_4_), channel_id=1, source_target_pairs={{0,48},{4,52},{8,56},{12,60},{16,32},{20,36},{24,40},{28,44},{32,1... | collective-permute-start | bytes 491528 | tf_op jit(solution)/shard_map/ppermute | solution.py:265
  45.8 9.7 %copy-start.2 = (bf16[2048,256]{1,0:T(8,128)(2,1)S(1)}, bf16[2048,256]{1,0:T(8,128)(2,1)}, u32[]{:S(2)}) copy-start(bf16[2048,256]{1,0:T(8,128)(2,1)} %refs_1_.3) | copy-start | bytes 3145732
  45.8 9.7 %copy-start.4 = (bf16[2048,256]{1,0:T(8,128)(2,1)S(1)}, bf16[2048,256]{1,0:T(8,128)(2,1)}, u32[]{:S(2)}) copy-start(bf16[2048,256]{1,0:T(8,128)(2,1)} %refs_2_.3) | copy-start | bytes 3145732
  45.8 7.2 %collective-permute-start.3 = (bf16[512,128]{1,0:T(8,128)(2,1)S(1)}, bf16[512,128]{1,0:T(8,128)(2,1)S(1)}, u32[]{:S(2)}, u32[]{:S(2)}) collective-permute-start(bf16[512,128]{1,0:T(8,128)(2,1)S(1)} %get-tuple-element.27), channel_id=1, source_target_pairs={{0,4},{4,0},{8,12},{12,8},{16,20},{20,16},{24,28},{28,24},{32,36},... | collective-permute-start | bytes 393224 | tf_op jit(solution)/shard_map/ppermute | solution.py:265
  46.3 11.4 %collective-permute-start.4 = (bf16[512,128]{1,0:T(8,128)(2,1)S(1)}, bf16[512,128]{1,0:T(8,128)(2,1)S(1)}, u32[]{:S(2)}, u32[]{:S(2)}) collective-permute-start(bf16[512,128]{1,0:T(8,128)(2,1)S(1)} %get-tuple-element.28), channel_id=1, source_target_pairs={{0,8},{4,12},{8,0},{12,4},{16,24},{20,28},{24,16},{28,20},{32,40},... | collective-permute-start | bytes 393224 | tf_op jit(solution)/shard_map/ppermute | solution.py:265
  46.9 10.9 %collective-permute-start.5 = (bf16[512,128]{1,0:T(8,128)(2,1)S(1)}, bf16[512,128]{1,0:T(8,128)(2,1)S(1)}, u32[]{:S(2)}, u32[]{:S(2)}) collective-permute-start(bf16[512,128]{1,0:T(8,128)(2,1)S(1)} %get-tuple-element.29), channel_id=1, source_target_pairs={{0,12},{4,8},{8,4},{12,0},{16,28},{20,24},{24,20},{28,16},{32,44},... | collective-permute-start | bytes 393224 | tf_op jit(solution)/shard_map/ppermute | solution.py:265
  51.9 6.0 %copy-start = (f32[4,2048,128]{2,1,0:T(8,128)S(1)}, f32[4,2048,128]{2,1,0:T(8,128)}, u32[]{:S(2)}) copy-start(f32[4,2048,128]{2,1,0:T(8,128)} %shard_map.46.refs_1_) | copy-start | bytes 12582916
  51.9 8.9 %collective-permute-start.16 = (bf16[160,128]{1,0:T(8,128)(2,1)S(1)}, bf16[160,128]{1,0:T(8,128)(2,1)S(1)}, u32[]{:S(2)}, u32[]{:S(2)}) collective-permute-start(bf16[160,128]{1,0:T(8,128)(2,1)S(1)} %get-tuple-element.35), channel_id=1, source_target_pairs={{0,4},{4,0},{8,12},{12,8},{16,20},{20,16},{24,28},{28,24},{32,36},... | collective-permute-start | bytes 122888 | tf_op jit(solution)/shard_map/ppermute | solution.py:265
  52.4 8.3 %collective-permute-start.17 = (bf16[160,128]{1,0:T(8,128)(2,1)S(1)}, bf16[160,128]{1,0:T(8,128)(2,1)S(1)}, u32[]{:S(2)}, u32[]{:S(2)}) collective-permute-start(bf16[160,128]{1,0:T(8,128)(2,1)S(1)} %get-tuple-element.36), channel_id=1, source_target_pairs={{0,8},{4,12},{8,0},{12,4},{16,24},{20,28},{24,16},{28,20},{32,40},... | collective-permute-start | bytes 122888 | tf_op jit(solution)/shard_map/ppermute | solution.py:265
  53.0 7.8 %collective-permute-start.18 = (bf16[160,128]{1,0:T(8,128)(2,1)S(1)}, bf16[160,128]{1,0:T(8,128)(2,1)S(1)}, u32[]{:S(2)}, u32[]{:S(2)}) collective-permute-start(bf16[160,128]{1,0:T(8,128)(2,1)S(1)} %get-tuple-element.37), channel_id=1, source_target_pairs={{0,12},{4,8},{8,4},{12,0},{16,28},{20,24},{24,20},{28,16},{32,44},... | collective-permute-start | bytes 122888 | tf_op jit(solution)/shard_map/ppermute | solution.py:265
  (1 other events, 1.2 us)

commit v2 on v1

--- a/solution.py
+++ b/solution.py
@@ -7,6 +7,7 @@
 
 
 SEG = 512
+PACK_MIB = 24
 RATE1 = 4
 bf16 = jnp.bfloat16
 f32 = jnp.float32
@@ -94,7 +95,7 @@
 
 
 def pack_kernel(levels, offs_any, q_any, k_any, v_any, *rest):
-    near_out, far_out, (qs, ks, vs, qb, kb, vb, offs, sems) = rest[0:4], rest[4:8], rest[8:]
+    near_out, far_out, (qb, kb, vb, qs, ks, vs, offs, sems) = rest[0:4], rest[4:8], rest[8:]
     mine = lax.rem(lax.axis_index("seq"), 4)
     copies = [fetch(k_any, kb, sems.at[0]), fetch(v_any, vb, sems.at[1])]
     copies += [fetch(q_any, qb, sems.at[2]), fetch(offs_any, offs, sems.at[3])]
@@ -108,7 +109,7 @@
         base = [0, 0]
         for what in ("kv", "q"):
             for level, count, rate, near in levels:
-                off = offs[level, head]
+                off = offs[head, level]
                 ref = near_out[d] if near else far_out[d]
                 at = base[near]
                 if what == "kv":
@@ -127,32 +128,30 @@
                     base[near] = at + few
 
 
-def first_kernel(q_ref, k_ref, v_ref, t_ref):
+def first_kernel(pair, q_ref, k_ref, v_ref, *rest):
+    t_ref = rest[-1]
     zero, one = jnp.asarray(0, bf16), jnp.asarray(1, bf16)
     scale = jnp.asarray(0.125, bf16)
+    cols = slice(pair * LANES, (pair + 1) * LANES)
 
     @pl.loop(0, q_ref.shape[0] // SEG)
     def _(s):
         part = pl.ds(pl.multiple_of(s * SEG, SEG), SEG)
-        for h in range(4):
-            cols = slice(h // 2 * LANES, (h // 2 + 1) * LANES)
-            vl = half_mask(SEG, h % 2)
+        for h in range(2):
+            vl = half_mask(SEG, h)
             q = q_ref[part, cols] * scale
             k = jnp.where(vl, k_ref[part, cols], zero)
             v = jnp.where(vl, v_ref[part, cols], one)
             t_ref[h, part, :] = softmax_tile(q, [k], [v], vl)
 
 
-def second_kernel(rate, offs_any, q_ref, k_ref, v_ref, found_ref, qs, ks, vs, offs, sem):
+def second_kernel(rate, offs_any, qs, ks, vs, found_ref, offs, sem):
     copy = fetch(offs_any, offs, sem)
-    count = q_ref.shape[0] // rate
-    widen(q_ref, qs)
-    widen(k_ref, ks)
-    widen(v_ref, vs)
+    count = found_ref.shape[1]
     copy.wait()
     for h in range(4):
         vl = half_mask(count, h % 2)
-        picked = pl.ds(offs[1, h], count, rate)
+        picked = pl.ds(offs[h, 1], count, rate)
         q = (qs[h // 2, picked, :] * 0.125).astype(bf16)
         k = jnp.where(vl, ks[h // 2, picked, :], 0.0).astype(bf16)
         v = jnp.where(vl, vs[h // 2, picked, :], 1.0).astype(bf16)
@@ -180,12 +179,12 @@
 
 
 def far_kernel(mid, top, *refs):
-    far, gathered, tops, outs = refs[:4], refs[4:8], refs[8:12], refs[12:16]
+    far, gathered, outs = refs[:4], refs[4:8], refs[8:12]
     half = lax.rem(lax.axis_index("seq"), 2)
     base = mid + top
     blocks = (
         ([r[: 4 * mid, :] for r in gathered], base, mid // 2, 0),
-        ([r[4 * mid :, :] for r in gathered] + [r[...] for r in tops], base + mid // 2, top // 2, mid),
+        ([r[4 * mid :, :] for r in gathered], base + mid // 2, top // 2, mid),
     )
     for tiles, q_at, few, out_at in blocks:
         keys, values = zip(*[keys_values(t, half) for t in tiles])
@@ -199,34 +198,35 @@
                 outs[d][at : at + few, :] = found[start : start + few, :].astype(bf16)
 
 
-def absorb(state, head, half, off, rate, coded):
-    count = coded.shape[0]
-    vl = half_mask(count, half)
+def absorb(state, head, off, rate, new, lse_new):
+    count = new.shape[0]
+    vl = half_mask(count, lax.rem(head, 2))
     picked = pl.ds(off, count, rate)
     old = state[head, picked, :]
-    state[head, picked, :] = merge(
-        vl, old, spread_lse(old, vl), coded.astype(f32), decode_lse(coded, half)
-    )
-
-
-def blend_kernel(rate, offs_any, state_in, found_ref, *refs):
+    state[head, picked, :] = merge(vl, old, spread_lse(old, vl), new, lse_new)
+
+
+def absorb_coded(state, head, off, rate, coded):
+    absorb(state, head, off, rate, coded.astype(f32), decode_lse(coded, lax.rem(head, 2)))
+
+
+def blend_kernel(rate, offs_any, low, high, found_ref, *refs):
     near, state, offs, sem = refs[:4], refs[4], refs[5], refs[6]
     copy = fetch(offs_any, offs, sem)
     mine = lax.rem(lax.axis_index("seq"), 4)
+    for h in range(4):
+        state[h, :, :] = (low, high)[h // 2][h % 2, :, :]
     copy.wait()
-    count = found_ref.shape[1]
     for h in range(4):
-        vl = half_mask(count, h % 2)
-        picked = pl.ds(offs[1, h], count, rate)
-        old, new = state[h, picked, :], found_ref[h, :, :]
-        state[h, picked, :] = merge(vl, old, spread_lse(old, vl), new, spread_lse(new, vl))
+        new = found_ref[h, :, :]
+        absorb(state, h, offs[h, 1], rate, new, spread_lse(new, half_mask(new.shape[0], h % 2)))
     for d in range(4):
         head = mine ^ d
-        absorb(state, head, lax.rem(head, 2), offs[2, head], rate, near[d][...])
+        absorb_coded(state, head, offs[head, 2], rate, near[d][...])
 
 
 def final_kernel(levels, offs_any, state_in, *refs):
-    far, state, out_ref, offs, sem = refs[:4], refs[4], refs[5], refs[6], refs[7]
+    far, state, out_any, offs, out, sem, sems = refs[:4], refs[4], refs[5], refs[6], refs[7], refs[8], refs[9]
     copy = fetch(offs_any, offs, sem)
     mine = lax.rem(lax.axis_index("seq"), 4)
     copy.wait()
@@ -235,28 +235,36 @@
         at = 0
         for level, count, rate, near in levels:
             if not near:
-                absorb(
-                    state, head, lax.rem(head, 2), offs[level, head], rate, far[d][at : at + count, :]
-                )
+                absorb_coded(state, head, offs[head, level], rate, far[d][at : at + count, :])
                 at += count
-    vl = half_mask(out_ref.shape[0], 0)
-    for p in range(2):
-        out_ref[:, p * LANES : (p + 1) * LANES] = jnp.where(
-            vl, state[2 * p, :, :], state[2 * p + 1, :, :]
-        ).astype(bf16)
-
-
-def call(body, outs, spaces, scratch=(), flops=0, bytes_moved=0, exps=0, aliases=None):
+    step = SEG
+    vl = half_mask(step, 0)
+    copies = []
+    for i in range(out.shape[0] // step):
+        part = slice(i * step, (i + 1) * step)
+        for p in range(2):
+            out[part, p * LANES : (p + 1) * LANES] = jnp.where(
+                vl, state[2 * p, part, :], state[2 * p + 1, part, :]
+            ).astype(bf16)
+        copies.append(pltpu.make_async_copy(out.at[part, :], out_any.at[part, :], sems.at[i]))
+        copies[-1].start()
+    for copy in copies:
+        copy.wait()
+
+
+def call(
+    body, outs, spaces, scratch=(), flops=0, bytes_moved=0, exps=0, aliases=None, out_spaces="", mib=24
+):
     whole = pl.BlockSpec(memory_space=VMEM)
     place = {"v": whole, "a": pl.BlockSpec(memory_space=pltpu.HBM)}
     return pl.pallas_call(
         body,
         out_shape=outs,
         in_specs=[place[c] for c in spaces],
-        out_specs=jax.tree.map(lambda _: whole, outs),
+        out_specs=[place[c] for c in out_spaces] if out_spaces else jax.tree.map(lambda _: whole, outs),
         scratch_shapes=list(scratch),
         input_output_aliases=aliases or {},
-        compiler_params=pltpu.CompilerParams(vmem_limit_bytes=48 << 20),
+        compiler_params=pltpu.CompilerParams(vmem_limit_bytes=mib << 20),
         cost_estimate=pl.CostEstimate(flops=flops, bytes_accessed=bytes_moved, transcendentals=exps),
     )
 
@@ -278,34 +286,46 @@
         (3, mid, rate_three, False),
         (4, top, rate_four, False),
     )
-    wide = VMEM((2, rows, LANES), f32)
-    narrow = VMEM((rows, width), bf16)
+    offsets = offsets.T
     table = pltpu.SMEM(offsets.shape, jnp.int32)
     one_sem = pltpu.SemaphoreType.DMA
 
     def tile(n, kind=bf16):
         return jax.ShapeDtypeStruct((n, LANES), kind)
 
+    wide = jax.ShapeDtypeStruct((2, rows, LANES), f32)
     state_shape = jax.ShapeDtypeStruct((4, rows, LANES), f32)
     parts = call(
         lambda *refs: pack_kernel(levels, *refs),
-        [tile(near_count * 3 // 2)] * 4 + [tile((mid + top) * 3 // 2)] * 4,
+        [tile(near_count * 3 // 2)] * 4
+        + [tile((mid + top) * 3 // 2)] * 4
+        + [jax.ShapeDtypeStruct(query.shape, bf16)] * 3
+        + [wide] * 3,
         "aaaa",
-        (wide, wide, wide, narrow, narrow, narrow, table, pltpu.SemaphoreType.DMA((4,))),
+        (table, pltpu.SemaphoreType.DMA((4,))),
         bytes_moved=5 << 20,
-    )(offsets, query, key, value)
-    near_sent, far_sent = parts[:4], parts[4:]
+        mib=PACK_MIB,
+    )(*(pltpu.with_memory_space_constraint(x, pltpu.HBM) for x in (offsets, query, key, value)))
+    near_sent, far_sent, narrow, wides = parts[:4], parts[4:8], parts[8:11], parts[11:]
     far_held = [far_sent[0]] + [swapped(far_sent[d], d) for d in (1, 2, 3)]
     near_held = [near_sent[0]] + [swapped(near_sent[d], d) for d in (1, 2, 3)]
 
-    state = call(
-        first_kernel, state_shape, "vvv", flops=4 << 30, bytes_moved=7 << 20, exps=4 << 20
-    )(query, key, value)
+    states = [
+        call(
+            lambda *refs, pair=pair: first_kernel(pair, *refs),
+            wide,
+            "vvv",
+            flops=2 << 30,
+            bytes_moved=4 << 20,
+            exps=2 << 20,
+        )(*narrow)
+        for pair in range(2)
+    ]
 
     own_top = jnp.concatenate([r[mid : mid + top] for r in far_held], axis=0)
-    held = jnp.concatenate([r[:mid] for r in far_held] + [own_top], axis=0)
-    gathered = [held] + [swapped(held, b) for b in (12, 8, 4)]
-    tops = [swapped(own_top, 16 + b) for b in (12, 8, 4, 0)]
+    other_top = swapped(own_top, 16)
+    held = jnp.concatenate([r[:mid] for r in far_held] + [own_top, other_top], axis=0)
+    gathered = [held] + [swapped(held, b) for b in (8, 4, 12)]
 
     near_found = call(
         lambda *refs: near_kernel(near_count, *refs),
@@ -321,38 +341,38 @@
         lambda *refs: second_kernel(RATE1, *refs),
         jax.ShapeDtypeStruct((4, near_count, LANES), f32),
         "avvv",
-        (wide, wide, wide, table, one_sem),
+        (table, one_sem),
         flops=2 << 30,
         bytes_moved=4 << 20,
         exps=1 << 20,
-    )(offsets, query, key, value)
+    )(offsets, *wides)
 
     far_found = call(
         lambda *refs: far_kernel(mid, top, *refs),
         [tile(mid + top)] * 4,
-        "v" * 12,
+        "v" * 8,
         flops=2 << 30,
         bytes_moved=2 << 20,
         exps=1 << 20,
-    )(*far_held, *gathered, *tops)
+    )(*far_held, *gathered)
     far_back = [far_found[0]] + [swapped(far_found[d], d) for d in (1, 2, 3)]
 
     state = call(
         lambda *refs: blend_kernel(RATE1, *refs),
         state_shape,
-        "avvvvvv",
+        "avvvvvvv",
         (table, one_sem),
         bytes_moved=10 << 20,
-        aliases={1: 0},
-    )(offsets, state, found, *near_back)
+    )(offsets, *states, found, *near_back)
 
     return call(
         lambda *refs: final_kernel(levels, *refs),
         [state_shape, jax.ShapeDtypeStruct((rows, width), bf16)],
         "avvvvv",
-        (table, one_sem),
+        (table, VMEM((rows, width), bf16), one_sem, pltpu.SemaphoreType.DMA((rows // SEG,))),
         bytes_moved=6 << 20,
         aliases={1: 0},
+        out_spaces="va",
     )(offsets, state, *far_back)[1]
 
 

time: 64.1 us -> 52.6 us (0.82)
  starting transfers between devices: 29.4 us -> 22.9 us
  local copies, waits for them, and re-layouts: 4.52 us -> 0.09 us
  waiting for transfers between devices: 1.7 us -> 0.04 us
  Pallas kernels: 28 us -> 29.1 us
    ppermute x19 -> x16, starting transfers between devices: 29.4 us -> 22.9 us  [swapped(): lax.ppermute(shard, 'seq', [(i, i ^ bits) for i in range(lax.axis_size('s...]
    unnamed x17 -> x6, local copies, waits for them, and re-layouts: 4.49 us -> 0.04 us
    ppermute x19 -> x16, waiting for transfers between devices: 1.7 us -> 0.04 us  [swapped(): lax.ppermute(shard, 'seq', [(i, i ^ bits) for i in range(lax.axis_size('s...]
    pallas_call x1, Pallas kernels: 1.84 us -> 3.07 us  [per_device(): call(lambda *refs: pack_kernel(levels, *refs), [tile(near_count * 3 // 2)...]
    pallas_call x2 -> x3, Pallas kernels: 11.9 us -> 12 us  [the longest x2 9.32 us: per_device(): call(lambda *refs, pair=pair: first_kernel(pair, *refs), wide, 'vvv', flo...]
  transfers between devices with their start and end apart: 19 -> 16, of which waited for: 1 -> 0; matrix products, arithmetic and copies ran while one was open for 0% -> 0% of each run, Pallas kernels for 36% -> 44%
where the time goes in v2:
time: 52.6 us; the launch traced here: 52.5 us
  Pallas kernels  29.1 us (55%)
  starting transfers between devices  22.9 us (44%)
    ppermute x16, starting transfers between devices, swapped(): lax.ppermute(shard, 'seq', [(i, i ^ bits) for i in range(lax.axis_size('s...  22.9 us
    pallas_call x2, Pallas kernels, per_device(): call(lambda *refs, pair=pair: first_kernel(pair, *refs), wide, 'vvv', flo...  9.32 us
    pallas_call x1, Pallas kernels, per_device(): call(lambda *refs: near_kernel(near_count, *refs), [tile(near_count)] * 4...  6.46 us
    pallas_call x1, Pallas kernels, per_device(): call(lambda *refs: pack_kernel(levels, *refs), [tile(near_count * 3 // 2)...  3.07 us
    pallas_call x1, Pallas kernels, per_device(): call(lambda *refs: final_kernel(levels, *refs), [state_shape, jax.ShapeDt...  2.73 us
    pallas_call x1, Pallas kernels, per_device(): call(lambda *refs: blend_kernel(RATE1, *refs), state_shape, 'avvvvvvv', (...  2.72 us
    pallas_call x1, Pallas kernels, per_device(): call(lambda *refs: far_kernel(mid, top, *refs), [tile(mid + top)] * 4, 'v...  2.49 us
    pallas_call x1, Pallas kernels, per_device(): call(lambda *refs: second_kernel(RATE1, *refs), jax.ShapeDtypeStruct((4,...  2.34 us
  transfers between devices with their start and end apart: 16, of which 0 were waited for; matrix products, arithmetic and copies ran while one was open for 0% of the time, Pallas kernels for 44%

profile of v2, /device:TPU:0, one launch (start us, length us, event | category | flops | bytes accessed | tf_op | source)
XLA Modules:
  0.0 52.5 jit_solution(13975351893030022236)
XLA Ops:
  0.0 3.1 %shard_map.46 = (bf16[768,128]{1,0:T(8,128)(2,1)S(1)}, bf16[768,128]{1,0:T(8,128)(2,1)S(1)}, bf16[768,128]{1,0:T(8,128)(2,1)S(1)}, bf16[768,128]{1,0:T(8,128)(2,...) custom-call(s32[4,5]{1,0:T(4,128)} %bitcast.1, ...), custom_call_target="tpu_custom_call" | custom-call | bytes 5242880 | tf_op jit(solution)/shard_map/pallas_call | solution.py:298
  3.1 1.8 %collective-permute-start.6 = (bf16[240,128]{1,0:T(8,128)(2,1)S(1)}, bf16[240,128]{1,0:T(8,128)(2,1)S(1)}, u32[]{:S(2)}, u32[]{:S(2)}) collective-permute-start(bf16[240,128]{1,0:T(8,128)(2,1)S(1)} %get-tuple-element.43), channel_id=1, source_target_pairs={{0,4},{4,0},{8,12},{12,8},{16,20},{20,16},{24,28},{28,24},{32,36},... | collective-permute-start | bytes 184328 | tf_op jit(solution)/shard_map/ppermute | solution.py:273
  4.8 1.9 %collective-permute-start.7 = (bf16[240,128]{1,0:T(8,128)(2,1)S(1)}, bf16[240,128]{1,0:T(8,128)(2,1)S(1)}, u32[]{:S(2)}, u32[]{:S(2)}) collective-permute-start(bf16[240,128]{1,0:T(8,128)(2,1)S(1)} %get-tuple-element.44), channel_id=1, source_target_pairs={{0,8},{4,12},{8,0},{12,4},{16,24},{20,28},{24,16},{28,20},{32,40},... | collective-permute-start | bytes 184328 | tf_op jit(solution)/shard_map/ppermute | solution.py:273
  6.8 1.6 %collective-permute-start = (bf16[768,128]{1,0:T(8,128)(2,1)S(1)}, bf16[768,128]{1,0:T(8,128)(2,1)S(1)}, u32[]{:S(2)}, u32[]{:S(2)}) collective-permute-start(bf16[768,128]{1,0:T(8,128)(2,1)S(1)} %get-tuple-element.35), channel_id=1, source_target_pairs={{0,4},{4,0},{8,12},{12,8},{16,20},{20,16},{24,28},{28,24},{32,36},... | collective-permute-start | bytes 589832 | tf_op jit(solution)/shard_map/ppermute | solution.py:273
  8.3 1.9 %collective-permute-start.1 = (bf16[768,128]{1,0:T(8,128)(2,1)S(1)}, bf16[768,128]{1,0:T(8,128)(2,1)S(1)}, u32[]{:S(2)}, u32[]{:S(2)}) collective-permute-start(bf16[768,128]{1,0:T(8,128)(2,1)S(1)} %get-tuple-element.36), channel_id=1, source_target_pairs={{0,8},{4,12},{8,0},{12,4},{16,24},{20,28},{24,16},{28,20},{32,40},... | collective-permute-start | bytes 589832 | tf_op jit(solution)/shard_map/ppermute | solution.py:273
  10.3 4.7 %shard_map.48.refs_2_ = f32[2,2048,128]{2,1,0:T(8,128)S(1)} custom-call(bf16[2048,256]{1,0:T(8,128)(2,1)S(1)} %get-tuple-element.28.refs_0_, bf16[2048,256]{1,0:T(8,128)(2,1)S(1)} %get-tuple-element.29.refs_1_, bf16[2048,256]{1,0:T(8,128)(2,1)S(1)} %get-tuple-element.30.refs_2_), custom_call_target="tpu_custom_call" | custom-call | flops 2147483648 | bytes 4194304 | tf_op jit(solution)/shard_map/pallas_call | solution.py:314
  14.9 0.0 collective-permute-done.6.refs_1_
  14.9 0.1 collective-permute-start.2
  15.2 3.1 %collective-permute-start.9 = (bf16[128,128]{1,0:T(8,128)(2,1)S(1)}, bf16[128,128]{1,0:T(8,128)(2,1)S(1)}, u32[]{:S(2)}, u32[]{:S(2)}) collective-permute-start(bf16[128,128]{1,0:T(8,128)(2,1)S(1)} %pad_maximum_fusion), channel_id=1, source_target_pairs={{0,64},{4,68},{8,72},{12,76},{16,80},{20,84},{24,88},{28,92},{32,9... | collective-permute-start | bytes 98312 | tf_op jit(solution)/shard_map/ppermute | solution.py:273
  18.3 4.7 %shard_map.47.refs_1_ = f32[2,2048,128]{2,1,0:T(8,128)S(1)} custom-call(bf16[2048,256]{1,0:T(8,128)(2,1)S(1)} %get-tuple-element.28.refs_0_, bf16[2048,256]{1,0:T(8,128)(2,1)S(1)} %get-tuple-element.29.refs_1_, bf16[2048,256]{1,0:T(8,128)(2,1)S(1)} %get-tuple-element.30.refs_2_), custom_call_target="tpu_custom_call" | custom-call | flops 2147483648 | bytes 4194304 | tf_op jit(solution)/shard_map/pallas_call | solution.py:314
  23.0 0.7 %collective-permute-start.10 = (bf16[768,128]{1,0:T(8,128)(2,1)S(1)}, bf16[768,128]{1,0:T(8,128)(2,1)S(1)}, u32[]{:S(2)}, u32[]{:S(2)}) collective-permute-start(bf16[768,128]{1,0:T(8,128)(2,1)S(1)} %constant_dynamic-update-slice_fusion.refs_4_), channel_id=1, source_target_pairs={{0,32},{4,36},{8,40},{12,44},{16,48},{20,52},{24,56},{28,60},{32,0... | collective-permute-start | bytes 589832 | tf_op jit(solution)/shard_map/ppermute | solution.py:273
  23.6 3.8 %collective-permute-start.11 = (bf16[768,128]{1,0:T(8,128)(2,1)S(1)}, bf16[768,128]{1,0:T(8,128)(2,1)S(1)}, u32[]{:S(2)}, u32[]{:S(2)}) collective-permute-start(bf16[768,128]{1,0:T(8,128)(2,1)S(1)} %constant_dynamic-update-slice_fusion.refs_4_), channel_id=1, source_target_pairs={{0,16},{4,20},{8,24},{12,28},{16,0},{20,4},{24,8},{28,12},{32,48},... | collective-permute-start | bytes 589832 | tf_op jit(solution)/shard_map/ppermute | solution.py:273
  27.5 0.9 %collective-permute-start.12 = (bf16[768,128]{1,0:T(8,128)(2,1)S(1)}, bf16[768,128]{1,0:T(8,128)(2,1)S(1)}, u32[]{:S(2)}, u32[]{:S(2)}) collective-permute-start(bf16[768,128]{1,0:T(8,128)(2,1)S(1)} %constant_dynamic-update-slice_fusion.refs_4_), channel_id=1, source_target_pairs={{0,48},{4,52},{8,56},{12,60},{16,32},{20,36},{24,40},{28,44},{32,1... | collective-permute-start | bytes 589832 | tf_op jit(solution)/shard_map/ppermute | solution.py:273
  28.4 6.5 %shard_map.50 = (bf16[512,128]{1,0:T(8,128)(2,1)S(1)}, bf16[512,128]{1,0:T(8,128)(2,1)S(1)}, bf16[512,128]{1,0:T(8,128)(2,1)S(1)}, bf16[512,128]{1,0:T(8,128)(2,1)S(1)}) custom-call(bf16[768,128]{1,0:T(8,128)(2,1)S(1)} %get-tuple-element.34.refs_0_, bf16[768,128]{1,0:T(8,128)(2,1)S(1)} %collective-permute-done.refs_1_, ...), custom_call_target="tpu_custom_call" | custom-call | flops 6442450944 | bytes 2097152 | tf_op jit(solution)/shard_map/pallas_call | solution.py:330
  34.8 1.6 %collective-permute-start.3 = (bf16[512,128]{1,0:T(8,128)(2,1)S(1)}, bf16[512,128]{1,0:T(8,128)(2,1)S(1)}, u32[]{:S(2)}, u32[]{:S(2)}) collective-permute-start(bf16[512,128]{1,0:T(8,128)(2,1)S(1)} %get-tuple-element.39), channel_id=1, source_target_pairs={{0,4},{4,0},{8,12},{12,8},{16,20},{20,16},{24,28},{28,24},{32,36},... | collective-permute-start | bytes 393224 | tf_op jit(solution)/shard_map/ppermute | solution.py:273
  36.5 1.6 %collective-permute-start.4 = (bf16[512,128]{1,0:T(8,128)(2,1)S(1)}, bf16[512,128]{1,0:T(8,128)(2,1)S(1)}, u32[]{:S(2)}, u32[]{:S(2)}) collective-permute-start(bf16[512,128]{1,0:T(8,128)(2,1)S(1)} %get-tuple-element.40), channel_id=1, source_target_pairs={{0,8},{4,12},{8,0},{12,4},{16,24},{20,28},{24,16},{28,20},{32,40},... | collective-permute-start | bytes 393224 | tf_op jit(solution)/shard_map/ppermute | solution.py:273
  38.0 0.4 collective-permute-start.5
  38.4 2.5 %shard_map.52 = (bf16[160,128]{1,0:T(8,128)(2,1)S(1)}, bf16[160,128]{1,0:T(8,128)(2,1)S(1)}, bf16[160,128]{1,0:T(8,128)(2,1)S(1)}, bf16[160,128]{1,0:T(8,128)(2,1)S(1)}) custom-call(bf16[240,128]{1,0:T(8,128)(2,1)S(1)} %get-tuple-element.42.refs_0_, bf16[240,128]{1,0:T(8,128)(2,1)S(1)} %collective-permute-done.6.refs_1_, ...), custom_call_target="tpu_custom_call" | custom-call | flops 2147483648 | bytes 2097152 | tf_op jit(solution)/shard_map/pallas_call | solution.py:350
  40.9 1.6 %collective-permute-start.13 = (bf16[160,128]{1,0:T(8,128)(2,1)S(1)}, bf16[160,128]{1,0:T(8,128)(2,1)S(1)}, u32[]{:S(2)}, u32[]{:S(2)}) collective-permute-start(bf16[160,128]{1,0:T(8,128)(2,1)S(1)} %get-tuple-element.47), channel_id=1, source_target_pairs={{0,4},{4,0},{8,12},{12,8},{16,20},{20,16},{24,28},{28,24},{32,36},... | collective-permute-start | bytes 122888 | tf_op jit(solution)/shard_map/ppermute | solution.py:273
  42.5 1.6 %collective-permute-start.14 = (bf16[160,128]{1,0:T(8,128)(2,1)S(1)}, bf16[160,128]{1,0:T(8,128)(2,1)S(1)}, u32[]{:S(2)}, u32[]{:S(2)}) collective-permute-start(bf16[160,128]{1,0:T(8,128)(2,1)S(1)} %get-tuple-element.48), channel_id=1, source_target_pairs={{0,8},{4,12},{8,0},{12,4},{16,24},{20,28},{24,16},{28,20},{32,40},... | collective-permute-start | bytes 122888 | tf_op jit(solution)/shard_map/ppermute | solution.py:273
  44.1 0.4 collective-permute-start.15
  44.5 2.3 %shard_map.49.refs_3_ = f32[4,512,128]{2,1,0:T(8,128)S(1)} custom-call(s32[4,5]{1,0:T(4,128)S(1)} %bitcast.2, f32[2,2048,128]{2,1,0:T(8,128)S(1)} %get-tuple-element.31.refs_1_, f32[2,2048,128]{2,1,0:T(8,128)S(1)} %get-tuple-element.32.refs_2_, f32[2,2048,128]{2,1,0:T(8,128)S(1)} %get-tuple-element.33.refs_3_), custom_call_target="tpu_custom_call" | custom-call | flops 2147483648 | bytes 4194304 | tf_op jit(solution)/shard_map/pallas_call | solution.py:340
  46.8 2.7 %shard_map.51.refs_1_ = f32[4,2048,128]{2,1,0:T(8,128)S(1)} custom-call(s32[4,5]{1,0:T(4,128)S(1)} %bitcast.3, f32[2,2048,128]{2,1,0:T(8,128)S(1)} %shard_map.47.refs_1_, f32[2,2048,128]{2,1,0:T(8,128)S(1)} %shard_map.48.refs_2_, f32[4,512,128]{2,1,0:T(8,128)S(1)} %shard_map.49.refs_3_, bf16[512,128]{1,0:T(8,128)(2,1)S(1)} %get-tuple-element.38.refs_4_, ...), custom_call_target="tpu_custom_call" | custom-call | bytes 10485760 | tf_op jit(solution)/shard_map/pallas_call | solution.py:360
  49.6 2.7 %shard_map.53 = (f32[4,2048,128]{2,1,0:T(8,128)S(1)}, bf16[2048,256]{1,0:T(8,128)(2,1)}) custom-call(s32[4,5]{1,0:T(4,128)S(1)} %bitcast.4, f32[4,2048,128]{2,1,0:T(8,128)S(1)} %shard_map.51.refs_1_, bf16[160,128]{1,0:T(8,128)(2,1)S(1)} %get-tuple-element.46.refs_2_, ...), custom_call_target="tpu_custom_call", output_to_operand_aliasing={{0}: (1, {})} | custom-call | bytes 6291456 | tf_op jit(solution)/shard_map/pallas_call | solution.py:368
  (28 shorter events, 0.1 us)
Async XLA Ops:
  3.1 11.8 %collective-permute-start.6 = (bf16[240,128]{1,0:T(8,128)(2,1)S(1)}, bf16[240,128]{1,0:T(8,128)(2,1)S(1)}, u32[]{:S(2)}, u32[]{:S(2)}) collective-permute-start(bf16[240,128]{1,0:T(8,128)(2,1)S(1)} %get-tuple-element.43), channel_id=1, source_target_pairs={{0,4},{4,0},{8,12},{12,8},{16,20},{20,16},{24,28},{28,24},{32,36},... | collective-permute-start | bytes 184328 | tf_op jit(solution)/shard_map/ppermute | solution.py:273
  4.8 10.2 %collective-permute-start.7 = (bf16[240,128]{1,0:T(8,128)(2,1)S(1)}, bf16[240,128]{1,0:T(8,128)(2,1)S(1)}, u32[]{:S(2)}, u32[]{:S(2)}) collective-permute-start(bf16[240,128]{1,0:T(8,128)(2,1)S(1)} %get-tuple-element.44), channel_id=1, source_target_pairs={{0,8},{4,12},{8,0},{12,4},{16,24},{20,28},{24,16},{28,20},{32,40},... | collective-permute-start | bytes 184328 | tf_op jit(solution)/shard_map/ppermute | solution.py:273
  6.8 8.3 %collective-permute-start.8 = (bf16[240,128]{1,0:T(8,128)(2,1)S(1)}, bf16[240,128]{1,0:T(8,128)(2,1)S(1)}, u32[]{:S(2)}, u32[]{:S(2)}) collective-permute-start(bf16[240,128]{1,0:T(8,128)(2,1)S(1)} %get-tuple-element.45), channel_id=1, source_target_pairs={{0,12},{4,8},{8,4},{12,0},{16,28},{20,24},{24,20},{28,16},{32,44},... | collective-permute-start | bytes 184328 | tf_op jit(solution)/shard_map/ppermute | solution.py:273
  6.8 20.7 %collective-permute-start = (bf16[768,128]{1,0:T(8,128)(2,1)S(1)}, bf16[768,128]{1,0:T(8,128)(2,1)S(1)}, u32[]{:S(2)}, u32[]{:S(2)}) collective-permute-start(bf16[768,128]{1,0:T(8,128)(2,1)S(1)} %get-tuple-element.35), channel_id=1, source_target_pairs={{0,4},{4,0},{8,12},{12,8},{16,20},{20,16},{24,28},{28,24},{32,36},... | collective-permute-start | bytes 589832 | tf_op jit(solution)/shard_map/ppermute | solution.py:273
  8.3 20.0 %collective-permute-start.1 = (bf16[768,128]{1,0:T(8,128)(2,1)S(1)}, bf16[768,128]{1,0:T(8,128)(2,1)S(1)}, u32[]{:S(2)}, u32[]{:S(2)}) collective-permute-start(bf16[768,128]{1,0:T(8,128)(2,1)S(1)} %get-tuple-element.36), channel_id=1, source_target_pairs={{0,8},{4,12},{8,0},{12,4},{16,24},{20,28},{24,16},{28,20},{32,40},... | collective-permute-start | bytes 589832 | tf_op jit(solution)/shard_map/ppermute | solution.py:273
  14.9 13.4 %collective-permute-start.2 = (bf16[768,128]{1,0:T(8,128)(2,1)S(1)}, bf16[768,128]{1,0:T(8,128)(2,1)S(1)}, u32[]{:S(2)}, u32[]{:S(2)}) collective-permute-start(bf16[768,128]{1,0:T(8,128)(2,1)S(1)} %get-tuple-element.37), channel_id=1, source_target_pairs={{0,12},{4,8},{8,4},{12,0},{16,28},{20,24},{24,20},{28,16},{32,44},... | collective-permute-start | bytes 589832 | tf_op jit(solution)/shard_map/ppermute | solution.py:273
  15.2 7.8 %collective-permute-start.9 = (bf16[128,128]{1,0:T(8,128)(2,1)S(1)}, bf16[128,128]{1,0:T(8,128)(2,1)S(1)}, u32[]{:S(2)}, u32[]{:S(2)}) collective-permute-start(bf16[128,128]{1,0:T(8,128)(2,1)S(1)} %pad_maximum_fusion), channel_id=1, source_target_pairs={{0,64},{4,68},{8,72},{12,76},{16,80},{20,84},{24,88},{28,92},{32,9... | collective-permute-start | bytes 98312 | tf_op jit(solution)/shard_map/ppermute | solution.py:273
  23.0 15.1 %collective-permute-start.10 = (bf16[768,128]{1,0:T(8,128)(2,1)S(1)}, bf16[768,128]{1,0:T(8,128)(2,1)S(1)}, u32[]{:S(2)}, u32[]{:S(2)}) collective-permute-start(bf16[768,128]{1,0:T(8,128)(2,1)S(1)} %constant_dynamic-update-slice_fusion.refs_4_), channel_id=1, source_target_pairs={{0,32},{4,36},{8,40},{12,44},{16,48},{20,52},{24,56},{28,60},{32,0... | collective-permute-start | bytes 589832 | tf_op jit(solution)/shard_map/ppermute | solution.py:273
  23.6 14.8 %collective-permute-start.11 = (bf16[768,128]{1,0:T(8,128)(2,1)S(1)}, bf16[768,128]{1,0:T(8,128)(2,1)S(1)}, u32[]{:S(2)}, u32[]{:S(2)}) collective-permute-start(bf16[768,128]{1,0:T(8,128)(2,1)S(1)} %constant_dynamic-update-slice_fusion.refs_4_), channel_id=1, source_target_pairs={{0,16},{4,20},{8,24},{12,28},{16,0},{20,4},{24,8},{28,12},{32,48},... | collective-permute-start | bytes 589832 | tf_op jit(solution)/shard_map/ppermute | solution.py:273
  27.5 10.9 %collective-permute-start.12 = (bf16[768,128]{1,0:T(8,128)(2,1)S(1)}, bf16[768,128]{1,0:T(8,128)(2,1)S(1)}, u32[]{:S(2)}, u32[]{:S(2)}) collective-permute-start(bf16[768,128]{1,0:T(8,128)(2,1)S(1)} %constant_dynamic-update-slice_fusion.refs_4_), channel_id=1, source_target_pairs={{0,48},{4,52},{8,56},{12,60},{16,32},{20,36},{24,40},{28,44},{32,1... | collective-permute-start | bytes 589832 | tf_op jit(solution)/shard_map/ppermute | solution.py:273
  34.8 9.3 %collective-permute-start.3 = (bf16[512,128]{1,0:T(8,128)(2,1)S(1)}, bf16[512,128]{1,0:T(8,128)(2,1)S(1)}, u32[]{:S(2)}, u32[]{:S(2)}) collective-permute-start(bf16[512,128]{1,0:T(8,128)(2,1)S(1)} %get-tuple-element.39), channel_id=1, source_target_pairs={{0,4},{4,0},{8,12},{12,8},{16,20},{20,16},{24,28},{28,24},{32,36},... | collective-permute-start | bytes 393224 | tf_op jit(solution)/shard_map/ppermute | solution.py:273
  36.5 10.4 %collective-permute-start.4 = (bf16[512,128]{1,0:T(8,128)(2,1)S(1)}, bf16[512,128]{1,0:T(8,128)(2,1)S(1)}, u32[]{:S(2)}, u32[]{:S(2)}) collective-permute-start(bf16[512,128]{1,0:T(8,128)(2,1)S(1)} %get-tuple-element.40), channel_id=1, source_target_pairs={{0,8},{4,12},{8,0},{12,4},{16,24},{20,28},{24,16},{28,20},{32,40},... | collective-permute-start | bytes 393224 | tf_op jit(solution)/shard_map/ppermute | solution.py:273
  38.0 6.4 %copy-start = (s32[5,4]{0,1:T(4,128)S(1)}, s32[5,4]{0,1:T(4,128)}, u32[]{:S(2)}) copy-start(s32[5,4]{0,1:T(4,128)} %param.7) | copy-start | bytes 244
  38.0 8.8 %collective-permute-start.5 = (bf16[512,128]{1,0:T(8,128)(2,1)S(1)}, bf16[512,128]{1,0:T(8,128)(2,1)S(1)}, u32[]{:S(2)}, u32[]{:S(2)}) collective-permute-start(bf16[512,128]{1,0:T(8,128)(2,1)S(1)} %get-tuple-element.41), channel_id=1, source_target_pairs={{0,12},{4,8},{8,4},{12,0},{16,28},{20,24},{24,20},{28,16},{32,44},... | collective-permute-start | bytes 393224 | tf_op jit(solution)/shard_map/ppermute | solution.py:273
  40.9 8.7 %collective-permute-start.13 = (bf16[160,128]{1,0:T(8,128)(2,1)S(1)}, bf16[160,128]{1,0:T(8,128)(2,1)S(1)}, u32[]{:S(2)}, u32[]{:S(2)}) collective-permute-start(bf16[160,128]{1,0:T(8,128)(2,1)S(1)} %get-tuple-element.47), channel_id=1, source_target_pairs={{0,4},{4,0},{8,12},{12,8},{16,20},{20,16},{24,28},{28,24},{32,36},... | collective-permute-start | bytes 122888 | tf_op jit(solution)/shard_map/ppermute | solution.py:273
  42.5 7.0 %collective-permute-start.14 = (bf16[160,128]{1,0:T(8,128)(2,1)S(1)}, bf16[160,128]{1,0:T(8,128)(2,1)S(1)}, u32[]{:S(2)}, u32[]{:S(2)}) collective-permute-start(bf16[160,128]{1,0:T(8,128)(2,1)S(1)} %get-tuple-element.48), channel_id=1, source_target_pairs={{0,8},{4,12},{8,0},{12,4},{16,24},{20,28},{24,16},{28,20},{32,40},... | collective-permute-start | bytes 122888 | tf_op jit(solution)/shard_map/ppermute | solution.py:273
  44.1 5.5 %collective-permute-start.15 = (bf16[160,128]{1,0:T(8,128)(2,1)S(1)}, bf16[160,128]{1,0:T(8,128)(2,1)S(1)}, u32[]{:S(2)}, u32[]{:S(2)}) collective-permute-start(bf16[160,128]{1,0:T(8,128)(2,1)S(1)} %get-tuple-element.49), channel_id=1, source_target_pairs={{0,12},{4,8},{8,4},{12,0},{16,28},{20,24},{24,20},{28,16},{32,44},... | collective-permute-start | bytes 122888 | tf_op jit(solution)/shard_map/ppermute | solution.py:273

commit v3 on v2

--- a/solution.py
+++ b/solution.py
@@ -33,42 +33,45 @@
     return pltpu.roll(x, HALF, 1)
 
 
-def softmax_tile(q, keys, values, vl):
-    scores = [dot_nt(q, k) for k in keys]
+def softmax(scores, values):
     top = scores[0].max(axis=1, keepdims=True)
     for s in scores[1:]:
         top = jnp.maximum(top, s.max(axis=1, keepdims=True))
-    acc = None
-    for s, v in zip(scores, values):
-        part = dot_nn(jnp.exp(s - top).astype(bf16), v)
-        acc = part if acc is None else acc + part
-    return jnp.where(vl, acc / swap_halves(acc), top + jnp.log(acc))
-
-
-def merge(vl, one, lse_one, two, lse_two):
-    gap = lse_two - lse_one
-    small = jnp.exp(-jnp.abs(gap))
-    ahead = gap > 0.0
-    big_out = jnp.where(ahead, two, one)
-    small_out = jnp.where(ahead, one, two)
-    weight = 1.0 + small
-    out = (big_out + small * small_out) / weight
-    return jnp.where(vl, out, jnp.maximum(lse_one, lse_two) + jnp.log(weight))
-
-
-def spread_lse(tile, vl):
-    return jnp.where(vl, swap_halves(tile), tile)
-
-
-def encode(tile, vl):
-    lane = lax.broadcasted_iota(jnp.int32, tile.shape, 1)
+    probs = [jnp.exp(s - top).astype(bf16) for s in scores]
+    return top, jnp.concatenate(probs, axis=1), jnp.concatenate(values, axis=0)
+
+
+def attend_one(q, keys, values):
+    top, probs, wide = softmax([dot_nt(q, k) for k in keys], values)
+    acc = dot_nn(probs, wide)
+    total = acc[:, LANES:]
+    return acc[:, :LANES] / total, top + jnp.log(total)
+
+
+def attend_pair(queries, keys, values):
+    low = half_mask(queries[0].shape[0], 0)
+    tops, probs, wides = zip(
+        *[softmax([dot_nt(q, k)], [v]) for q, k, v in zip(queries, keys, values)]
+    )
+    acc = dot_nn(jnp.concatenate(probs, axis=1), jnp.concatenate(wides, axis=0))
+    total = acc[:, LANES:]
+    return acc[:, :LANES] / total, jnp.where(low, tops[0], tops[1]) + jnp.log(total)
+
+
+def with_ones(v, vl):
+    zero, one = jnp.zeros_like(v), jnp.ones_like(v)
+    return jnp.concatenate([jnp.where(vl, v, zero), jnp.where(vl, one, zero)], axis=1)
+
+
+def encode(out, lse, vl):
+    lane = lax.broadcasted_iota(jnp.int32, out.shape, 1)
     spot = lax.rem(lane, HALF)
-    first = tile.astype(bf16).astype(f32)
-    rest = tile - first
+    first = lse.astype(bf16).astype(f32)
+    rest = lse - first
     second = rest.astype(bf16).astype(f32)
     third = rest - second
     coded = jnp.where(spot == 0, first, jnp.where(spot == 1, second, third))
-    return jnp.where(vl, tile, coded).astype(bf16)
+    return jnp.where(vl, out, coded)
 
 
 def decode_lse(coded, half):
@@ -129,39 +132,47 @@
 
 
 def first_kernel(pair, q_ref, k_ref, v_ref, *rest):
-    t_ref = rest[-1]
-    zero, one = jnp.asarray(0, bf16), jnp.asarray(1, bf16)
+    out_ref, lse_ref = rest[-2:]
     scale = jnp.asarray(0.125, bf16)
     cols = slice(pair * LANES, (pair + 1) * LANES)
 
     @pl.loop(0, q_ref.shape[0] // SEG)
     def _(s):
         part = pl.ds(pl.multiple_of(s * SEG, SEG), SEG)
-        for h in range(2):
-            vl = half_mask(SEG, h)
-            q = q_ref[part, cols] * scale
-            k = jnp.where(vl, k_ref[part, cols], zero)
-            v = jnp.where(vl, v_ref[part, cols], one)
-            t_ref[h, part, :] = softmax_tile(q, [k], [v], vl)
-
-
-def second_kernel(rate, offs_any, qs, ks, vs, found_ref, offs, sem):
-    copy = fetch(offs_any, offs, sem)
-    count = found_ref.shape[1]
-    copy.wait()
-    for h in range(4):
-        vl = half_mask(count, h % 2)
-        picked = pl.ds(offs[h, 1], count, rate)
-        q = (qs[h // 2, picked, :] * 0.125).astype(bf16)
-        k = jnp.where(vl, ks[h // 2, picked, :], 0.0).astype(bf16)
-        v = jnp.where(vl, vs[h // 2, picked, :], 1.0).astype(bf16)
-        found_ref[h, :, :] = softmax_tile(q, [k], [v], vl)
+        q, k, v = q_ref[part, cols] * scale, k_ref[part, cols], v_ref[part, cols]
+        halves = [half_mask(SEG, h) for h in range(2)]
+        out, lse = attend_pair(
+            [q, q],
+            [jnp.where(vl, k, jnp.zeros_like(k)) for vl in halves],
+            [with_ones(v, vl) for vl in halves],
+        )
+        out_ref[pair, part, :] = out
+        lse_ref[pair, part, :] = lse
+
+
+def absorb(outs, lses, head, off, rate, new, lse_new):
+    pair, half = lax.div(head, 2), lax.rem(head, 2)
+    count = new.shape[0]
+    vl = half_mask(count, half)
+    picked = pl.ds(off, count, rate)
+    old, lse_old = outs[pair, picked, :], lses[pair, picked, :]
+    gap = lse_new - lse_old
+    small = jnp.exp(-jnp.abs(gap))
+    share = jnp.where(gap > 0.0, 1.0, small) / (1.0 + small)
+    outs[pair, picked, :] = jnp.where(vl, old + share * (new - old), old)
+    lse = jnp.maximum(lse_old, lse_new) + jnp.log(1.0 + small)
+    lses[pair, picked, :] = jnp.where(vl, lse, lse_old)
+
+
+def absorb_coded(outs, lses, head, off, rate, coded):
+    lse = decode_lse(coded, lax.rem(head, 2))
+    absorb(outs, lses, head, off, rate, coded.astype(f32), lse)
 
 
 def keys_values(tile, half):
     vl = half_mask(tile.shape[0], half)
-    zero, one = jnp.asarray(0, bf16), jnp.asarray(1, bf16)
-    return jnp.where(vl, zero, tile), jnp.where(vl, tile, one)
+    zero, one = jnp.zeros_like(tile), jnp.ones_like(tile)
+    return jnp.where(vl, zero, tile), jnp.concatenate([jnp.where(vl, tile, zero), one], axis=1)
 
 
 def near_kernel(count, *refs):
@@ -169,13 +180,12 @@
     half = lax.rem(lax.axis_index("seq"), 2)
     keys, values = zip(*[keys_values(r[:count, :], half) for r in ins])
     few = count // 2
-    vl = half_mask(few, half)
+    vl = half_mask(count, half)
     for d in range(4):
         tile = ins[d][count : count + few, :]
-        for part in range(2):
-            q = tile if part == 0 else swap_halves(tile.astype(f32)).astype(bf16)
-            found = softmax_tile(q, keys, values, vl)
-            outs[d][part * few : (part + 1) * few, :] = encode(found, vl)
+        other = swap_halves(tile.astype(f32)).astype(bf16)
+        out, lse = attend_one(jnp.concatenate([tile, other], axis=0), keys, values)
+        outs[d][...] = encode(out, lse, vl).astype(bf16)
 
 
 def far_kernel(mid, top, *refs):
@@ -190,43 +200,41 @@
         keys, values = zip(*[keys_values(t, half) for t in tiles])
         tile = jnp.concatenate([r[q_at : q_at + few, :].astype(f32) for r in far], axis=0)
         q = jnp.concatenate([tile, swap_halves(tile)], axis=0).astype(bf16)
-        vl = half_mask(8 * few, half)
-        found = encode(softmax_tile(q, keys, values, vl), vl).astype(f32)
+        out, lse = attend_one(q, keys, values)
+        found = encode(out, lse, half_mask(8 * few, half))
         for part in range(2):
             for d in range(4):
                 at, start = out_at + part * few, (part * 4 + d) * few
                 outs[d][at : at + few, :] = found[start : start + few, :].astype(bf16)
 
 
-def absorb(state, head, off, rate, new, lse_new):
-    count = new.shape[0]
-    vl = half_mask(count, lax.rem(head, 2))
-    picked = pl.ds(off, count, rate)
-    old = state[head, picked, :]
-    state[head, picked, :] = merge(vl, old, spread_lse(old, vl), new, lse_new)
-
-
-def absorb_coded(state, head, off, rate, coded):
-    absorb(state, head, off, rate, coded.astype(f32), decode_lse(coded, lax.rem(head, 2)))
-
-
-def blend_kernel(rate, offs_any, low, high, found_ref, *refs):
-    near, state, offs, sem = refs[:4], refs[4], refs[5], refs[6]
+def second_kernel(rate, offs_any, qs, ks, vs, outs_in, lses_in, *refs):
+    near, outs, lses, offs, sem = refs[:4], refs[4], refs[5], refs[6], refs[7]
     copy = fetch(offs_any, offs, sem)
     mine = lax.rem(lax.axis_index("seq"), 4)
-    for h in range(4):
-        state[h, :, :] = (low, high)[h // 2][h % 2, :, :]
+    count = near[0].shape[0]
     copy.wait()
-    for h in range(4):
-        new = found_ref[h, :, :]
-        absorb(state, h, offs[h, 1], rate, new, spread_lse(new, half_mask(new.shape[0], h % 2)))
+    for p in range(2):
+        queries, keys, values = [], [], []
+        for h in range(2):
+            vl = half_mask(count, h)
+            picked = pl.ds(offs[2 * p + h, 1], count, rate)
+            queries.append((qs[p, picked, :] * 0.125).astype(bf16))
+            k = ks[p, picked, :]
+            keys.append(jnp.where(vl, k, jnp.zeros_like(k)).astype(bf16))
+            values.append(with_ones(vs[p, picked, :], vl).astype(bf16))
+        out, lse = attend_pair(queries, keys, values)
+        for h in range(2):
+            head = 2 * p + h
+            absorb(outs, lses, head, offs[head, 1], rate, out, lse)
     for d in range(4):
         head = mine ^ d
-        absorb_coded(state, head, offs[head, 2], rate, near[d][...])
-
-
-def final_kernel(levels, offs_any, state_in, *refs):
-    far, state, out_any, offs, out, sem, sems = refs[:4], refs[4], refs[5], refs[6], refs[7], refs[8], refs[9]
+        absorb_coded(outs, lses, head, offs[head, 2], rate, near[d][...])
+
+
+def final_kernel(levels, offs_any, outs_in, lses_in, *refs):
+    far, outs, lses, out_any = refs[:4], refs[4], refs[5], refs[6]
+    offs, out, sem, sems = refs[7:]
     copy = fetch(offs_any, offs, sem)
     mine = lax.rem(lax.axis_index("seq"), 4)
     copy.wait()
@@ -235,17 +243,13 @@
         at = 0
         for level, count, rate, near in levels:
             if not near:
-                absorb_coded(state, head, offs[head, level], rate, far[d][at : at + count, :])
+                absorb_coded(outs, lses, head, offs[head, level], rate, far[d][at : at + count, :])
                 at += count
-    step = SEG
-    vl = half_mask(step, 0)
     copies = []
-    for i in range(out.shape[0] // step):
-        part = slice(i * step, (i + 1) * step)
+    for i in range(out.shape[0] // SEG):
+        part = slice(i * SEG, (i + 1) * SEG)
         for p in range(2):
-            out[part, p * LANES : (p + 1) * LANES] = jnp.where(
-                vl, state[2 * p, part, :], state[2 * p + 1, part, :]
-            ).astype(bf16)
+            out[part, p * LANES : (p + 1) * LANES] = outs[p, part, :].astype(bf16)
         copies.append(pltpu.make_async_copy(out.at[part, :], out_any.at[part, :], sems.at[i]))
         copies[-1].start()
     for copy in copies:
@@ -294,7 +298,6 @@
         return jax.ShapeDtypeStruct((n, LANES), kind)
 
     wide = jax.ShapeDtypeStruct((2, rows, LANES), f32)
-    state_shape = jax.ShapeDtypeStruct((4, rows, LANES), f32)
     parts = call(
         lambda *refs: pack_kernel(levels, *refs),
         [tile(near_count * 3 // 2)] * 4
@@ -310,17 +313,17 @@
     far_held = [far_sent[0]] + [swapped(far_sent[d], d) for d in (1, 2, 3)]
     near_held = [near_sent[0]] + [swapped(near_sent[d], d) for d in (1, 2, 3)]
 
-    states = [
-        call(
+    state = ()
+    for pair in range(2):
+        state = call(
             lambda *refs, pair=pair: first_kernel(pair, *refs),
-            wide,
-            "vvv",
+            [wide, wide],
+            "vvv" + "v" * len(state),
             flops=2 << 30,
             bytes_moved=4 << 20,
             exps=2 << 20,
-        )(*narrow)
-        for pair in range(2)
-    ]
+            aliases={3: 0, 4: 1} if state else None,
+        )(*narrow, *state)
 
     own_top = jnp.concatenate([r[mid : mid + top] for r in far_held], axis=0)
     other_top = swapped(own_top, 16)
@@ -337,16 +340,6 @@
     )(*near_held)
     near_back = [near_found[0]] + [swapped(near_found[d], d) for d in (1, 2, 3)]
 
-    found = call(
-        lambda *refs: second_kernel(RATE1, *refs),
-        jax.ShapeDtypeStruct((4, near_count, LANES), f32),
-        "avvv",
-        (table, one_sem),
-        flops=2 << 30,
-        bytes_moved=4 << 20,
-        exps=1 << 20,
-    )(offsets, *wides)
-
     far_found = call(
         lambda *refs: far_kernel(mid, top, *refs),
         [tile(mid + top)] * 4,
@@ -358,22 +351,25 @@
     far_back = [far_found[0]] + [swapped(far_found[d], d) for d in (1, 2, 3)]
 
     state = call(
-        lambda *refs: blend_kernel(RATE1, *refs),
-        state_shape,
-        "avvvvvvv",
+        lambda *refs: second_kernel(RATE1, *refs),
+        [wide, wide],
+        "avvvvvvvvv",
         (table, one_sem),
-        bytes_moved=10 << 20,
-    )(offsets, *states, found, *near_back)
+        flops=2 << 30,
+        bytes_moved=4 << 20,
+        exps=1 << 20,
+        aliases={4: 0, 5: 1},
+    )(offsets, *wides, *state, *near_back)
 
     return call(
         lambda *refs: final_kernel(levels, *refs),
-        [state_shape, jax.ShapeDtypeStruct((rows, width), bf16)],
-        "avvvvv",
+        [wide, wide, jax.ShapeDtypeStruct((rows, width), bf16)],
+        "avvvvvv",
         (table, VMEM((rows, width), bf16), one_sem, pltpu.SemaphoreType.DMA((rows // SEG,))),
         bytes_moved=6 << 20,
-        aliases={1: 0},
-        out_spaces="va",
-    )(offsets, state, *far_back)[1]
+        aliases={1: 0, 2: 1},
+        out_spaces="vva",
+    )(offsets, *state, *far_back)[2]
 
 
 def solution(mesh):

time: 52.6 us -> 50.7 us (0.964)
  Pallas kernels: 29.1 us -> 26.9 us
    pallas_call x5 -> x4, Pallas kernels: 17.1 us -> 15.2 us  [the longest x2 8.52 us: per_device(): call(lambda *refs, pair=pair: first_kernel(pair, *refs), [wide, wide], 'v...]
  transfers between devices with their start and end apart: 16 -> 16, of which waited for: 0 -> 1; matrix products, arithmetic and copies ran while one was open for 0% -> 0% of each run, Pallas kernels for 44% -> 42%
where the time goes in v3:
time: 50.7 us; the launch traced here: 50.6 us
  Pallas kernels  26.9 us (53%)
  starting transfers between devices  22.9 us (45%)
    ppermute x16, starting transfers between devices, swapped(): lax.ppermute(shard, 'seq', [(i, i ^ bits) for i in range(lax.axis_size('s...  22.9 us
    pallas_call x2, Pallas kernels, per_device(): call(lambda *refs, pair=pair: first_kernel(pair, *refs), [wide, wide], 'v...  8.52 us
    pallas_call x1, Pallas kernels, per_device(): call(lambda *refs: near_kernel(near_count, *refs), [tile(near_count)] * 4...  6.24 us
    pallas_call x1, Pallas kernels, per_device(): call(lambda *refs: second_kernel(RATE1, *refs), [wide, wide], 'avvvvvvvvv...  4.2 us
    pallas_call x1, Pallas kernels, per_device(): call(lambda *refs: pack_kernel(levels, *refs), [tile(near_count * 3 // 2)...  3.06 us
    pallas_call x1, Pallas kernels, per_device(): call(lambda *refs: final_kernel(levels, *refs), [wide, wide, jax.ShapeDty...  2.5 us
    pallas_call x1, Pallas kernels, per_device(): call(lambda *refs: far_kernel(mid, top, *refs), [tile(mid + top)] * 4, 'v...  2.36 us
  transfers between devices with their start and end apart: 16, of which 1 were waited for; matrix products, arithmetic and copies ran while one was open for 0% of the time, Pallas kernels for 42%

profile of v3, /device:TPU:0, one launch (start us, length us, event | category | flops | bytes accessed | tf_op | source)
XLA Modules:
  0.0 50.6 jit_solution(15535258270251671700)
XLA Ops:
  0.0 3.1 %shard_map.46 = (bf16[768,128]{1,0:T(8,128)(2,1)S(1)}, bf16[768,128]{1,0:T(8,128)(2,1)S(1)}, bf16[768,128]{1,0:T(8,128)(2,1)S(1)}, bf16[768,128]{1,0:T(8,128)(2,...) custom-call(s32[4,5]{1,0:T(4,128)} %bitcast.1, ...), custom_call_target="tpu_custom_call" | custom-call | bytes 5242880 | tf_op jit(solution)/shard_map/pallas_call | solution.py:301
  3.1 1.8 %collective-permute-start.6 = (bf16[240,128]{1,0:T(8,128)(2,1)S(1)}, bf16[240,128]{1,0:T(8,128)(2,1)S(1)}, u32[]{:S(2)}, u32[]{:S(2)}) collective-permute-start(bf16[240,128]{1,0:T(8,128)(2,1)S(1)} %get-tuple-element.55), channel_id=1, source_target_pairs={{0,4},{4,0},{8,12},{12,8},{16,20},{20,16},{24,28},{28,24},{32,36},... | collective-permute-start | bytes 184328 | tf_op jit(solution)/shard_map/ppermute | solution.py:277
  4.8 1.9 %collective-permute-start.7 = (bf16[240,128]{1,0:T(8,128)(2,1)S(1)}, bf16[240,128]{1,0:T(8,128)(2,1)S(1)}, u32[]{:S(2)}, u32[]{:S(2)}) collective-permute-start(bf16[240,128]{1,0:T(8,128)(2,1)S(1)} %get-tuple-element.56), channel_id=1, source_target_pairs={{0,8},{4,12},{8,0},{12,4},{16,24},{20,28},{24,16},{28,20},{32,40},... | collective-permute-start | bytes 184328 | tf_op jit(solution)/shard_map/ppermute | solution.py:277
  6.8 1.6 %collective-permute-start = (bf16[768,128]{1,0:T(8,128)(2,1)S(1)}, bf16[768,128]{1,0:T(8,128)(2,1)S(1)}, u32[]{:S(2)}, u32[]{:S(2)}) collective-permute-start(bf16[768,128]{1,0:T(8,128)(2,1)S(1)} %get-tuple-element.45), channel_id=1, source_target_pairs={{0,4},{4,0},{8,12},{12,8},{16,20},{20,16},{24,28},{28,24},{32,36},... | collective-permute-start | bytes 589832 | tf_op jit(solution)/shard_map/ppermute | solution.py:277
  8.3 1.9 %collective-permute-start.1 = (bf16[768,128]{1,0:T(8,128)(2,1)S(1)}, bf16[768,128]{1,0:T(8,128)(2,1)S(1)}, u32[]{:S(2)}, u32[]{:S(2)}) collective-permute-start(bf16[768,128]{1,0:T(8,128)(2,1)S(1)} %get-tuple-element.46), channel_id=1, source_target_pairs={{0,8},{4,12},{8,0},{12,4},{16,24},{20,28},{24,16},{28,20},{32,40},... | collective-permute-start | bytes 589832 | tf_op jit(solution)/shard_map/ppermute | solution.py:277
  10.3 4.3 %shard_map.47 = (f32[2,2048,128]{2,1,0:T(8,128)S(1)}, f32[2,2048,128]{2,1,0:T(8,128)S(1)}) custom-call(bf16[2048,256]{1,0:T(8,128)(2,1)S(1)} %get-tuple-element.37.refs_0_, bf16[2048,256]{1,0:T(8,128)(2,1)S(1)} %get-tuple-element.38.refs_1_, bf16[2048,256]{1,0:T(8,128)(2,1)S(1)} %get-tuple-element.39.refs_2_), custom_call_target="tpu_custom_call" | custom-call | flops 2147483648 | bytes 4194304 | tf_op jit(solution)/shard_map/pallas_call | solution.py:318
  14.5 0.1 collective-permute-start.2
  14.8 3.1 %collective-permute-start.9 = (bf16[128,128]{1,0:T(8,128)(2,1)S(1)}, bf16[128,128]{1,0:T(8,128)(2,1)S(1)}, u32[]{:S(2)}, u32[]{:S(2)}) collective-permute-start(bf16[128,128]{1,0:T(8,128)(2,1)S(1)} %pad_maximum_fusion), channel_id=1, source_target_pairs={{0,64},{4,68},{8,72},{12,76},{16,80},{20,84},{24,88},{28,92},{32,9... | collective-permute-start | bytes 98312 | tf_op jit(solution)/shard_map/ppermute | solution.py:277
  17.9 4.3 %shard_map.48 = (f32[2,2048,128]{2,1,0:T(8,128)S(1)}, f32[2,2048,128]{2,1,0:T(8,128)S(1)}) custom-call(bf16[2048,256]{1,0:T(8,128)(2,1)S(1)} %get-tuple-element.37.refs_0_, bf16[2048,256]{1,0:T(8,128)(2,1)S(1)} %get-tuple-element.38.refs_1_, bf16[2048,256]{1,0:T(8,128)(2,1)S(1)} %get-tuple-element.39.refs_2_, ...), custom_call_target="tpu_custom_call", output_to_operand_aliasing={{0}: (3, {}), {1}: (4, {})} | custom-call | flops 2147483648 | bytes 4194304 | tf_op jit(solution)/shard_map/pallas_call | solution.py:318
  22.1 3.9 %collective-permute-start.12 = (bf16[768,128]{1,0:T(8,128)(2,1)S(1)}, bf16[768,128]{1,0:T(8,128)(2,1)S(1)}, u32[]{:S(2)}, u32[]{:S(2)}) collective-permute-start(bf16[768,128]{1,0:T(8,128)(2,1)S(1)} %constant_dynamic-update-slice_fusion.refs_4_), channel_id=1, source_target_pairs={{0,48},{4,52},{8,56},{12,60},{16,32},{20,36},{24,40},{28,44},{32,1... | collective-permute-start | bytes 589832 | tf_op jit(solution)/shard_map/ppermute | solution.py:277
  26.1 0.1 collective-permute-start.11
  26.2 1.4 %collective-permute-start.10 = (bf16[768,128]{1,0:T(8,128)(2,1)S(1)}, bf16[768,128]{1,0:T(8,128)(2,1)S(1)}, u32[]{:S(2)}, u32[]{:S(2)}) collective-permute-start(bf16[768,128]{1,0:T(8,128)(2,1)S(1)} %constant_dynamic-update-slice_fusion.refs_4_), channel_id=1, source_target_pairs={{0,32},{4,36},{8,40},{12,44},{16,48},{20,52},{24,56},{28,60},{32,0... | collective-permute-start | bytes 589832 | tf_op jit(solution)/shard_map/ppermute | solution.py:277
  27.6 6.2 %shard_map.49 = (bf16[512,128]{1,0:T(8,128)(2,1)S(1)}, bf16[512,128]{1,0:T(8,128)(2,1)S(1)}, bf16[512,128]{1,0:T(8,128)(2,1)S(1)}, bf16[512,128]{1,0:T(8,128)(2,1)S(1)}) custom-call(bf16[768,128]{1,0:T(8,128)(2,1)S(1)} %get-tuple-element.44.refs_0_, bf16[768,128]{1,0:T(8,128)(2,1)S(1)} %collective-permute-done.refs_1_, ...), custom_call_target="tpu_custom_call" | custom-call | flops 6442450944 | bytes 2097152 | tf_op jit(solution)/shard_map/pallas_call | solution.py:333
  33.8 1.7 %collective-permute-start.3 = (bf16[512,128]{1,0:T(8,128)(2,1)S(1)}, bf16[512,128]{1,0:T(8,128)(2,1)S(1)}, u32[]{:S(2)}, u32[]{:S(2)}) collective-permute-start(bf16[512,128]{1,0:T(8,128)(2,1)S(1)} %get-tuple-element.49), channel_id=1, source_target_pairs={{0,4},{4,0},{8,12},{12,8},{16,20},{20,16},{24,28},{28,24},{32,36},... | collective-permute-start | bytes 393224 | tf_op jit(solution)/shard_map/ppermute | solution.py:277
  35.5 1.6 %collective-permute-start.4 = (bf16[512,128]{1,0:T(8,128)(2,1)S(1)}, bf16[512,128]{1,0:T(8,128)(2,1)S(1)}, u32[]{:S(2)}, u32[]{:S(2)}) collective-permute-start(bf16[512,128]{1,0:T(8,128)(2,1)S(1)} %get-tuple-element.50), channel_id=1, source_target_pairs={{0,8},{4,12},{8,0},{12,4},{16,24},{20,28},{24,16},{28,20},{32,40},... | collective-permute-start | bytes 393224 | tf_op jit(solution)/shard_map/ppermute | solution.py:277
  37.0 0.3 collective-permute-start.5
  37.4 2.4 %shard_map.51 = (bf16[160,128]{1,0:T(8,128)(2,1)S(1)}, bf16[160,128]{1,0:T(8,128)(2,1)S(1)}, bf16[160,128]{1,0:T(8,128)(2,1)S(1)}, bf16[160,128]{1,0:T(8,128)(2,1)S(1)}) custom-call(bf16[240,128]{1,0:T(8,128)(2,1)S(1)} %get-tuple-element.54.refs_0_, bf16[240,128]{1,0:T(8,128)(2,1)S(1)} %collective-permute-done.6.refs_1_, ...), custom_call_target="tpu_custom_call" | custom-call | flops 2147483648 | bytes 2097152 | tf_op jit(solution)/shard_map/pallas_call | solution.py:343
  39.7 1.7 %collective-permute-start.13 = (bf16[160,128]{1,0:T(8,128)(2,1)S(1)}, bf16[160,128]{1,0:T(8,128)(2,1)S(1)}, u32[]{:S(2)}, u32[]{:S(2)}) collective-permute-start(bf16[160,128]{1,0:T(8,128)(2,1)S(1)} %get-tuple-element.59), channel_id=1, source_target_pairs={{0,4},{4,0},{8,12},{12,8},{16,20},{20,16},{24,28},{28,24},{32,36},... | collective-permute-start | bytes 122888 | tf_op jit(solution)/shard_map/ppermute | solution.py:277
  41.4 1.6 %collective-permute-start.14 = (bf16[160,128]{1,0:T(8,128)(2,1)S(1)}, bf16[160,128]{1,0:T(8,128)(2,1)S(1)}, u32[]{:S(2)}, u32[]{:S(2)}) collective-permute-start(bf16[160,128]{1,0:T(8,128)(2,1)S(1)} %get-tuple-element.60), channel_id=1, source_target_pairs={{0,8},{4,12},{8,0},{12,4},{16,24},{20,28},{24,16},{28,20},{32,40},... | collective-permute-start | bytes 122888 | tf_op jit(solution)/shard_map/ppermute | solution.py:277
  43.0 0.4 collective-permute-start.15
  43.3 0.0 collective-permute-done.5.refs_9_
  43.3 4.2 %shard_map.50 = (f32[2,2048,128]{2,1,0:T(8,128)S(1)}, f32[2,2048,128]{2,1,0:T(8,128)S(1)}) custom-call(s32[4,5]{1,0:T(4,128)S(1)} %bitcast.2, f32[2,2048,128]{2,1,0:T(8,128)S(1)} %get-tuple-element.34.refs_1_, f32[2,2048,128]{2,1,0:T(8,128)S(1)} %get-tuple-element.35.refs_2_, ...), custom_call_target="tpu_custom_call", output_to_operand_aliasing={{0}: (4, {}), {1}: (5, {})} | custom-call | flops 2147483648 | bytes 4194304 | tf_op jit(solution)/shard_map/pallas_call | solution.py:353
  47.6 0.3 collective-permute-done.15.refs_6_
  47.9 2.5 %shard_map.52 = (f32[2,2048,128]{2,1,0:T(8,128)S(1)}, f32[2,2048,128]{2,1,0:T(8,128)S(1)}, bf16[2048,256]{1,0:T(8,128)(2,1)}) custom-call(s32[4,5]{1,0:T(4,128)S(1)} %bitcast.3, f32[2,2048,128]{2,1,0:T(8,128)S(1)} %get-tuple-element.52.refs_1_, f32[2,2048,128]{2,1,0:T(8,128)S(1)} %get-tuple-element.53.refs_2_, ...), custom_call_target="tpu_custom_call", output_to_operand_aliasing={{0}: (1, {}), {1}: (2, {})} | custom-call | bytes 6291456 | tf_op jit(solution)/shard_map/pallas_call | solution.py:364
  (27 shorter events, 0.1 us)
Async XLA Ops:
  3.1 11.4 %collective-permute-start.6 = (bf16[240,128]{1,0:T(8,128)(2,1)S(1)}, bf16[240,128]{1,0:T(8,128)(2,1)S(1)}, u32[]{:S(2)}, u32[]{:S(2)}) collective-permute-start(bf16[240,128]{1,0:T(8,128)(2,1)S(1)} %get-tuple-element.55), channel_id=1, source_target_pairs={{0,4},{4,0},{8,12},{12,8},{16,20},{20,16},{24,28},{28,24},{32,36},... | collective-permute-start | bytes 184328 | tf_op jit(solution)/shard_map/ppermute | solution.py:277
  4.8 9.8 %collective-permute-start.7 = (bf16[240,128]{1,0:T(8,128)(2,1)S(1)}, bf16[240,128]{1,0:T(8,128)(2,1)S(1)}, u32[]{:S(2)}, u32[]{:S(2)}) collective-permute-start(bf16[240,128]{1,0:T(8,128)(2,1)S(1)} %get-tuple-element.56), channel_id=1, source_target_pairs={{0,8},{4,12},{8,0},{12,4},{16,24},{20,28},{24,16},{28,20},{32,40},... | collective-permute-start | bytes 184328 | tf_op jit(solution)/shard_map/ppermute | solution.py:277
  6.8 7.9 %collective-permute-start.8 = (bf16[240,128]{1,0:T(8,128)(2,1)S(1)}, bf16[240,128]{1,0:T(8,128)(2,1)S(1)}, u32[]{:S(2)}, u32[]{:S(2)}) collective-permute-start(bf16[240,128]{1,0:T(8,128)(2,1)S(1)} %get-tuple-element.57), channel_id=1, source_target_pairs={{0,12},{4,8},{8,4},{12,0},{16,28},{20,24},{24,20},{28,16},{32,44},... | collective-permute-start | bytes 184328 | tf_op jit(solution)/shard_map/ppermute | solution.py:277
  6.8 19.4 %collective-permute-start = (bf16[768,128]{1,0:T(8,128)(2,1)S(1)}, bf16[768,128]{1,0:T(8,128)(2,1)S(1)}, u32[]{:S(2)}, u32[]{:S(2)}) collective-permute-start(bf16[768,128]{1,0:T(8,128)(2,1)S(1)} %get-tuple-element.45), channel_id=1, source_target_pairs={{0,4},{4,0},{8,12},{12,8},{16,20},{20,16},{24,28},{28,24},{32,36},... | collective-permute-start | bytes 589832 | tf_op jit(solution)/shard_map/ppermute | solution.py:277
  8.3 19.2 %collective-permute-start.1 = (bf16[768,128]{1,0:T(8,128)(2,1)S(1)}, bf16[768,128]{1,0:T(8,128)(2,1)S(1)}, u32[]{:S(2)}, u32[]{:S(2)}) collective-permute-start(bf16[768,128]{1,0:T(8,128)(2,1)S(1)} %get-tuple-element.46), channel_id=1, source_target_pairs={{0,8},{4,12},{8,0},{12,4},{16,24},{20,28},{24,16},{28,20},{32,40},... | collective-permute-start | bytes 589832 | tf_op jit(solution)/shard_map/ppermute | solution.py:277
  14.5 13.0 %collective-permute-start.2 = (bf16[768,128]{1,0:T(8,128)(2,1)S(1)}, bf16[768,128]{1,0:T(8,128)(2,1)S(1)}, u32[]{:S(2)}, u32[]{:S(2)}) collective-permute-start(bf16[768,128]{1,0:T(8,128)(2,1)S(1)} %get-tuple-element.47), channel_id=1, source_target_pairs={{0,12},{4,8},{8,4},{12,0},{16,28},{20,24},{24,20},{28,16},{32,44},... | collective-permute-start | bytes 589832 | tf_op jit(solution)/shard_map/ppermute | solution.py:277
  14.8 7.4 %collective-permute-start.9 = (bf16[128,128]{1,0:T(8,128)(2,1)S(1)}, bf16[128,128]{1,0:T(8,128)(2,1)S(1)}, u32[]{:S(2)}, u32[]{:S(2)}) collective-permute-start(bf16[128,128]{1,0:T(8,128)(2,1)S(1)} %pad_maximum_fusion), channel_id=1, source_target_pairs={{0,64},{4,68},{8,72},{12,76},{16,80},{20,84},{24,88},{28,92},{32,9... | collective-permute-start | bytes 98312 | tf_op jit(solution)/shard_map/ppermute | solution.py:277
  22.1 14.9 %collective-permute-start.12 = (bf16[768,128]{1,0:T(8,128)(2,1)S(1)}, bf16[768,128]{1,0:T(8,128)(2,1)S(1)}, u32[]{:S(2)}, u32[]{:S(2)}) collective-permute-start(bf16[768,128]{1,0:T(8,128)(2,1)S(1)} %constant_dynamic-update-slice_fusion.refs_4_), channel_id=1, source_target_pairs={{0,48},{4,52},{8,56},{12,60},{16,32},{20,36},{24,40},{28,44},{32,1... | collective-permute-start | bytes 589832 | tf_op jit(solution)/shard_map/ppermute | solution.py:277
  26.1 11.3 %collective-permute-start.11 = (bf16[768,128]{1,0:T(8,128)(2,1)S(1)}, bf16[768,128]{1,0:T(8,128)(2,1)S(1)}, u32[]{:S(2)}, u32[]{:S(2)}) collective-permute-start(bf16[768,128]{1,0:T(8,128)(2,1)S(1)} %constant_dynamic-update-slice_fusion.refs_4_), channel_id=1, source_target_pairs={{0,16},{4,20},{8,24},{12,28},{16,0},{20,4},{24,8},{28,12},{32,48},... | collective-permute-start | bytes 589832 | tf_op jit(solution)/shard_map/ppermute | solution.py:277
  26.2 11.2 %collective-permute-start.10 = (bf16[768,128]{1,0:T(8,128)(2,1)S(1)}, bf16[768,128]{1,0:T(8,128)(2,1)S(1)}, u32[]{:S(2)}, u32[]{:S(2)}) collective-permute-start(bf16[768,128]{1,0:T(8,128)(2,1)S(1)} %constant_dynamic-update-slice_fusion.refs_4_), channel_id=1, source_target_pairs={{0,32},{4,36},{8,40},{12,44},{16,48},{20,52},{24,56},{28,60},{32,0... | collective-permute-start | bytes 589832 | tf_op jit(solution)/shard_map/ppermute | solution.py:277
  33.8 9.2 %collective-permute-start.3 = (bf16[512,128]{1,0:T(8,128)(2,1)S(1)}, bf16[512,128]{1,0:T(8,128)(2,1)S(1)}, u32[]{:S(2)}, u32[]{:S(2)}) collective-permute-start(bf16[512,128]{1,0:T(8,128)(2,1)S(1)} %get-tuple-element.49), channel_id=1, source_target_pairs={{0,4},{4,0},{8,12},{12,8},{16,20},{20,16},{24,28},{28,24},{32,36},... | collective-permute-start | bytes 393224 | tf_op jit(solution)/shard_map/ppermute | solution.py:277
  35.5 7.9 %collective-permute-start.4 = (bf16[512,128]{1,0:T(8,128)(2,1)S(1)}, bf16[512,128]{1,0:T(8,128)(2,1)S(1)}, u32[]{:S(2)}, u32[]{:S(2)}) collective-permute-start(bf16[512,128]{1,0:T(8,128)(2,1)S(1)} %get-tuple-element.50), channel_id=1, source_target_pairs={{0,8},{4,12},{8,0},{12,4},{16,24},{20,28},{24,16},{28,20},{32,40},... | collective-permute-start | bytes 393224 | tf_op jit(solution)/shard_map/ppermute | solution.py:277
  37.0 6.3 %copy-start = (s32[5,4]{0,1:T(4,128)S(1)}, s32[5,4]{0,1:T(4,128)}, u32[]{:S(2)}) copy-start(s32[5,4]{0,1:T(4,128)} %param.7) | copy-start | bytes 244
  37.0 6.3 %collective-permute-start.5 = (bf16[512,128]{1,0:T(8,128)(2,1)S(1)}, bf16[512,128]{1,0:T(8,128)(2,1)S(1)}, u32[]{:S(2)}, u32[]{:S(2)}) collective-permute-start(bf16[512,128]{1,0:T(8,128)(2,1)S(1)} %get-tuple-element.51), channel_id=1, source_target_pairs={{0,12},{4,8},{8,4},{12,0},{16,28},{20,24},{24,20},{28,16},{32,44},... | collective-permute-start | bytes 393224 | tf_op jit(solution)/shard_map/ppermute | solution.py:277
  39.7 7.8 %collective-permute-start.13 = (bf16[160,128]{1,0:T(8,128)(2,1)S(1)}, bf16[160,128]{1,0:T(8,128)(2,1)S(1)}, u32[]{:S(2)}, u32[]{:S(2)}) collective-permute-start(bf16[160,128]{1,0:T(8,128)(2,1)S(1)} %get-tuple-element.59), channel_id=1, source_target_pairs={{0,4},{4,0},{8,12},{12,8},{16,20},{20,16},{24,28},{28,24},{32,36},... | collective-permute-start | bytes 122888 | tf_op jit(solution)/shard_map/ppermute | solution.py:277
  41.4 6.1 %collective-permute-start.14 = (bf16[160,128]{1,0:T(8,128)(2,1)S(1)}, bf16[160,128]{1,0:T(8,128)(2,1)S(1)}, u32[]{:S(2)}, u32[]{:S(2)}) collective-permute-start(bf16[160,128]{1,0:T(8,128)(2,1)S(1)} %get-tuple-element.60), channel_id=1, source_target_pairs={{0,8},{4,12},{8,0},{12,4},{16,24},{20,28},{24,16},{28,20},{32,40},... | collective-permute-start | bytes 122888 | tf_op jit(solution)/shard_map/ppermute | solution.py:277
  43.0 4.9 %collective-permute-start.15 = (bf16[160,128]{1,0:T(8,128)(2,1)S(1)}, bf16[160,128]{1,0:T(8,128)(2,1)S(1)}, u32[]{:S(2)}, u32[]{:S(2)}) collective-permute-start(bf16[160,128]{1,0:T(8,128)(2,1)S(1)} %get-tuple-element.61), channel_id=1, source_target_pairs={{0,12},{4,8},{8,4},{12,0},{16,28},{20,24},{24,20},{28,16},{32,44},... | collective-permute-start | bytes 122888 | tf_op jit(solution)/shard_map/ppermute | solution.py:277

commit v4 on v3

--- a/solution.py
+++ b/solution.py
@@ -74,10 +74,51 @@
     return jnp.where(vl, out, coded)
 
 
-def decode_lse(coded, half):
+def decode_pair(one, two, odd):
+    even = jnp.where(odd == 1, two, one)
+    other = jnp.where(odd == 1, one, two)
+    low = half_mask(one.shape[0], 0)
     row = lax.broadcasted_iota(jnp.int32, (LANES, LANES), 0)
-    pick = jnp.logical_and(lax.div(row, HALF) != half, lax.rem(row, HALF) < 3)
-    return dot_nn(coded, jnp.where(pick, 1.0, 0.0).astype(bf16))
+    column = lax.broadcasted_iota(jnp.int32, (LANES, LANES), 1)
+    pick = jnp.logical_and(
+        lax.div(row, HALF) != lax.div(column, HALF), lax.rem(row, HALF) < 3
+    )
+    lse = dot_nn(jnp.where(low, other, even), jnp.where(pick, 1.0, 0.0).astype(bf16))
+    return jnp.where(low, even, other).astype(f32), lse
+
+
+def absorb_pairs(outs, lses, items, rate):
+    loaded = []
+    for pair, offs, new, lse_new in items:
+        count = new.shape[0]
+        low = half_mask(count, 0)
+        spots = [pl.ds(off, count, rate) for off in offs]
+        olds = [outs[pair, spot, :] for spot in spots]
+        lse_olds = [lses[pair, spot, :] for spot in spots]
+        loaded.append((low, spots, olds, lse_olds))
+    merged = []
+    for (pair, offs, new, lse_new), (low, spots, olds, lse_olds) in zip(items, loaded):
+        old, lse_old = jnp.where(low, *olds), jnp.where(low, *lse_olds)
+        gap = lse_new - lse_old
+        small = jnp.exp(-jnp.abs(gap))
+        share = jnp.where(gap > 0.0, 1.0, small) / (1.0 + small)
+        lse = jnp.maximum(lse_old, lse_new) + jnp.log(1.0 + small)
+        merged.append((old + share * (new - old), lse))
+    for (pair, *_), (low, spots, olds, lse_olds), (out, lse) in zip(items, loaded, merged):
+        outs[pair, spots[0], :] = jnp.where(low, out, olds[0])
+        lses[pair, spots[0], :] = jnp.where(low, lse, lse_olds[0])
+        outs[pair, spots[1], :] = jnp.where(low, outs[pair, spots[1], :], out)
+        lses[pair, spots[1], :] = jnp.where(low, lses[pair, spots[1], :], lse)
+
+
+def absorb_coded(outs, lses, coded, offs, level, rate):
+    mine = lax.rem(lax.axis_index("seq"), 4)
+    items = []
+    for j in range(2):
+        pair = lax.div(mine, 2) ^ j
+        out, lse = decode_pair(coded[2 * j], coded[2 * j + 1], lax.rem(mine, 2))
+        items.append((pair, (offs.of(2 * pair, level), offs.of(2 * pair + 1, level)), out, lse))
+    absorb_pairs(outs, lses, items, rate)
 
 
 def widen(src, dst):
@@ -89,6 +130,19 @@
         part = pl.ds(pl.multiple_of(i * step, step), step)
         for p in range(src.shape[1] // LANES):
             dst[p, part, :] = src[part, p * LANES : (p + 1) * LANES].astype(f32)
+
+
+class Table:
+    def __init__(self, ref):
+        self.rows = ref[...]
+
+    def of(self, head, level):
+        if isinstance(head, int):
+            return self.rows[head, level]
+        found = self.rows[0, level]
+        for h in range(1, 4):
+            found = jnp.where(head == h, self.rows[h, level], found)
+        return found
 
 
 def fetch(offs_any, offs, sem):
@@ -113,6 +167,7 @@
         for what in ("kv", "q"):
             for level, count, rate, near in levels:
                 off = offs[head, level]
+                near = near or what == "q"
                 ref = near_out[d] if near else far_out[d]
                 at = base[near]
                 if what == "kv":
@@ -136,7 +191,7 @@
     scale = jnp.asarray(0.125, bf16)
     cols = slice(pair * LANES, (pair + 1) * LANES)
 
-    @pl.loop(0, q_ref.shape[0] // SEG)
+    @pl.loop(0, q_ref.shape[0] // SEG, unroll=4)
     def _(s):
         part = pl.ds(pl.multiple_of(s * SEG, SEG), SEG)
         q, k, v = q_ref[part, cols] * scale, k_ref[part, cols], v_ref[part, cols]
@@ -150,25 +205,6 @@
         lse_ref[pair, part, :] = lse
 
 
-def absorb(outs, lses, head, off, rate, new, lse_new):
-    pair, half = lax.div(head, 2), lax.rem(head, 2)
-    count = new.shape[0]
-    vl = half_mask(count, half)
-    picked = pl.ds(off, count, rate)
-    old, lse_old = outs[pair, picked, :], lses[pair, picked, :]
-    gap = lse_new - lse_old
-    small = jnp.exp(-jnp.abs(gap))
-    share = jnp.where(gap > 0.0, 1.0, small) / (1.0 + small)
-    outs[pair, picked, :] = jnp.where(vl, old + share * (new - old), old)
-    lse = jnp.maximum(lse_old, lse_new) + jnp.log(1.0 + small)
-    lses[pair, picked, :] = jnp.where(vl, lse, lse_old)
-
-
-def absorb_coded(outs, lses, head, off, rate, coded):
-    lse = decode_lse(coded, lax.rem(head, 2))
-    absorb(outs, lses, head, off, rate, coded.astype(f32), lse)
-
-
 def keys_values(tile, half):
     vl = half_mask(tile.shape[0], half)
     zero, one = jnp.zeros_like(tile), jnp.ones_like(tile)
@@ -188,17 +224,16 @@
         outs[d][...] = encode(out, lse, vl).astype(bf16)
 
 
-def far_kernel(mid, top, *refs):
-    far, gathered, outs = refs[:4], refs[4:8], refs[8:12]
+def far_kernel(base, mid, top, *refs):
+    held, gathered, outs = refs[:4], refs[4:8], refs[8:12]
     half = lax.rem(lax.axis_index("seq"), 2)
-    base = mid + top
     blocks = (
         ([r[: 4 * mid, :] for r in gathered], base, mid // 2, 0),
         ([r[4 * mid :, :] for r in gathered], base + mid // 2, top // 2, mid),
     )
     for tiles, q_at, few, out_at in blocks:
         keys, values = zip(*[keys_values(t, half) for t in tiles])
-        tile = jnp.concatenate([r[q_at : q_at + few, :].astype(f32) for r in far], axis=0)
+        tile = jnp.concatenate([r[q_at : q_at + few, :].astype(f32) for r in held], axis=0)
         q = jnp.concatenate([tile, swap_halves(tile)], axis=0).astype(bf16)
         out, lse = attend_one(q, keys, values)
         found = encode(out, lse, half_mask(8 * few, half))
@@ -208,43 +243,33 @@
                 outs[d][at : at + few, :] = found[start : start + few, :].astype(bf16)
 
 
-def second_kernel(rate, offs_any, qs, ks, vs, outs_in, lses_in, *refs):
-    near, outs, lses, offs, sem = refs[:4], refs[4], refs[5], refs[6], refs[7]
-    copy = fetch(offs_any, offs, sem)
-    mine = lax.rem(lax.axis_index("seq"), 4)
+def second_kernel(rate, offs_ref, qs, ks, vs, outs_in, lses_in, *refs):
+    near, outs, lses = refs[:4], refs[4], refs[5]
+    offs = Table(offs_ref)
     count = near[0].shape[0]
-    copy.wait()
     for p in range(2):
         queries, keys, values = [], [], []
         for h in range(2):
             vl = half_mask(count, h)
-            picked = pl.ds(offs[2 * p + h, 1], count, rate)
+            picked = pl.ds(offs.of(2 * p + h, 1), count, rate)
             queries.append((qs[p, picked, :] * 0.125).astype(bf16))
             k = ks[p, picked, :]
             keys.append(jnp.where(vl, k, jnp.zeros_like(k)).astype(bf16))
             values.append(with_ones(vs[p, picked, :], vl).astype(bf16))
         out, lse = attend_pair(queries, keys, values)
-        for h in range(2):
-            head = 2 * p + h
-            absorb(outs, lses, head, offs[head, 1], rate, out, lse)
-    for d in range(4):
-        head = mine ^ d
-        absorb_coded(outs, lses, head, offs[head, 2], rate, near[d][...])
-
-
-def final_kernel(levels, offs_any, outs_in, lses_in, *refs):
+        absorb_pairs(outs, lses, [(p, (offs.of(2 * p, 1), offs.of(2 * p + 1, 1)), out, lse)], rate)
+    absorb_coded(outs, lses, [r[...] for r in near], offs, 2, rate)
+
+
+def final_kernel(levels, offs_ref, outs_in, lses_in, *refs):
     far, outs, lses, out_any = refs[:4], refs[4], refs[5], refs[6]
-    offs, out, sem, sems = refs[7:]
-    copy = fetch(offs_any, offs, sem)
-    mine = lax.rem(lax.axis_index("seq"), 4)
-    copy.wait()
-    for d in range(4):
-        head = mine ^ d
-        at = 0
-        for level, count, rate, near in levels:
-            if not near:
-                absorb_coded(outs, lses, head, offs[head, level], rate, far[d][at : at + count, :])
-                at += count
+    out, sems = refs[7:]
+    offs = Table(offs_ref)
+    at = 0
+    for level, count, rate, near in levels:
+        if not near:
+            absorb_coded(outs, lses, [r[at : at + count, :] for r in far], offs, level, rate)
+            at += count
     copies = []
     for i in range(out.shape[0] // SEG):
         part = slice(i * SEG, (i + 1) * SEG)
@@ -260,7 +285,7 @@
     body, outs, spaces, scratch=(), flops=0, bytes_moved=0, exps=0, aliases=None, out_spaces="", mib=24
 ):
     whole = pl.BlockSpec(memory_space=VMEM)
-    place = {"v": whole, "a": pl.BlockSpec(memory_space=pltpu.HBM)}
+    place = {"v": whole, "a": pl.BlockSpec(memory_space=pltpu.HBM), "s": pl.BlockSpec(memory_space=pltpu.SMEM)}
     return pl.pallas_call(
         body,
         out_shape=outs,
@@ -290,9 +315,9 @@
         (3, mid, rate_three, False),
         (4, top, rate_four, False),
     )
+    queries = (near_count + mid + top) // 2
     offsets = offsets.T
     table = pltpu.SMEM(offsets.shape, jnp.int32)
-    one_sem = pltpu.SemaphoreType.DMA
 
     def tile(n, kind=bf16):
         return jax.ShapeDtypeStruct((n, LANES), kind)
@@ -300,8 +325,8 @@
     wide = jax.ShapeDtypeStruct((2, rows, LANES), f32)
     parts = call(
         lambda *refs: pack_kernel(levels, *refs),
-        [tile(near_count * 3 // 2)] * 4
-        + [tile((mid + top) * 3 // 2)] * 4
+        [tile(near_count + queries)] * 4
+        + [tile(mid + top)] * 4
         + [jax.ShapeDtypeStruct(query.shape, bf16)] * 3
         + [wide] * 3,
         "aaaa",
@@ -341,20 +366,19 @@
     near_back = [near_found[0]] + [swapped(near_found[d], d) for d in (1, 2, 3)]
 
     far_found = call(
-        lambda *refs: far_kernel(mid, top, *refs),
+        lambda *refs: far_kernel(near_count * 3 // 2, mid, top, *refs),
         [tile(mid + top)] * 4,
         "v" * 8,
         flops=2 << 30,
         bytes_moved=2 << 20,
         exps=1 << 20,
-    )(*far_held, *gathered)
+    )(*near_held, *gathered)
     far_back = [far_found[0]] + [swapped(far_found[d], d) for d in (1, 2, 3)]
 
     state = call(
         lambda *refs: second_kernel(RATE1, *refs),
         [wide, wide],
-        "avvvvvvvvv",
-        (table, one_sem),
+        "vvvvvvvvvv",
         flops=2 << 30,
         bytes_moved=4 << 20,
         exps=1 << 20,
@@ -364,8 +388,8 @@
     return call(
         lambda *refs: final_kernel(levels, *refs),
         [wide, wide, jax.ShapeDtypeStruct((rows, width), bf16)],
-        "avvvvvv",
-        (table, VMEM((rows, width), bf16), one_sem, pltpu.SemaphoreType.DMA((rows // SEG,))),
+        "vvvvvvv",
+        (VMEM((rows, width), bf16), pltpu.SemaphoreType.DMA((rows // SEG,))),
         bytes_moved=6 << 20,
         aliases={1: 0, 2: 1},
         out_spaces="vva",

time: 50.7 us -> 47.5 us (0.937)
  Pallas kernels: 26.9 us -> 23.3 us
    pallas_call x2, Pallas kernels: 8.52 us -> 5.76 us  [per_device(): call(lambda *refs, pair=pair: first_kernel(pair, *refs), [wide, wide], 'v...]
  transfers between devices with their start and end apart: 16 -> 16, of which waited for: 1 -> 1; matrix products, arithmetic and copies ran while one was open for 0% -> 0% of each run, Pallas kernels for 42% -> 38%
where the time goes in v4:
time: 47.5 us; the launch traced here: 47.4 us
  Pallas kernels  23.3 us (49%)
  starting transfers between devices  22.9 us (48%)
  waiting for transfers between devices  0.82 us (2%)
    ppermute x16, starting transfers between devices, swapped(): lax.ppermute(shard, 'seq', [(i, i ^ bits) for i in range(lax.axis_size('s...  22.9 us
    pallas_call x1, Pallas kernels, per_device(): call(lambda *refs: near_kernel(near_count, *refs), [tile(near_count)] * 4...  6.22 us
    pallas_call x2, Pallas kernels, per_device(): call(lambda *refs, pair=pair: first_kernel(pair, *refs), [wide, wide], 'v...  5.76 us
    pallas_call x1, Pallas kernels, per_device(): call(lambda *refs: second_kernel(RATE1, *refs), [wide, wide], 'vvvvvvvvvv...  3.73 us
    pallas_call x1, Pallas kernels, per_device(): call(lambda *refs: pack_kernel(levels, *refs), [tile(near_count + queries...  3.06 us
    pallas_call x1, Pallas kernels, per_device(): call(lambda *refs: far_kernel(near_count * 3 // 2, mid, top, *refs), [til...  2.35 us
    pallas_call x1, Pallas kernels, per_device(): call(lambda *refs: final_kernel(levels, *refs), [wide, wide, jax.ShapeDty...  2.13 us
  transfers between devices with their start and end apart: 16, of which 1 were waited for; matrix products, arithmetic and copies ran while one was open for 0% of the time, Pallas kernels for 38%

profile of v4, /device:TPU:0, one launch (start us, length us, event | category | flops | bytes accessed | tf_op | source)
XLA Modules:
  0.0 47.4 jit_solution(16690840145843704929)
XLA Ops:
  0.0 3.1 %shard_map.46 = (bf16[848,128]{1,0:T(8,128)(2,1)S(1)}, bf16[848,128]{1,0:T(8,128)(2,1)S(1)}, bf16[848,128]{1,0:T(8,128)(2,1)S(1)}, bf16[848,128]{1,0:T(8,128)(2,...) custom-call(s32[4,5]{1,0:T(4,128)} %bitcast.1, ...), custom_call_target="tpu_custom_call" | custom-call | bytes 5242880 | tf_op jit(solution)/shard_map/pallas_call | solution.py:326
  3.1 1.8 %collective-permute-start.6 = (bf16[160,128]{1,0:T(8,128)(2,1)S(1)}, bf16[160,128]{1,0:T(8,128)(2,1)S(1)}, u32[]{:S(2)}, u32[]{:S(2)}) collective-permute-start(bf16[160,128]{1,0:T(8,128)(2,1)S(1)} %get-tuple-element.55), channel_id=1, source_target_pairs={{0,4},{4,0},{8,12},{12,8},{16,20},{20,16},{24,28},{28,24},{32,36},... | collective-permute-start | bytes 122888 | tf_op jit(solution)/shard_map/ppermute | solution.py:302
  4.8 1.9 %collective-permute-start.7 = (bf16[160,128]{1,0:T(8,128)(2,1)S(1)}, bf16[160,128]{1,0:T(8,128)(2,1)S(1)}, u32[]{:S(2)}, u32[]{:S(2)}) collective-permute-start(bf16[160,128]{1,0:T(8,128)(2,1)S(1)} %get-tuple-element.56), channel_id=1, source_target_pairs={{0,8},{4,12},{8,0},{12,4},{16,24},{20,28},{24,16},{28,20},{32,40},... | collective-permute-start | bytes 122888 | tf_op jit(solution)/shard_map/ppermute | solution.py:302
  6.8 0.0 collective-permute-start.8
  6.8 1.6 %collective-permute-start = (bf16[848,128]{1,0:T(8,128)(2,1)S(1)}, bf16[848,128]{1,0:T(8,128)(2,1)S(1)}, u32[]{:S(2)}, u32[]{:S(2)}) collective-permute-start(bf16[848,128]{1,0:T(8,128)(2,1)S(1)} %get-tuple-element.45), channel_id=1, source_target_pairs={{0,4},{4,0},{8,12},{12,8},{16,20},{20,16},{24,28},{28,24},{32,36},... | collective-permute-start | bytes 651272 | tf_op jit(solution)/shard_map/ppermute | solution.py:302
  8.3 1.9 %collective-permute-start.1 = (bf16[848,128]{1,0:T(8,128)(2,1)S(1)}, bf16[848,128]{1,0:T(8,128)(2,1)S(1)}, u32[]{:S(2)}, u32[]{:S(2)}) collective-permute-start(bf16[848,128]{1,0:T(8,128)(2,1)S(1)} %get-tuple-element.46), channel_id=1, source_target_pairs={{0,8},{4,12},{8,0},{12,4},{16,24},{20,28},{24,16},{28,20},{32,40},... | collective-permute-start | bytes 651272 | tf_op jit(solution)/shard_map/ppermute | solution.py:302
  10.3 2.9 %shard_map.47 = (f32[2,2048,128]{2,1,0:T(8,128)S(1)}, f32[2,2048,128]{2,1,0:T(8,128)S(1)}) custom-call(bf16[2048,256]{1,0:T(8,128)(2,1)S(1)} %get-tuple-element.37.refs_0_, bf16[2048,256]{1,0:T(8,128)(2,1)S(1)} %get-tuple-element.38.refs_1_, bf16[2048,256]{1,0:T(8,128)(2,1)S(1)} %get-tuple-element.39.refs_2_), custom_call_target="tpu_custom_call" | custom-call | flops 2147483648 | bytes 4194304 | tf_op jit(solution)/shard_map/pallas_call | solution.py:343
  13.2 0.1 collective-permute-start.2
  13.4 3.1 %collective-permute-start.9 = (bf16[128,128]{1,0:T(8,128)(2,1)S(1)}, bf16[128,128]{1,0:T(8,128)(2,1)S(1)}, u32[]{:S(2)}, u32[]{:S(2)}) collective-permute-start(bf16[128,128]{1,0:T(8,128)(2,1)S(1)} %pad_maximum_fusion), channel_id=1, source_target_pairs={{0,64},{4,68},{8,72},{12,76},{16,80},{20,84},{24,88},{28,92},{32,9... | collective-permute-start | bytes 98312 | tf_op jit(solution)/shard_map/ppermute | solution.py:302
  16.5 2.9 %shard_map.48 = (f32[2,2048,128]{2,1,0:T(8,128)S(1)}, f32[2,2048,128]{2,1,0:T(8,128)S(1)}) custom-call(bf16[2048,256]{1,0:T(8,128)(2,1)S(1)} %get-tuple-element.37.refs_0_, bf16[2048,256]{1,0:T(8,128)(2,1)S(1)} %get-tuple-element.38.refs_1_, bf16[2048,256]{1,0:T(8,128)(2,1)S(1)} %get-tuple-element.39.refs_2_, ...), custom_call_target="tpu_custom_call", output_to_operand_aliasing={{0}: (3, {}), {1}: (4, {})} | custom-call | flops 2147483648 | bytes 4194304 | tf_op jit(solution)/shard_map/pallas_call | solution.py:343
  19.4 4.3 %collective-permute-start.12 = (bf16[768,128]{1,0:T(8,128)(2,1)S(1)}, bf16[768,128]{1,0:T(8,128)(2,1)S(1)}, u32[]{:S(2)}, u32[]{:S(2)}) collective-permute-start(bf16[768,128]{1,0:T(8,128)(2,1)S(1)} %constant_dynamic-update-slice_fusion.refs_4_), channel_id=1, source_target_pairs={{0,48},{4,52},{8,56},{12,60},{16,32},{20,36},{24,40},{28,44},{32,1... | collective-permute-start | bytes 589832 | tf_op jit(solution)/shard_map/ppermute | solution.py:302
  23.7 1.1 %collective-permute-start.10 = (bf16[768,128]{1,0:T(8,128)(2,1)S(1)}, bf16[768,128]{1,0:T(8,128)(2,1)S(1)}, u32[]{:S(2)}, u32[]{:S(2)}) collective-permute-start(bf16[768,128]{1,0:T(8,128)(2,1)S(1)} %constant_dynamic-update-slice_fusion.refs_4_), channel_id=1, source_target_pairs={{0,32},{4,36},{8,40},{12,44},{16,48},{20,52},{24,56},{28,60},{32,0... | collective-permute-start | bytes 589832 | tf_op jit(solution)/shard_map/ppermute | solution.py:302
  24.8 6.2 %shard_map.49 = (bf16[512,128]{1,0:T(8,128)(2,1)S(1)}, bf16[512,128]{1,0:T(8,128)(2,1)S(1)}, bf16[512,128]{1,0:T(8,128)(2,1)S(1)}, bf16[512,128]{1,0:T(8,128)(2,1)S(1)}) custom-call(bf16[848,128]{1,0:T(8,128)(2,1)S(1)} %get-tuple-element.44.refs_0_, bf16[848,128]{1,0:T(8,128)(2,1)S(1)} %collective-permute-done.refs_1_, ...), custom_call_target="tpu_custom_call" | custom-call | flops 6442450944 | bytes 2097152 | tf_op jit(solution)/shard_map/pallas_call | solution.py:358
  31.0 1.7 %collective-permute-start.3 = (bf16[512,128]{1,0:T(8,128)(2,1)S(1)}, bf16[512,128]{1,0:T(8,128)(2,1)S(1)}, u32[]{:S(2)}, u32[]{:S(2)}) collective-permute-start(bf16[512,128]{1,0:T(8,128)(2,1)S(1)} %get-tuple-element.49), channel_id=1, source_target_pairs={{0,4},{4,0},{8,12},{12,8},{16,20},{20,16},{24,28},{28,24},{32,36},... | collective-permute-start | bytes 393224 | tf_op jit(solution)/shard_map/ppermute | solution.py:302
  32.7 1.6 %collective-permute-start.4 = (bf16[512,128]{1,0:T(8,128)(2,1)S(1)}, bf16[512,128]{1,0:T(8,128)(2,1)S(1)}, u32[]{:S(2)}, u32[]{:S(2)}) collective-permute-start(bf16[512,128]{1,0:T(8,128)(2,1)S(1)} %get-tuple-element.50), channel_id=1, source_target_pairs={{0,8},{4,12},{8,0},{12,4},{16,24},{20,28},{24,16},{28,20},{32,40},... | collective-permute-start | bytes 393224 | tf_op jit(solution)/shard_map/ppermute | solution.py:302
  34.3 0.3 collective-permute-start.5
  34.6 2.4 %shard_map.51 = (bf16[160,128]{1,0:T(8,128)(2,1)S(1)}, bf16[160,128]{1,0:T(8,128)(2,1)S(1)}, bf16[160,128]{1,0:T(8,128)(2,1)S(1)}, bf16[160,128]{1,0:T(8,128)(2,1)S(1)}) custom-call(bf16[848,128]{1,0:T(8,128)(2,1)S(1)} %get-tuple-element.44.refs_0_, bf16[848,128]{1,0:T(8,128)(2,1)S(1)} %collective-permute-done.refs_1_, ...), custom_call_target="tpu_custom_call" | custom-call | flops 2147483648 | bytes 2097152 | tf_op jit(solution)/shard_map/pallas_call | solution.py:368
  37.0 1.7 %collective-permute-start.13 = (bf16[160,128]{1,0:T(8,128)(2,1)S(1)}, bf16[160,128]{1,0:T(8,128)(2,1)S(1)}, u32[]{:S(2)}, u32[]{:S(2)}) collective-permute-start(bf16[160,128]{1,0:T(8,128)(2,1)S(1)} %get-tuple-element.59), channel_id=1, source_target_pairs={{0,4},{4,0},{8,12},{12,8},{16,20},{20,16},{24,28},{28,24},{32,36},... | collective-permute-start | bytes 122888 | tf_op jit(solution)/shard_map/ppermute | solution.py:302
  38.6 1.6 %collective-permute-start.14 = (bf16[160,128]{1,0:T(8,128)(2,1)S(1)}, bf16[160,128]{1,0:T(8,128)(2,1)S(1)}, u32[]{:S(2)}, u32[]{:S(2)}) collective-permute-start(bf16[160,128]{1,0:T(8,128)(2,1)S(1)} %get-tuple-element.60), channel_id=1, source_target_pairs={{0,8},{4,12},{8,0},{12,4},{16,24},{20,28},{24,16},{28,20},{32,40},... | collective-permute-start | bytes 122888 | tf_op jit(solution)/shard_map/ppermute | solution.py:302
  40.2 0.4 collective-permute-start.15
  40.5 0.0 collective-permute-done.5.refs_9_
  40.6 3.7 %shard_map.50 = (f32[2,2048,128]{2,1,0:T(8,128)S(1)}, f32[2,2048,128]{2,1,0:T(8,128)S(1)}) custom-call(s32[4,5]{1,0:T(4,128)S(1)} %bitcast.2, f32[2,2048,128]{2,1,0:T(8,128)S(1)} %get-tuple-element.34.refs_1_, f32[2,2048,128]{2,1,0:T(8,128)S(1)} %get-tuple-element.35.refs_2_, ...), custom_call_target="tpu_custom_call", output_to_operand_aliasing={{0}: (4, {}), {1}: (5, {})} | custom-call | flops 2147483648 | bytes 4194304 | tf_op jit(solution)/shard_map/pallas_call | solution.py:378
  44.3 0.8 %collective-permute-done.15.refs_6_ = bf16[160,128]{1,0:T(8,128)(2,1)S(1)} collective-permute-done((bf16[160,128]{1,0:T(8,128)(2,1)S(1)}, bf16[160,128]{1,0:T(8,128)(2,1)S(1)}, u32[]{:S(2)}, u32[]{:S(2)}) %collective-permute-start.15) | collective-permute-done | bytes 40992 | tf_op jit(solution)/shard_map/ppermute | solution.py:302
  45.1 2.1 %shard_map.52 = (f32[2,2048,128]{2,1,0:T(8,128)S(1)}, f32[2,2048,128]{2,1,0:T(8,128)S(1)}, bf16[2048,256]{1,0:T(8,128)(2,1)}) custom-call(s32[4,5]{1,0:T(4,128)S(1)} %bitcast.3, f32[2,2048,128]{2,1,0:T(8,128)S(1)} %get-tuple-element.52.refs_1_, f32[2,2048,128]{2,1,0:T(8,128)S(1)} %get-tuple-element.53.refs_2_, ...), custom_call_target="tpu_custom_call", output_to_operand_aliasing={{0}: (1, {}), {1}: (2, {})} | custom-call | bytes 6291456 | tf_op jit(solution)/shard_map/pallas_call | solution.py:388
  (27 shorter events, 0.1 us)
Async XLA Ops:
  3.1 10.1 %collective-permute-start.6 = (bf16[160,128]{1,0:T(8,128)(2,1)S(1)}, bf16[160,128]{1,0:T(8,128)(2,1)S(1)}, u32[]{:S(2)}, u32[]{:S(2)}) collective-permute-start(bf16[160,128]{1,0:T(8,128)(2,1)S(1)} %get-tuple-element.55), channel_id=1, source_target_pairs={{0,4},{4,0},{8,12},{12,8},{16,20},{20,16},{24,28},{28,24},{32,36},... | collective-permute-start | bytes 122888 | tf_op jit(solution)/shard_map/ppermute | solution.py:302
  4.8 8.4 %collective-permute-start.7 = (bf16[160,128]{1,0:T(8,128)(2,1)S(1)}, bf16[160,128]{1,0:T(8,128)(2,1)S(1)}, u32[]{:S(2)}, u32[]{:S(2)}) collective-permute-start(bf16[160,128]{1,0:T(8,128)(2,1)S(1)} %get-tuple-element.56), channel_id=1, source_target_pairs={{0,8},{4,12},{8,0},{12,4},{16,24},{20,28},{24,16},{28,20},{32,40},... | collective-permute-start | bytes 122888 | tf_op jit(solution)/shard_map/ppermute | solution.py:302
  6.8 6.5 %collective-permute-start.8 = (bf16[160,128]{1,0:T(8,128)(2,1)S(1)}, bf16[160,128]{1,0:T(8,128)(2,1)S(1)}, u32[]{:S(2)}, u32[]{:S(2)}) collective-permute-start(bf16[160,128]{1,0:T(8,128)(2,1)S(1)} %get-tuple-element.57), channel_id=1, source_target_pairs={{0,12},{4,8},{8,4},{12,0},{16,28},{20,24},{24,20},{28,16},{32,44},... | collective-permute-start | bytes 122888 | tf_op jit(solution)/shard_map/ppermute | solution.py:302
  6.8 16.9 %collective-permute-start = (bf16[848,128]{1,0:T(8,128)(2,1)S(1)}, bf16[848,128]{1,0:T(8,128)(2,1)S(1)}, u32[]{:S(2)}, u32[]{:S(2)}) collective-permute-start(bf16[848,128]{1,0:T(8,128)(2,1)S(1)} %get-tuple-element.45), channel_id=1, source_target_pairs={{0,4},{4,0},{8,12},{12,8},{16,20},{20,16},{24,28},{28,24},{32,36},... | collective-permute-start | bytes 651272 | tf_op jit(solution)/shard_map/ppermute | solution.py:302
  8.3 16.5 %collective-permute-start.1 = (bf16[848,128]{1,0:T(8,128)(2,1)S(1)}, bf16[848,128]{1,0:T(8,128)(2,1)S(1)}, u32[]{:S(2)}, u32[]{:S(2)}) collective-permute-start(bf16[848,128]{1,0:T(8,128)(2,1)S(1)} %get-tuple-element.46), channel_id=1, source_target_pairs={{0,8},{4,12},{8,0},{12,4},{16,24},{20,28},{24,16},{28,20},{32,40},... | collective-permute-start | bytes 651272 | tf_op jit(solution)/shard_map/ppermute | solution.py:302
  13.2 11.6 %collective-permute-start.2 = (bf16[848,128]{1,0:T(8,128)(2,1)S(1)}, bf16[848,128]{1,0:T(8,128)(2,1)S(1)}, u32[]{:S(2)}, u32[]{:S(2)}) collective-permute-start(bf16[848,128]{1,0:T(8,128)(2,1)S(1)} %get-tuple-element.47), channel_id=1, source_target_pairs={{0,12},{4,8},{8,4},{12,0},{16,28},{20,24},{24,20},{28,16},{32,44},... | collective-permute-start | bytes 651272 | tf_op jit(solution)/shard_map/ppermute | solution.py:302
  13.4 6.0 %collective-permute-start.9 = (bf16[128,128]{1,0:T(8,128)(2,1)S(1)}, bf16[128,128]{1,0:T(8,128)(2,1)S(1)}, u32[]{:S(2)}, u32[]{:S(2)}) collective-permute-start(bf16[128,128]{1,0:T(8,128)(2,1)S(1)} %pad_maximum_fusion), channel_id=1, source_target_pairs={{0,64},{4,68},{8,72},{12,76},{16,80},{20,84},{24,88},{28,92},{32,9... | collective-permute-start | bytes 98312 | tf_op jit(solution)/shard_map/ppermute | solution.py:302
  19.4 14.9 %collective-permute-start.12 = (bf16[768,128]{1,0:T(8,128)(2,1)S(1)}, bf16[768,128]{1,0:T(8,128)(2,1)S(1)}, u32[]{:S(2)}, u32[]{:S(2)}) collective-permute-start(bf16[768,128]{1,0:T(8,128)(2,1)S(1)} %constant_dynamic-update-slice_fusion.refs_4_), channel_id=1, source_target_pairs={{0,48},{4,52},{8,56},{12,60},{16,32},{20,36},{24,40},{28,44},{32,1... | collective-permute-start | bytes 589832 | tf_op jit(solution)/shard_map/ppermute | solution.py:302
  23.7 10.9 %collective-permute-start.11 = (bf16[768,128]{1,0:T(8,128)(2,1)S(1)}, bf16[768,128]{1,0:T(8,128)(2,1)S(1)}, u32[]{:S(2)}, u32[]{:S(2)}) collective-permute-start(bf16[768,128]{1,0:T(8,128)(2,1)S(1)} %constant_dynamic-update-slice_fusion.refs_4_), channel_id=1, source_target_pairs={{0,16},{4,20},{8,24},{12,28},{16,0},{20,4},{24,8},{28,12},{32,48},... | collective-permute-start | bytes 589832 | tf_op jit(solution)/shard_map/ppermute | solution.py:302
  23.7 10.9 %collective-permute-start.10 = (bf16[768,128]{1,0:T(8,128)(2,1)S(1)}, bf16[768,128]{1,0:T(8,128)(2,1)S(1)}, u32[]{:S(2)}, u32[]{:S(2)}) collective-permute-start(bf16[768,128]{1,0:T(8,128)(2,1)S(1)} %constant_dynamic-update-slice_fusion.refs_4_), channel_id=1, source_target_pairs={{0,32},{4,36},{8,40},{12,44},{16,48},{20,52},{24,56},{28,60},{32,0... | collective-permute-start | bytes 589832 | tf_op jit(solution)/shard_map/ppermute | solution.py:302
  31.0 9.2 %collective-permute-start.3 = (bf16[512,128]{1,0:T(8,128)(2,1)S(1)}, bf16[512,128]{1,0:T(8,128)(2,1)S(1)}, u32[]{:S(2)}, u32[]{:S(2)}) collective-permute-start(bf16[512,128]{1,0:T(8,128)(2,1)S(1)} %get-tuple-element.49), channel_id=1, source_target_pairs={{0,4},{4,0},{8,12},{12,8},{16,20},{20,16},{24,28},{28,24},{32,36},... | collective-permute-start | bytes 393224 | tf_op jit(solution)/shard_map/ppermute | solution.py:302
  32.7 7.9 %collective-permute-start.4 = (bf16[512,128]{1,0:T(8,128)(2,1)S(1)}, bf16[512,128]{1,0:T(8,128)(2,1)S(1)}, u32[]{:S(2)}, u32[]{:S(2)}) collective-permute-start(bf16[512,128]{1,0:T(8,128)(2,1)S(1)} %get-tuple-element.50), channel_id=1, source_target_pairs={{0,8},{4,12},{8,0},{12,4},{16,24},{20,28},{24,16},{28,20},{32,40},... | collective-permute-start | bytes 393224 | tf_op jit(solution)/shard_map/ppermute | solution.py:302
  34.3 6.3 %copy-start = (s32[5,4]{0,1:T(4,128)S(1)}, s32[5,4]{0,1:T(4,128)}, u32[]{:S(2)}) copy-start(s32[5,4]{0,1:T(4,128)} %param.7) | copy-start | bytes 244
  34.3 6.3 %collective-permute-start.5 = (bf16[512,128]{1,0:T(8,128)(2,1)S(1)}, bf16[512,128]{1,0:T(8,128)(2,1)S(1)}, u32[]{:S(2)}, u32[]{:S(2)}) collective-permute-start(bf16[512,128]{1,0:T(8,128)(2,1)S(1)} %get-tuple-element.51), channel_id=1, source_target_pairs={{0,12},{4,8},{8,4},{12,0},{16,28},{20,24},{24,20},{28,16},{32,44},... | collective-permute-start | bytes 393224 | tf_op jit(solution)/shard_map/ppermute | solution.py:302
  37.0 7.3 %collective-permute-start.13 = (bf16[160,128]{1,0:T(8,128)(2,1)S(1)}, bf16[160,128]{1,0:T(8,128)(2,1)S(1)}, u32[]{:S(2)}, u32[]{:S(2)}) collective-permute-start(bf16[160,128]{1,0:T(8,128)(2,1)S(1)} %get-tuple-element.59), channel_id=1, source_target_pairs={{0,4},{4,0},{8,12},{12,8},{16,20},{20,16},{24,28},{28,24},{32,36},... | collective-permute-start | bytes 122888 | tf_op jit(solution)/shard_map/ppermute | solution.py:302
  38.6 5.7 %collective-permute-start.14 = (bf16[160,128]{1,0:T(8,128)(2,1)S(1)}, bf16[160,128]{1,0:T(8,128)(2,1)S(1)}, u32[]{:S(2)}, u32[]{:S(2)}) collective-permute-start(bf16[160,128]{1,0:T(8,128)(2,1)S(1)} %get-tuple-element.60), channel_id=1, source_target_pairs={{0,8},{4,12},{8,0},{12,4},{16,24},{20,28},{24,16},{28,20},{32,40},... | collective-permute-start | bytes 122888 | tf_op jit(solution)/shard_map/ppermute | solution.py:302
  40.2 4.9 %collective-permute-start.15 = (bf16[160,128]{1,0:T(8,128)(2,1)S(1)}, bf16[160,128]{1,0:T(8,128)(2,1)S(1)}, u32[]{:S(2)}, u32[]{:S(2)}) collective-permute-start(bf16[160,128]{1,0:T(8,128)(2,1)S(1)} %get-tuple-element.61), channel_id=1, source_target_pairs={{0,12},{4,8},{8,4},{12,0},{16,28},{20,24},{24,20},{28,16},{32,44},... | collective-permute-start | bytes 122888 | tf_op jit(solution)/shard_map/ppermute | solution.py:302

commit v5 on v4

--- a/solution.py
+++ b/solution.py
@@ -9,6 +9,7 @@
 SEG = 512
 PACK_MIB = 24
 RATE1 = 4
+SAFE = 46.0
 bf16 = jnp.bfloat16
 f32 = jnp.float32
 LANES = 128
@@ -33,29 +34,49 @@
     return pltpu.roll(x, HALF, 1)
 
 
-def softmax(scores, values):
-    top = scores[0].max(axis=1, keepdims=True)
-    for s in scores[1:]:
-        top = jnp.maximum(top, s.max(axis=1, keepdims=True))
-    probs = [jnp.exp(s - top).astype(bf16) for s in scores]
+def softmax(scores, values, shift):
+    top = None
+    if shift:
+        top = scores[0].max(axis=1, keepdims=True)
+        for s in scores[1:]:
+            top = jnp.maximum(top, s.max(axis=1, keepdims=True))
+        scores = [s - top for s in scores]
+    probs = [jnp.exp(s).astype(bf16) for s in scores]
     return top, jnp.concatenate(probs, axis=1), jnp.concatenate(values, axis=0)
 
 
-def attend_one(q, keys, values):
-    top, probs, wide = softmax([dot_nt(q, k) for k in keys], values)
+def attend_one(q, keys, values, shift):
+    top, probs, wide = softmax([dot_nt(q, k) for k in keys], values, shift)
     acc = dot_nn(probs, wide)
     total = acc[:, LANES:]
-    return acc[:, :LANES] / total, top + jnp.log(total)
-
-
-def attend_pair(queries, keys, values):
+    lse = jnp.log(total)
+    return acc[:, :LANES] / total, top + lse if shift else lse
+
+
+def attend_pair(queries, keys, values, shift):
     low = half_mask(queries[0].shape[0], 0)
     tops, probs, wides = zip(
-        *[softmax([dot_nt(q, k)], [v]) for q, k, v in zip(queries, keys, values)]
+        *[softmax([dot_nt(q, k)], [v], shift) for q, k, v in zip(queries, keys, values)]
     )
     acc = dot_nn(jnp.concatenate(probs, axis=1), jnp.concatenate(wides, axis=0))
     total = acc[:, LANES:]
-    return acc[:, :LANES] / total, jnp.where(low, tops[0], tops[1]) + jnp.log(total)
+    lse = jnp.log(total)
+    return acc[:, :LANES] / total, jnp.where(low, *tops) + lse if shift else lse
+
+
+def out_of_range(lse):
+    return jnp.where(jnp.abs(lse) < SAFE, 0.0, 1.0).max(axis=0, keepdims=True)
+
+
+def with_fallback(run):
+    flags = run(False)
+    worst = flags[0]
+    for flag in flags[1:]:
+        worst = jnp.maximum(worst, flag)
+
+    @pl.when(jnp.max(worst) > 0.0)
+    def _():
+        run(True)
 
 
 def with_ones(v, vl):
@@ -191,18 +212,29 @@
     scale = jnp.asarray(0.125, bf16)
     cols = slice(pair * LANES, (pair + 1) * LANES)
 
-    @pl.loop(0, q_ref.shape[0] // SEG, unroll=4)
-    def _(s):
-        part = pl.ds(pl.multiple_of(s * SEG, SEG), SEG)
+    def segment(part, shift):
         q, k, v = q_ref[part, cols] * scale, k_ref[part, cols], v_ref[part, cols]
         halves = [half_mask(SEG, h) for h in range(2)]
         out, lse = attend_pair(
             [q, q],
             [jnp.where(vl, k, jnp.zeros_like(k)) for vl in halves],
             [with_ones(v, vl) for vl in halves],
+            shift,
         )
         out_ref[pair, part, :] = out
         lse_ref[pair, part, :] = lse
+        return out_of_range(lse)
+
+    def run(shift):
+        segments = q_ref.shape[0] // SEG
+        if not shift:
+            return [segment(slice(i * SEG, (i + 1) * SEG), False) for i in range(segments)]
+
+        @pl.loop(0, segments)
+        def _(i):
+            segment(pl.ds(pl.multiple_of(i * SEG, SEG), SEG), True)
+
+    with_fallback(run)
 
 
 def keys_values(tile, half):
@@ -217,11 +249,18 @@
     keys, values = zip(*[keys_values(r[:count, :], half) for r in ins])
     few = count // 2
     vl = half_mask(count, half)
-    for d in range(4):
-        tile = ins[d][count : count + few, :]
-        other = swap_halves(tile.astype(f32)).astype(bf16)
-        out, lse = attend_one(jnp.concatenate([tile, other], axis=0), keys, values)
-        outs[d][...] = encode(out, lse, vl).astype(bf16)
+
+    def run(shift):
+        flags = []
+        for d in range(4):
+            tile = ins[d][count : count + few, :]
+            other = swap_halves(tile.astype(f32)).astype(bf16)
+            out, lse = attend_one(jnp.concatenate([tile, other], axis=0), keys, values, shift)
+            outs[d][...] = encode(out, lse, vl).astype(bf16)
+            flags.append(out_of_range(lse))
+        return flags
+
+    with_fallback(run)
 
 
 def far_kernel(base, mid, top, *refs):
@@ -231,16 +270,23 @@
         ([r[: 4 * mid, :] for r in gathered], base, mid // 2, 0),
         ([r[4 * mid :, :] for r in gathered], base + mid // 2, top // 2, mid),
     )
-    for tiles, q_at, few, out_at in blocks:
-        keys, values = zip(*[keys_values(t, half) for t in tiles])
-        tile = jnp.concatenate([r[q_at : q_at + few, :].astype(f32) for r in held], axis=0)
-        q = jnp.concatenate([tile, swap_halves(tile)], axis=0).astype(bf16)
-        out, lse = attend_one(q, keys, values)
-        found = encode(out, lse, half_mask(8 * few, half))
-        for part in range(2):
-            for d in range(4):
-                at, start = out_at + part * few, (part * 4 + d) * few
-                outs[d][at : at + few, :] = found[start : start + few, :].astype(bf16)
+
+    def run(shift):
+        flags = []
+        for tiles, q_at, few, out_at in blocks:
+            keys, values = zip(*[keys_values(t, half) for t in tiles])
+            tile = jnp.concatenate([r[q_at : q_at + few, :].astype(f32) for r in held], axis=0)
+            q = jnp.concatenate([tile, swap_halves(tile)], axis=0).astype(bf16)
+            out, lse = attend_one(q, keys, values, shift)
+            found = encode(out, lse, half_mask(8 * few, half))
+            for part in range(2):
+                for d in range(4):
+                    at, start = out_at + part * few, (part * 4 + d) * few
+                    outs[d][at : at + few, :] = found[start : start + few, :].astype(bf16)
+            flags.append(out_of_range(lse))
+        return flags
+
+    with_fallback(run)
 
 
 def second_kernel(rate, offs_ref, qs, ks, vs, outs_in, lses_in, *refs):
@@ -256,7 +302,7 @@
             k = ks[p, picked, :]
             keys.append(jnp.where(vl, k, jnp.zeros_like(k)).astype(bf16))
             values.append(with_ones(vs[p, picked, :], vl).astype(bf16))
-        out, lse = attend_pair(queries, keys, values)
+        out, lse = attend_pair(queries, keys, values, True)
         absorb_pairs(outs, lses, [(p, (offs.of(2 * p, 1), offs.of(2 * p + 1, 1)), out, lse)], rate)
     absorb_coded(outs, lses, [r[...] for r in near], offs, 2, rate)
 

time: 47.5 us -> 61.8 us (1.30)
  Pallas kernels: 23.3 us -> 37.6 us
    pallas_call x2, Pallas kernels: 5.76 us -> 13.6 us  [per_device(): call(lambda *refs, pair=pair: first_kernel(pair, *refs), [wide, wide], 'v...]
    pallas_call x1, Pallas kernels: 6.22 us -> 11.1 us  [per_device(): call(lambda *refs: near_kernel(near_count, *refs), [tile(near_count)] * 4...]
    pallas_call x1, Pallas kernels: 2.35 us -> 3.91 us  [per_device(): call(lambda *refs: far_kernel(near_count * 3 // 2, mid, top, *refs), [til...]
  transfers between devices with their start and end apart: 16 -> 16, of which waited for: 1 -> 1; matrix products, arithmetic and copies ran while one was open for 0% -> 0% of each run, Pallas kernels for 38% -> 52%
where the time goes in v5:
time: 61.8 us; the launch traced here: 61.7 us
  Pallas kernels  37.6 us (61%)
  starting transfers between devices  22.9 us (37%)
  waiting for transfers between devices  0.83 us (1%)
    ppermute x16, starting transfers between devices, swapped(): lax.ppermute(shard, 'seq', [(i, i ^ bits) for i in range(lax.axis_size('s...  22.9 us
    pallas_call x2, Pallas kernels, per_device(): call(lambda *refs, pair=pair: first_kernel(pair, *refs), [wide, wide], 'v...  13.6 us
    pallas_call x1, Pallas kernels, per_device(): call(lambda *refs: near_kernel(near_count, *refs), [tile(near_count)] * 4...  11.1 us
    pallas_call x1, Pallas kernels, per_device(): call(lambda *refs: far_kernel(near_count * 3 // 2, mid, top, *refs), [til...  3.91 us
    pallas_call x1, Pallas kernels, per_device(): call(lambda *refs: second_kernel(RATE1, *refs), [wide, wide], 'vvvvvvvvvv...  3.72 us
    pallas_call x1, Pallas kernels, per_device(): call(lambda *refs: pack_kernel(levels, *refs), [tile(near_count + queries...  3.06 us
    pallas_call x1, Pallas kernels, per_device(): call(lambda *refs: final_kernel(levels, *refs), [wide, wide, jax.ShapeDty...  2.13 us
  transfers between devices with their start and end apart: 16, of which 1 were waited for; matrix products, arithmetic and copies ran while one was open for 0% of the time, Pallas kernels for 52%

profile of v5, /device:TPU:0, one launch (start us, length us, event | category | flops | bytes accessed | tf_op | source)
XLA Modules:
  0.0 61.7 jit_solution(11876895856864889509)
XLA Ops:
  0.0 3.1 %shard_map.46 = (bf16[848,128]{1,0:T(8,128)(2,1)S(1)}, bf16[848,128]{1,0:T(8,128)(2,1)S(1)}, bf16[848,128]{1,0:T(8,128)(2,1)S(1)}, bf16[848,128]{1,0:T(8,128)(2,...) custom-call(s32[4,5]{1,0:T(4,128)} %bitcast.1, ...), custom_call_target="tpu_custom_call" | custom-call | bytes 5242880 | tf_op jit(solution)/shard_map/pallas_call | solution.py:372
  3.1 1.8 %collective-permute-start.6 = (bf16[160,128]{1,0:T(8,128)(2,1)S(1)}, bf16[160,128]{1,0:T(8,128)(2,1)S(1)}, u32[]{:S(2)}, u32[]{:S(2)}) collective-permute-start(bf16[160,128]{1,0:T(8,128)(2,1)S(1)} %get-tuple-element.55), channel_id=1, source_target_pairs={{0,4},{4,0},{8,12},{12,8},{16,20},{20,16},{24,28},{28,24},{32,36},... | collective-permute-start | bytes 122888 | tf_op jit(solution)/shard_map/ppermute | solution.py:348
  4.8 1.9 %collective-permute-start.7 = (bf16[160,128]{1,0:T(8,128)(2,1)S(1)}, bf16[160,128]{1,0:T(8,128)(2,1)S(1)}, u32[]{:S(2)}, u32[]{:S(2)}) collective-permute-start(bf16[160,128]{1,0:T(8,128)(2,1)S(1)} %get-tuple-element.56), channel_id=1, source_target_pairs={{0,8},{4,12},{8,0},{12,4},{16,24},{20,28},{24,16},{28,20},{32,40},... | collective-permute-start | bytes 122888 | tf_op jit(solution)/shard_map/ppermute | solution.py:348
  6.8 0.0 collective-permute-start.8
  6.8 1.6 %collective-permute-start = (bf16[848,128]{1,0:T(8,128)(2,1)S(1)}, bf16[848,128]{1,0:T(8,128)(2,1)S(1)}, u32[]{:S(2)}, u32[]{:S(2)}) collective-permute-start(bf16[848,128]{1,0:T(8,128)(2,1)S(1)} %get-tuple-element.45), channel_id=1, source_target_pairs={{0,4},{4,0},{8,12},{12,8},{16,20},{20,16},{24,28},{28,24},{32,36},... | collective-permute-start | bytes 651272 | tf_op jit(solution)/shard_map/ppermute | solution.py:348
  8.3 1.9 %collective-permute-start.1 = (bf16[848,128]{1,0:T(8,128)(2,1)S(1)}, bf16[848,128]{1,0:T(8,128)(2,1)S(1)}, u32[]{:S(2)}, u32[]{:S(2)}) collective-permute-start(bf16[848,128]{1,0:T(8,128)(2,1)S(1)} %get-tuple-element.46), channel_id=1, source_target_pairs={{0,8},{4,12},{8,0},{12,4},{16,24},{20,28},{24,16},{28,20},{32,40},... | collective-permute-start | bytes 651272 | tf_op jit(solution)/shard_map/ppermute | solution.py:348
  10.3 6.8 %shard_map.47 = (f32[2,2048,128]{2,1,0:T(8,128)S(1)}, f32[2,2048,128]{2,1,0:T(8,128)S(1)}) custom-call(bf16[2048,256]{1,0:T(8,128)(2,1)S(1)} %get-tuple-element.37.refs_0_, bf16[2048,256]{1,0:T(8,128)(2,1)S(1)} %get-tuple-element.38.refs_1_, bf16[2048,256]{1,0:T(8,128)(2,1)S(1)} %get-tuple-element.39.refs_2_), custom_call_target="tpu_custom_call" | custom-call | flops 2147483648 | bytes 4194304 | tf_op jit(solution)/shard_map/pallas_call | solution.py:389
  17.1 0.1 collective-permute-start.2
  17.3 3.1 %collective-permute-start.9 = (bf16[128,128]{1,0:T(8,128)(2,1)S(1)}, bf16[128,128]{1,0:T(8,128)(2,1)S(1)}, u32[]{:S(2)}, u32[]{:S(2)}) collective-permute-start(bf16[128,128]{1,0:T(8,128)(2,1)S(1)} %pad_maximum_fusion), channel_id=1, source_target_pairs={{0,64},{4,68},{8,72},{12,76},{16,80},{20,84},{24,88},{28,92},{32,9... | collective-permute-start | bytes 98312 | tf_op jit(solution)/shard_map/ppermute | solution.py:348
  20.4 6.8 %shard_map.48 = (f32[2,2048,128]{2,1,0:T(8,128)S(1)}, f32[2,2048,128]{2,1,0:T(8,128)S(1)}) custom-call(bf16[2048,256]{1,0:T(8,128)(2,1)S(1)} %get-tuple-element.37.refs_0_, bf16[2048,256]{1,0:T(8,128)(2,1)S(1)} %get-tuple-element.38.refs_1_, bf16[2048,256]{1,0:T(8,128)(2,1)S(1)} %get-tuple-element.39.refs_2_, ...), custom_call_target="tpu_custom_call", output_to_operand_aliasing={{0}: (3, {}), {1}: (4, {})} | custom-call | flops 2147483648 | bytes 4194304 | tf_op jit(solution)/shard_map/pallas_call | solution.py:389
  27.3 4.0 %collective-permute-start.12 = (bf16[768,128]{1,0:T(8,128)(2,1)S(1)}, bf16[768,128]{1,0:T(8,128)(2,1)S(1)}, u32[]{:S(2)}, u32[]{:S(2)}) collective-permute-start(bf16[768,128]{1,0:T(8,128)(2,1)S(1)} %constant_dynamic-update-slice_fusion.refs_4_), channel_id=1, source_target_pairs={{0,48},{4,52},{8,56},{12,60},{16,32},{20,36},{24,40},{28,44},{32,1... | collective-permute-start | bytes 589832 | tf_op jit(solution)/shard_map/ppermute | solution.py:348
  31.2 0.1 collective-permute-start.11
  31.3 1.4 %collective-permute-start.10 = (bf16[768,128]{1,0:T(8,128)(2,1)S(1)}, bf16[768,128]{1,0:T(8,128)(2,1)S(1)}, u32[]{:S(2)}, u32[]{:S(2)}) collective-permute-start(bf16[768,128]{1,0:T(8,128)(2,1)S(1)} %constant_dynamic-update-slice_fusion.refs_4_), channel_id=1, source_target_pairs={{0,32},{4,36},{8,40},{12,44},{16,48},{20,52},{24,56},{28,60},{32,0... | collective-permute-start | bytes 589832 | tf_op jit(solution)/shard_map/ppermute | solution.py:348
  32.7 11.1 %shard_map.49 = (bf16[512,128]{1,0:T(8,128)(2,1)S(1)}, bf16[512,128]{1,0:T(8,128)(2,1)S(1)}, bf16[512,128]{1,0:T(8,128)(2,1)S(1)}, bf16[512,128]{1,0:T(8,128)(2,1)S(1)}) custom-call(bf16[848,128]{1,0:T(8,128)(2,1)S(1)} %get-tuple-element.44.refs_0_, bf16[848,128]{1,0:T(8,128)(2,1)S(1)} %collective-permute-done.refs_1_, ...), custom_call_target="tpu_custom_call" | custom-call | flops 6442450944 | bytes 2097152 | tf_op jit(solution)/shard_map/pallas_call | solution.py:404
  43.8 1.7 %collective-permute-start.3 = (bf16[512,128]{1,0:T(8,128)(2,1)S(1)}, bf16[512,128]{1,0:T(8,128)(2,1)S(1)}, u32[]{:S(2)}, u32[]{:S(2)}) collective-permute-start(bf16[512,128]{1,0:T(8,128)(2,1)S(1)} %get-tuple-element.49), channel_id=1, source_target_pairs={{0,4},{4,0},{8,12},{12,8},{16,20},{20,16},{24,28},{28,24},{32,36},... | collective-permute-start | bytes 393224 | tf_op jit(solution)/shard_map/ppermute | solution.py:348
  45.4 1.6 %collective-permute-start.4 = (bf16[512,128]{1,0:T(8,128)(2,1)S(1)}, bf16[512,128]{1,0:T(8,128)(2,1)S(1)}, u32[]{:S(2)}, u32[]{:S(2)}) collective-permute-start(bf16[512,128]{1,0:T(8,128)(2,1)S(1)} %get-tuple-element.50), channel_id=1, source_target_pairs={{0,8},{4,12},{8,0},{12,4},{16,24},{20,28},{24,16},{28,20},{32,40},... | collective-permute-start | bytes 393224 | tf_op jit(solution)/shard_map/ppermute | solution.py:348
  47.0 0.3 collective-permute-start.5
  47.3 3.9 %shard_map.51 = (bf16[160,128]{1,0:T(8,128)(2,1)S(1)}, bf16[160,128]{1,0:T(8,128)(2,1)S(1)}, bf16[160,128]{1,0:T(8,128)(2,1)S(1)}, bf16[160,128]{1,0:T(8,128)(2,1)S(1)}) custom-call(bf16[848,128]{1,0:T(8,128)(2,1)S(1)} %get-tuple-element.44.refs_0_, bf16[848,128]{1,0:T(8,128)(2,1)S(1)} %collective-permute-done.refs_1_, ...), custom_call_target="tpu_custom_call" | custom-call | flops 2147483648 | bytes 2097152 | tf_op jit(solution)/shard_map/pallas_call | solution.py:414
  51.3 1.7 %collective-permute-start.13 = (bf16[160,128]{1,0:T(8,128)(2,1)S(1)}, bf16[160,128]{1,0:T(8,128)(2,1)S(1)}, u32[]{:S(2)}, u32[]{:S(2)}) collective-permute-start(bf16[160,128]{1,0:T(8,128)(2,1)S(1)} %get-tuple-element.59), channel_id=1, source_target_pairs={{0,4},{4,0},{8,12},{12,8},{16,20},{20,16},{24,28},{28,24},{32,36},... | collective-permute-start | bytes 122888 | tf_op jit(solution)/shard_map/ppermute | solution.py:348
  52.9 1.6 %collective-permute-start.14 = (bf16[160,128]{1,0:T(8,128)(2,1)S(1)}, bf16[160,128]{1,0:T(8,128)(2,1)S(1)}, u32[]{:S(2)}, u32[]{:S(2)}) collective-permute-start(bf16[160,128]{1,0:T(8,128)(2,1)S(1)} %get-tuple-element.60), channel_id=1, source_target_pairs={{0,8},{4,12},{8,0},{12,4},{16,24},{20,28},{24,16},{28,20},{32,40},... | collective-permute-start | bytes 122888 | tf_op jit(solution)/shard_map/ppermute | solution.py:348
  54.5 0.3 collective-permute-start.15
  54.9 3.7 %shard_map.50 = (f32[2,2048,128]{2,1,0:T(8,128)S(1)}, f32[2,2048,128]{2,1,0:T(8,128)S(1)}) custom-call(s32[4,5]{1,0:T(4,128)S(1)} %bitcast.2, f32[2,2048,128]{2,1,0:T(8,128)S(1)} %get-tuple-element.34.refs_1_, f32[2,2048,128]{2,1,0:T(8,128)S(1)} %get-tuple-element.35.refs_2_, ...), custom_call_target="tpu_custom_call", output_to_operand_aliasing={{0}: (4, {}), {1}: (5, {})} | custom-call | flops 2147483648 | bytes 4194304 | tf_op jit(solution)/shard_map/pallas_call | solution.py:424
  58.6 0.8 %collective-permute-done.15.refs_6_ = bf16[160,128]{1,0:T(8,128)(2,1)S(1)} collective-permute-done((bf16[160,128]{1,0:T(8,128)(2,1)S(1)}, bf16[160,128]{1,0:T(8,128)(2,1)S(1)}, u32[]{:S(2)}, u32[]{:S(2)}) %collective-permute-start.15) | collective-permute-done | bytes 40992 | tf_op jit(solution)/shard_map/ppermute | solution.py:348
  59.4 2.1 %shard_map.52 = (f32[2,2048,128]{2,1,0:T(8,128)S(1)}, f32[2,2048,128]{2,1,0:T(8,128)S(1)}, bf16[2048,256]{1,0:T(8,128)(2,1)}) custom-call(s32[4,5]{1,0:T(4,128)S(1)} %bitcast.3, f32[2,2048,128]{2,1,0:T(8,128)S(1)} %get-tuple-element.52.refs_1_, f32[2,2048,128]{2,1,0:T(8,128)S(1)} %get-tuple-element.53.refs_2_, ...), custom_call_target="tpu_custom_call", output_to_operand_aliasing={{0}: (1, {}), {1}: (2, {})} | custom-call | bytes 6291456 | tf_op jit(solution)/shard_map/pallas_call | solution.py:434
  (27 shorter events, 0.1 us)
Async XLA Ops:
  3.1 14.0 %collective-permute-start.6 = (bf16[160,128]{1,0:T(8,128)(2,1)S(1)}, bf16[160,128]{1,0:T(8,128)(2,1)S(1)}, u32[]{:S(2)}, u32[]{:S(2)}) collective-permute-start(bf16[160,128]{1,0:T(8,128)(2,1)S(1)} %get-tuple-element.55), channel_id=1, source_target_pairs={{0,4},{4,0},{8,12},{12,8},{16,20},{20,16},{24,28},{28,24},{32,36},... | collective-permute-start | bytes 122888 | tf_op jit(solution)/shard_map/ppermute | solution.py:348
  4.8 12.4 %collective-permute-start.7 = (bf16[160,128]{1,0:T(8,128)(2,1)S(1)}, bf16[160,128]{1,0:T(8,128)(2,1)S(1)}, u32[]{:S(2)}, u32[]{:S(2)}) collective-permute-start(bf16[160,128]{1,0:T(8,128)(2,1)S(1)} %get-tuple-element.56), channel_id=1, source_target_pairs={{0,8},{4,12},{8,0},{12,4},{16,24},{20,28},{24,16},{28,20},{32,40},... | collective-permute-start | bytes 122888 | tf_op jit(solution)/shard_map/ppermute | solution.py:348
  6.8 10.5 %collective-permute-start.8 = (bf16[160,128]{1,0:T(8,128)(2,1)S(1)}, bf16[160,128]{1,0:T(8,128)(2,1)S(1)}, u32[]{:S(2)}, u32[]{:S(2)}) collective-permute-start(bf16[160,128]{1,0:T(8,128)(2,1)S(1)} %get-tuple-element.57), channel_id=1, source_target_pairs={{0,12},{4,8},{8,4},{12,0},{16,28},{20,24},{24,20},{28,16},{32,44},... | collective-permute-start | bytes 122888 | tf_op jit(solution)/shard_map/ppermute | solution.py:348
  6.8 24.5 %collective-permute-start = (bf16[848,128]{1,0:T(8,128)(2,1)S(1)}, bf16[848,128]{1,0:T(8,128)(2,1)S(1)}, u32[]{:S(2)}, u32[]{:S(2)}) collective-permute-start(bf16[848,128]{1,0:T(8,128)(2,1)S(1)} %get-tuple-element.45), channel_id=1, source_target_pairs={{0,4},{4,0},{8,12},{12,8},{16,20},{20,16},{24,28},{28,24},{32,36},... | collective-permute-start | bytes 651272 | tf_op jit(solution)/shard_map/ppermute | solution.py:348
  8.3 24.3 %collective-permute-start.1 = (bf16[848,128]{1,0:T(8,128)(2,1)S(1)}, bf16[848,128]{1,0:T(8,128)(2,1)S(1)}, u32[]{:S(2)}, u32[]{:S(2)}) collective-permute-start(bf16[848,128]{1,0:T(8,128)(2,1)S(1)} %get-tuple-element.46), channel_id=1, source_target_pairs={{0,8},{4,12},{8,0},{12,4},{16,24},{20,28},{24,16},{28,20},{32,40},... | collective-permute-start | bytes 651272 | tf_op jit(solution)/shard_map/ppermute | solution.py:348
  17.1 15.6 %collective-permute-start.2 = (bf16[848,128]{1,0:T(8,128)(2,1)S(1)}, bf16[848,128]{1,0:T(8,128)(2,1)S(1)}, u32[]{:S(2)}, u32[]{:S(2)}) collective-permute-start(bf16[848,128]{1,0:T(8,128)(2,1)S(1)} %get-tuple-element.47), channel_id=1, source_target_pairs={{0,12},{4,8},{8,4},{12,0},{16,28},{20,24},{24,20},{28,16},{32,44},... | collective-permute-start | bytes 651272 | tf_op jit(solution)/shard_map/ppermute | solution.py:348
  17.3 9.9 %collective-permute-start.9 = (bf16[128,128]{1,0:T(8,128)(2,1)S(1)}, bf16[128,128]{1,0:T(8,128)(2,1)S(1)}, u32[]{:S(2)}, u32[]{:S(2)}) collective-permute-start(bf16[128,128]{1,0:T(8,128)(2,1)S(1)} %pad_maximum_fusion), channel_id=1, source_target_pairs={{0,64},{4,68},{8,72},{12,76},{16,80},{20,84},{24,88},{28,92},{32,9... | collective-permute-start | bytes 98312 | tf_op jit(solution)/shard_map/ppermute | solution.py:348
  27.3 19.7 %collective-permute-start.12 = (bf16[768,128]{1,0:T(8,128)(2,1)S(1)}, bf16[768,128]{1,0:T(8,128)(2,1)S(1)}, u32[]{:S(2)}, u32[]{:S(2)}) collective-permute-start(bf16[768,128]{1,0:T(8,128)(2,1)S(1)} %constant_dynamic-update-slice_fusion.refs_4_), channel_id=1, source_target_pairs={{0,48},{4,52},{8,56},{12,60},{16,32},{20,36},{24,40},{28,44},{32,1... | collective-permute-start | bytes 589832 | tf_op jit(solution)/shard_map/ppermute | solution.py:348
  31.2 16.1 %collective-permute-start.11 = (bf16[768,128]{1,0:T(8,128)(2,1)S(1)}, bf16[768,128]{1,0:T(8,128)(2,1)S(1)}, u32[]{:S(2)}, u32[]{:S(2)}) collective-permute-start(bf16[768,128]{1,0:T(8,128)(2,1)S(1)} %constant_dynamic-update-slice_fusion.refs_4_), channel_id=1, source_target_pairs={{0,16},{4,20},{8,24},{12,28},{16,0},{20,4},{24,8},{28,12},{32,48},... | collective-permute-start | bytes 589832 | tf_op jit(solution)/shard_map/ppermute | solution.py:348
  31.3 16.1 %collective-permute-start.10 = (bf16[768,128]{1,0:T(8,128)(2,1)S(1)}, bf16[768,128]{1,0:T(8,128)(2,1)S(1)}, u32[]{:S(2)}, u32[]{:S(2)}) collective-permute-start(bf16[768,128]{1,0:T(8,128)(2,1)S(1)} %constant_dynamic-update-slice_fusion.refs_4_), channel_id=1, source_target_pairs={{0,32},{4,36},{8,40},{12,44},{16,48},{20,52},{24,56},{28,60},{32,0... | collective-permute-start | bytes 589832 | tf_op jit(solution)/shard_map/ppermute | solution.py:348
  43.8 10.7 %collective-permute-start.3 = (bf16[512,128]{1,0:T(8,128)(2,1)S(1)}, bf16[512,128]{1,0:T(8,128)(2,1)S(1)}, u32[]{:S(2)}, u32[]{:S(2)}) collective-permute-start(bf16[512,128]{1,0:T(8,128)(2,1)S(1)} %get-tuple-element.49), channel_id=1, source_target_pairs={{0,4},{4,0},{8,12},{12,8},{16,20},{20,16},{24,28},{28,24},{32,36},... | collective-permute-start | bytes 393224 | tf_op jit(solution)/shard_map/ppermute | solution.py:348
  45.4 9.4 %collective-permute-start.4 = (bf16[512,128]{1,0:T(8,128)(2,1)S(1)}, bf16[512,128]{1,0:T(8,128)(2,1)S(1)}, u32[]{:S(2)}, u32[]{:S(2)}) collective-permute-start(bf16[512,128]{1,0:T(8,128)(2,1)S(1)} %get-tuple-element.50), channel_id=1, source_target_pairs={{0,8},{4,12},{8,0},{12,4},{16,24},{20,28},{24,16},{28,20},{32,40},... | collective-permute-start | bytes 393224 | tf_op jit(solution)/shard_map/ppermute | solution.py:348
  47.0 7.9 %copy-start = (s32[5,4]{0,1:T(4,128)S(1)}, s32[5,4]{0,1:T(4,128)}, u32[]{:S(2)}) copy-start(s32[5,4]{0,1:T(4,128)} %param.7) | copy-start | bytes 244
  47.0 7.8 %collective-permute-start.5 = (bf16[512,128]{1,0:T(8,128)(2,1)S(1)}, bf16[512,128]{1,0:T(8,128)(2,1)S(1)}, u32[]{:S(2)}, u32[]{:S(2)}) collective-permute-start(bf16[512,128]{1,0:T(8,128)(2,1)S(1)} %get-tuple-element.51), channel_id=1, source_target_pairs={{0,12},{4,8},{8,4},{12,0},{16,28},{20,24},{24,20},{28,16},{32,44},... | collective-permute-start | bytes 393224 | tf_op jit(solution)/shard_map/ppermute | solution.py:348
  51.3 7.3 %collective-permute-start.13 = (bf16[160,128]{1,0:T(8,128)(2,1)S(1)}, bf16[160,128]{1,0:T(8,128)(2,1)S(1)}, u32[]{:S(2)}, u32[]{:S(2)}) collective-permute-start(bf16[160,128]{1,0:T(8,128)(2,1)S(1)} %get-tuple-element.59), channel_id=1, source_target_pairs={{0,4},{4,0},{8,12},{12,8},{16,20},{20,16},{24,28},{28,24},{32,36},... | collective-permute-start | bytes 122888 | tf_op jit(solution)/shard_map/ppermute | solution.py:348
  52.9 5.7 %collective-permute-start.14 = (bf16[160,128]{1,0:T(8,128)(2,1)S(1)}, bf16[160,128]{1,0:T(8,128)(2,1)S(1)}, u32[]{:S(2)}, u32[]{:S(2)}) collective-permute-start(bf16[160,128]{1,0:T(8,128)(2,1)S(1)} %get-tuple-element.60), channel_id=1, source_target_pairs={{0,8},{4,12},{8,0},{12,4},{16,24},{20,28},{24,16},{28,20},{32,40},... | collective-permute-start | bytes 122888 | tf_op jit(solution)/shard_map/ppermute | solution.py:348
  54.5 4.9 %collective-permute-start.15 = (bf16[160,128]{1,0:T(8,128)(2,1)S(1)}, bf16[160,128]{1,0:T(8,128)(2,1)S(1)}, u32[]{:S(2)}, u32[]{:S(2)}) collective-permute-start(bf16[160,128]{1,0:T(8,128)(2,1)S(1)} %get-tuple-element.61), channel_id=1, source_target_pairs={{0,12},{4,8},{8,4},{12,0},{16,28},{20,24},{24,20},{28,16},{32,44},... | collective-permute-start | bytes 122888 | tf_op jit(solution)/shard_map/ppermute | solution.py:348

commit v6 on v5

--- a/solution.py
+++ b/solution.py
@@ -10,6 +10,7 @@
 PACK_MIB = 24
 RATE1 = 4
 SAFE = 46.0
+FAR = (0, 1, 8, 9)
 bf16 = jnp.bfloat16
 f32 = jnp.float32
 LANES = 128
@@ -132,8 +133,7 @@
         lses[pair, spots[1], :] = jnp.where(low, lses[pair, spots[1], :], lse)
 
 
-def absorb_coded(outs, lses, coded, offs, level, rate):
-    mine = lax.rem(lax.axis_index("seq"), 4)
+def absorb_coded(outs, lses, coded, offs, level, rate, mine):
     items = []
     for j in range(2):
         pair = lax.div(mine, 2) ^ j
@@ -172,39 +172,52 @@
     return copy
 
 
+def near_place():
+    return lax.rem(lax.axis_index("seq"), 4)
+
+
+def far_place():
+    index = lax.axis_index("seq")
+    return lax.rem(index, 2) + 2 * lax.rem(lax.div(index, 8), 2)
+
+
 def pack_kernel(levels, offs_any, q_any, k_any, v_any, *rest):
     near_out, far_out, (qb, kb, vb, qs, ks, vs, offs, sems) = rest[0:4], rest[4:8], rest[8:]
-    mine = lax.rem(lax.axis_index("seq"), 4)
-    copies = [fetch(k_any, kb, sems.at[0]), fetch(v_any, vb, sems.at[1])]
-    copies += [fetch(q_any, qb, sems.at[2]), fetch(offs_any, offs, sems.at[3])]
-    for copy, narrow, wide in zip(copies, (kb, vb, qb), (ks, vs, qs)):
-        copy.wait()
-        widen(narrow, wide)
+    copies = [fetch(offs_any, offs, sems.at[3]), fetch(k_any, kb, sems.at[0])]
+    copies += [fetch(v_any, vb, sems.at[1]), fetch(q_any, qb, sems.at[2])]
+    copies[1].wait()
+    widen(kb, ks)
+    copies[2].wait()
+    widen(vb, vs)
+    copies[0].wait()
+    groups = ((far_place(), far_out, levels[1:]), (near_place(), near_out, levels[:1]))
+    ends = []
+    for mine, outs, group in groups:
+        for d in range(4):
+            head = mine ^ d
+            pair, half = lax.div(head, 2), lax.rem(head, 2)
+            at = 0
+            for level, count, rate in group:
+                picked = pl.ds(offs[head, level], count, rate)
+                vl = half_mask(count, half)
+                tile = jnp.where(vl, vs[pair, picked, :], swap_halves(ks[pair, picked, :]))
+                outs[d][at : at + count, :] = tile.astype(bf16)
+                at += count
+            ends.append(at)
     copies[3].wait()
-    for d in range(4):
-        head = mine ^ d
-        pair, half = lax.div(head, 2), lax.rem(head, 2)
-        base = [0, 0]
-        for what in ("kv", "q"):
-            for level, count, rate, near in levels:
-                off = offs[head, level]
-                near = near or what == "q"
-                ref = near_out[d] if near else far_out[d]
-                at = base[near]
-                if what == "kv":
-                    vl = half_mask(count, half)
-                    k = ks[pair, pl.ds(off, count, rate), :]
-                    v = vs[pair, pl.ds(off, count, rate), :]
-                    ref[at : at + count, :] = jnp.where(vl, v, swap_halves(k)).astype(bf16)
-                    base[near] = at + count
-                else:
-                    few = count // 2
-                    vl = half_mask(few, half)
-                    q_one = qs[pair, pl.ds(off, few, rate), :]
-                    q_two = qs[pair, pl.ds(off + few * rate, few, rate), :]
-                    tile = jnp.where(vl, q_two, swap_halves(q_one))
-                    ref[at : at + few, :] = (tile * 0.125).astype(bf16)
-                    base[near] = at + few
+    widen(qb, qs)
+    for (mine, outs, group), end in zip(groups, ends[::4]):
+        for d in range(4):
+            head = mine ^ d
+            pair, half = lax.div(head, 2), lax.rem(head, 2)
+            at = end
+            for level, count, rate in group:
+                off, few = offs[head, level], count // 2
+                q_one = qs[pair, pl.ds(off, few, rate), :]
+                q_two = qs[pair, pl.ds(off + few * rate, few, rate), :]
+                tile = jnp.where(half_mask(few, half), q_two, swap_halves(q_one))
+                outs[d][at : at + few, :] = (tile * 0.125).astype(bf16)
+                at += few
 
 
 def first_kernel(pair, q_ref, k_ref, v_ref, *rest):
@@ -304,7 +317,7 @@
             values.append(with_ones(vs[p, picked, :], vl).astype(bf16))
         out, lse = attend_pair(queries, keys, values, True)
         absorb_pairs(outs, lses, [(p, (offs.of(2 * p, 1), offs.of(2 * p + 1, 1)), out, lse)], rate)
-    absorb_coded(outs, lses, [r[...] for r in near], offs, 2, rate)
+    absorb_coded(outs, lses, [r[...] for r in near], offs, 2, rate, near_place())
 
 
 def final_kernel(levels, offs_ref, outs_in, lses_in, *refs):
@@ -312,10 +325,10 @@
     out, sems = refs[7:]
     offs = Table(offs_ref)
     at = 0
-    for level, count, rate, near in levels:
-        if not near:
-            absorb_coded(outs, lses, [r[at : at + count, :] for r in far], offs, level, rate)
-            at += count
+    for level, count, rate in levels[1:]:
+        coded = [r[at : at + count, :] for r in far]
+        absorb_coded(outs, lses, coded, offs, level, rate, far_place())
+        at += count
     copies = []
     for i in range(out.shape[0] // SEG):
         part = slice(i * SEG, (i + 1) * SEG)
@@ -357,11 +370,10 @@
     rate_four = 4 * rate_three
     near_count, mid, top = rows // RATE1, rows // rate_three, rows // rate_four
     levels = (
-        (2, near_count, RATE1, True),
-        (3, mid, rate_three, False),
-        (4, top, rate_four, False),
-    )
-    queries = (near_count + mid + top) // 2
+        (2, near_count, RATE1),
+        (3, mid, rate_three),
+        (4, top, rate_four),
+    )
     offsets = offsets.T
     table = pltpu.SMEM(offsets.shape, jnp.int32)
 
@@ -371,8 +383,8 @@
     wide = jax.ShapeDtypeStruct((2, rows, LANES), f32)
     parts = call(
         lambda *refs: pack_kernel(levels, *refs),
-        [tile(near_count + queries)] * 4
-        + [tile(mid + top)] * 4
+        [tile(near_count * 3 // 2)] * 4
+        + [tile((mid + top) * 3 // 2)] * 4
         + [jax.ShapeDtypeStruct(query.shape, bf16)] * 3
         + [wide] * 3,
         "aaaa",
@@ -381,7 +393,7 @@
         mib=PACK_MIB,
     )(*(pltpu.with_memory_space_constraint(x, pltpu.HBM) for x in (offsets, query, key, value)))
     near_sent, far_sent, narrow, wides = parts[:4], parts[4:8], parts[8:11], parts[11:]
-    far_held = [far_sent[0]] + [swapped(far_sent[d], d) for d in (1, 2, 3)]
+    far_held = [far_sent[0]] + [swapped(far_sent[d], FAR[d]) for d in (1, 2, 3)]
     near_held = [near_sent[0]] + [swapped(near_sent[d], d) for d in (1, 2, 3)]
 
     state = ()
@@ -399,7 +411,7 @@
     own_top = jnp.concatenate([r[mid : mid + top] for r in far_held], axis=0)
     other_top = swapped(own_top, 16)
     held = jnp.concatenate([r[:mid] for r in far_held] + [own_top, other_top], axis=0)
-    gathered = [held] + [swapped(held, b) for b in (8, 4, 12)]
+    gathered = [held] + [swapped(held, b) for b in (2, 6, 4)]
 
     near_found = call(
         lambda *refs: near_kernel(near_count, *refs),
@@ -412,14 +424,14 @@
     near_back = [near_found[0]] + [swapped(near_found[d], d) for d in (1, 2, 3)]
 
     far_found = call(
-        lambda *refs: far_kernel(near_count * 3 // 2, mid, top, *refs),
+        lambda *refs: far_kernel(mid + top, mid, top, *refs),
         [tile(mid + top)] * 4,
         "v" * 8,
         flops=2 << 30,
         bytes_moved=2 << 20,
         exps=1 << 20,
-    )(*near_held, *gathered)
-    far_back = [far_found[0]] + [swapped(far_found[d], d) for d in (1, 2, 3)]
+    )(*far_held, *gathered)
+    far_back = [far_found[0]] + [swapped(far_found[d], FAR[d]) for d in (1, 2, 3)]
 
     state = call(
         lambda *refs: second_kernel(RATE1, *refs),

time: 61.8 us -> 60.5 us (0.979)
  waiting for transfers between devices: 0.83 us -> 0.04 us
    ppermute x16, waiting for transfers between devices: 0.83 us -> 0.04 us  [swapped(): lax.ppermute(shard, 'seq', [(i, i ^ bits) for i in range(lax.axis_size('s...]
  transfers between devices with their start and end apart: 16 -> 16, of which waited for: 1 -> 0; matrix products, arithmetic and copies ran while one was open for 0% -> 0% of each run, Pallas kernels for 52% -> 54%
where the time goes in v6:
time: 60.5 us; the launch traced here: 60.4 us
  Pallas kernels  37.5 us (62%)
  starting transfers between devices  22.4 us (37%)
    ppermute x16, starting transfers between devices, swapped(): lax.ppermute(shard, 'seq', [(i, i ^ bits) for i in range(lax.axis_size('s...  22.4 us
    pallas_call x2, Pallas kernels, per_device(): call(lambda *refs, pair=pair: first_kernel(pair, *refs), [wide, wide], 'v...  13.6 us
    pallas_call x1, Pallas kernels, per_device(): call(lambda *refs: near_kernel(near_count, *refs), [tile(near_count)] * 4...  11.1 us
    pallas_call x1, Pallas kernels, per_device(): call(lambda *refs: far_kernel(mid + top, mid, top, *refs), [tile(mid + to...  3.92 us
    pallas_call x1, Pallas kernels, per_device(): call(lambda *refs: second_kernel(RATE1, *refs), [wide, wide], 'vvvvvvvvvv...  3.72 us
    pallas_call x1, Pallas kernels, per_device(): call(lambda *refs: pack_kernel(levels, *refs), [tile(near_count * 3 // 2)...  2.96 us
    pallas_call x1, Pallas kernels, per_device(): call(lambda *refs: final_kernel(levels, *refs), [wide, wide, jax.ShapeDty...  2.14 us
  transfers between devices with their start and end apart: 16, of which 0 were waited for; matrix products, arithmetic and copies ran while one was open for 0% of the time, Pallas kernels for 54%

profile of v6, /device:TPU:0, one launch (start us, length us, event | category | flops | bytes accessed | tf_op | source)
XLA Modules:
  0.0 60.4 jit_solution(18038593076789269337)
XLA Ops:
  0.0 3.0 %shard_map.46 = (bf16[768,128]{1,0:T(8,128)(2,1)S(1)}, bf16[768,128]{1,0:T(8,128)(2,1)S(1)}, bf16[768,128]{1,0:T(8,128)(2,1)S(1)}, bf16[768,128]{1,0:T(8,128)(2,...) custom-call(s32[4,5]{1,0:T(4,128)} %bitcast.1, ...), custom_call_target="tpu_custom_call" | custom-call | bytes 5242880 | tf_op jit(solution)/shard_map/pallas_call | solution.py:384
  3.0 1.8 %collective-permute-start.6 = (bf16[240,128]{1,0:T(8,128)(2,1)S(1)}, bf16[240,128]{1,0:T(8,128)(2,1)S(1)}, u32[]{:S(2)}, u32[]{:S(2)}) collective-permute-start(bf16[240,128]{1,0:T(8,128)(2,1)S(1)} %get-tuple-element.55), channel_id=1, source_target_pairs={{0,4},{4,0},{8,12},{12,8},{16,20},{20,16},{24,28},{28,24},{32,36},... | collective-permute-start | bytes 184328 | tf_op jit(solution)/shard_map/ppermute | solution.py:361
  4.7 1.5 %collective-permute-start.7 = (bf16[240,128]{1,0:T(8,128)(2,1)S(1)}, bf16[240,128]{1,0:T(8,128)(2,1)S(1)}, u32[]{:S(2)}, u32[]{:S(2)}) collective-permute-start(bf16[240,128]{1,0:T(8,128)(2,1)S(1)} %get-tuple-element.56), channel_id=1, source_target_pairs={{0,32},{4,36},{8,40},{12,44},{16,48},{20,52},{24,56},{28,60},{32,0... | collective-permute-start | bytes 184328 | tf_op jit(solution)/shard_map/ppermute | solution.py:361
  6.2 0.3 collective-permute-start.8
  6.5 1.7 %collective-permute-start = (bf16[768,128]{1,0:T(8,128)(2,1)S(1)}, bf16[768,128]{1,0:T(8,128)(2,1)S(1)}, u32[]{:S(2)}, u32[]{:S(2)}) collective-permute-start(bf16[768,128]{1,0:T(8,128)(2,1)S(1)} %get-tuple-element.45), channel_id=1, source_target_pairs={{0,4},{4,0},{8,12},{12,8},{16,20},{20,16},{24,28},{28,24},{32,36},... | collective-permute-start | bytes 589832 | tf_op jit(solution)/shard_map/ppermute | solution.py:361
  8.2 1.9 %collective-permute-start.1 = (bf16[768,128]{1,0:T(8,128)(2,1)S(1)}, bf16[768,128]{1,0:T(8,128)(2,1)S(1)}, u32[]{:S(2)}, u32[]{:S(2)}) collective-permute-start(bf16[768,128]{1,0:T(8,128)(2,1)S(1)} %get-tuple-element.46), channel_id=1, source_target_pairs={{0,8},{4,12},{8,0},{12,4},{16,24},{20,28},{24,16},{28,20},{32,40},... | collective-permute-start | bytes 589832 | tf_op jit(solution)/shard_map/ppermute | solution.py:361
  10.1 6.8 %shard_map.47 = (f32[2,2048,128]{2,1,0:T(8,128)S(1)}, f32[2,2048,128]{2,1,0:T(8,128)S(1)}) custom-call(bf16[2048,256]{1,0:T(8,128)(2,1)S(1)} %get-tuple-element.37.refs_0_, bf16[2048,256]{1,0:T(8,128)(2,1)S(1)} %get-tuple-element.38.refs_1_, bf16[2048,256]{1,0:T(8,128)(2,1)S(1)} %get-tuple-element.39.refs_2_), custom_call_target="tpu_custom_call" | custom-call | flops 2147483648 | bytes 4194304 | tf_op jit(solution)/shard_map/pallas_call | solution.py:401
  17.0 0.0 collective-permute-done.6.refs_1_
  17.0 0.1 collective-permute-start.2
  17.2 3.1 %collective-permute-start.9 = (bf16[128,128]{1,0:T(8,128)(2,1)S(1)}, bf16[128,128]{1,0:T(8,128)(2,1)S(1)}, u32[]{:S(2)}, u32[]{:S(2)}) collective-permute-start(bf16[128,128]{1,0:T(8,128)(2,1)S(1)} %pad_maximum_fusion), channel_id=1, source_target_pairs={{0,64},{4,68},{8,72},{12,76},{16,80},{20,84},{24,88},{28,92},{32,9... | collective-permute-start | bytes 98312 | tf_op jit(solution)/shard_map/ppermute | solution.py:361
  20.3 6.8 %shard_map.48 = (f32[2,2048,128]{2,1,0:T(8,128)S(1)}, f32[2,2048,128]{2,1,0:T(8,128)S(1)}) custom-call(bf16[2048,256]{1,0:T(8,128)(2,1)S(1)} %get-tuple-element.37.refs_0_, bf16[2048,256]{1,0:T(8,128)(2,1)S(1)} %get-tuple-element.38.refs_1_, bf16[2048,256]{1,0:T(8,128)(2,1)S(1)} %get-tuple-element.39.refs_2_, ...), custom_call_target="tpu_custom_call", output_to_operand_aliasing={{0}: (3, {}), {1}: (4, {})} | custom-call | flops 2147483648 | bytes 4194304 | tf_op jit(solution)/shard_map/pallas_call | solution.py:401
  27.2 3.9 %collective-permute-start.12 = (bf16[768,128]{1,0:T(8,128)(2,1)S(1)}, bf16[768,128]{1,0:T(8,128)(2,1)S(1)}, u32[]{:S(2)}, u32[]{:S(2)}) collective-permute-start(bf16[768,128]{1,0:T(8,128)(2,1)S(1)} %constant_dynamic-update-slice_fusion.refs_4_), channel_id=1, source_target_pairs={{0,16},{4,20},{8,24},{12,28},{16,0},{20,4},{24,8},{28,12},{32,48},... | collective-permute-start | bytes 589832 | tf_op jit(solution)/shard_map/ppermute | solution.py:361
  31.1 0.7 %collective-permute-start.11 = (bf16[768,128]{1,0:T(8,128)(2,1)S(1)}, bf16[768,128]{1,0:T(8,128)(2,1)S(1)}, u32[]{:S(2)}, u32[]{:S(2)}) collective-permute-start(bf16[768,128]{1,0:T(8,128)(2,1)S(1)} %constant_dynamic-update-slice_fusion.refs_4_), channel_id=1, source_target_pairs={{0,24},{4,28},{8,16},{12,20},{16,8},{20,12},{24,0},{28,4},{32,56},... | collective-permute-start | bytes 589832 | tf_op jit(solution)/shard_map/ppermute | solution.py:361
  31.8 0.3 collective-permute-start.10
  32.1 11.1 %shard_map.49 = (bf16[512,128]{1,0:T(8,128)(2,1)S(1)}, bf16[512,128]{1,0:T(8,128)(2,1)S(1)}, bf16[512,128]{1,0:T(8,128)(2,1)S(1)}, bf16[512,128]{1,0:T(8,128)(2,1)S(1)}) custom-call(bf16[768,128]{1,0:T(8,128)(2,1)S(1)} %get-tuple-element.44.refs_0_, bf16[768,128]{1,0:T(8,128)(2,1)S(1)} %collective-permute-done.refs_1_, ...), custom_call_target="tpu_custom_call" | custom-call | flops 6442450944 | bytes 2097152 | tf_op jit(solution)/shard_map/pallas_call | solution.py:416
  43.2 1.7 %collective-permute-start.3 = (bf16[512,128]{1,0:T(8,128)(2,1)S(1)}, bf16[512,128]{1,0:T(8,128)(2,1)S(1)}, u32[]{:S(2)}, u32[]{:S(2)}) collective-permute-start(bf16[512,128]{1,0:T(8,128)(2,1)S(1)} %get-tuple-element.49), channel_id=1, source_target_pairs={{0,4},{4,0},{8,12},{12,8},{16,20},{20,16},{24,28},{28,24},{32,36},... | collective-permute-start | bytes 393224 | tf_op jit(solution)/shard_map/ppermute | solution.py:361
  44.9 1.7 %collective-permute-start.4 = (bf16[512,128]{1,0:T(8,128)(2,1)S(1)}, bf16[512,128]{1,0:T(8,128)(2,1)S(1)}, u32[]{:S(2)}, u32[]{:S(2)}) collective-permute-start(bf16[512,128]{1,0:T(8,128)(2,1)S(1)} %get-tuple-element.50), channel_id=1, source_target_pairs={{0,8},{4,12},{8,0},{12,4},{16,24},{20,28},{24,16},{28,20},{32,40},... | collective-permute-start | bytes 393224 | tf_op jit(solution)/shard_map/ppermute | solution.py:361
  46.6 0.2 collective-permute-start.5
  46.8 3.9 %shard_map.51 = (bf16[160,128]{1,0:T(8,128)(2,1)S(1)}, bf16[160,128]{1,0:T(8,128)(2,1)S(1)}, bf16[160,128]{1,0:T(8,128)(2,1)S(1)}, bf16[160,128]{1,0:T(8,128)(2,1)S(1)}) custom-call(bf16[240,128]{1,0:T(8,128)(2,1)S(1)} %get-tuple-element.54.refs_0_, bf16[240,128]{1,0:T(8,128)(2,1)S(1)} %collective-permute-done.6.refs_1_, ...), custom_call_target="tpu_custom_call" | custom-call | flops 2147483648 | bytes 2097152 | tf_op jit(solution)/shard_map/pallas_call | solution.py:426
  50.7 1.7 %collective-permute-start.13 = (bf16[160,128]{1,0:T(8,128)(2,1)S(1)}, bf16[160,128]{1,0:T(8,128)(2,1)S(1)}, u32[]{:S(2)}, u32[]{:S(2)}) collective-permute-start(bf16[160,128]{1,0:T(8,128)(2,1)S(1)} %get-tuple-element.59), channel_id=1, source_target_pairs={{0,4},{4,0},{8,12},{12,8},{16,20},{20,16},{24,28},{28,24},{32,36},... | collective-permute-start | bytes 122888 | tf_op jit(solution)/shard_map/ppermute | solution.py:361
  52.4 0.6 collective-permute-start.14
  53.0 1.3 %collective-permute-start.15 = (bf16[160,128]{1,0:T(8,128)(2,1)S(1)}, bf16[160,128]{1,0:T(8,128)(2,1)S(1)}, u32[]{:S(2)}, u32[]{:S(2)}) collective-permute-start(bf16[160,128]{1,0:T(8,128)(2,1)S(1)} %get-tuple-element.61), channel_id=1, source_target_pairs={{0,36},{4,32},{8,44},{12,40},{16,52},{20,48},{24,60},{28,56},{32,4... | collective-permute-start | bytes 122888 | tf_op jit(solution)/shard_map/ppermute | solution.py:361
  54.3 3.7 %shard_map.50 = (f32[2,2048,128]{2,1,0:T(8,128)S(1)}, f32[2,2048,128]{2,1,0:T(8,128)S(1)}) custom-call(s32[4,5]{1,0:T(4,128)S(1)} %bitcast.2, f32[2,2048,128]{2,1,0:T(8,128)S(1)} %get-tuple-element.34.refs_1_, f32[2,2048,128]{2,1,0:T(8,128)S(1)} %get-tuple-element.35.refs_2_, ...), custom_call_target="tpu_custom_call", output_to_operand_aliasing={{0}: (4, {}), {1}: (5, {})} | custom-call | flops 2147483648 | bytes 4194304 | tf_op jit(solution)/shard_map/pallas_call | solution.py:436
  58.1 2.1 %shard_map.52 = (f32[2,2048,128]{2,1,0:T(8,128)S(1)}, f32[2,2048,128]{2,1,0:T(8,128)S(1)}, bf16[2048,256]{1,0:T(8,128)(2,1)}) custom-call(s32[4,5]{1,0:T(4,128)S(1)} %bitcast.3, f32[2,2048,128]{2,1,0:T(8,128)S(1)} %get-tuple-element.52.refs_1_, f32[2,2048,128]{2,1,0:T(8,128)S(1)} %get-tuple-element.53.refs_2_, ...), custom_call_target="tpu_custom_call", output_to_operand_aliasing={{0}: (1, {}), {1}: (2, {})} | custom-call | bytes 6291456 | tf_op jit(solution)/shard_map/pallas_call | solution.py:446
  (27 shorter events, 0.1 us)
Async XLA Ops:
  3.0 14.0 %collective-permute-start.6 = (bf16[240,128]{1,0:T(8,128)(2,1)S(1)}, bf16[240,128]{1,0:T(8,128)(2,1)S(1)}, u32[]{:S(2)}, u32[]{:S(2)}) collective-permute-start(bf16[240,128]{1,0:T(8,128)(2,1)S(1)} %get-tuple-element.55), channel_id=1, source_target_pairs={{0,4},{4,0},{8,12},{12,8},{16,20},{20,16},{24,28},{28,24},{32,36},... | collective-permute-start | bytes 184328 | tf_op jit(solution)/shard_map/ppermute | solution.py:361
  4.7 12.4 %collective-permute-start.7 = (bf16[240,128]{1,0:T(8,128)(2,1)S(1)}, bf16[240,128]{1,0:T(8,128)(2,1)S(1)}, u32[]{:S(2)}, u32[]{:S(2)}) collective-permute-start(bf16[240,128]{1,0:T(8,128)(2,1)S(1)} %get-tuple-element.56), channel_id=1, source_target_pairs={{0,32},{4,36},{8,40},{12,44},{16,48},{20,52},{24,56},{28,60},{32,0... | collective-permute-start | bytes 184328 | tf_op jit(solution)/shard_map/ppermute | solution.py:361
  6.2 10.9 %collective-permute-start.8 = (bf16[240,128]{1,0:T(8,128)(2,1)S(1)}, bf16[240,128]{1,0:T(8,128)(2,1)S(1)}, u32[]{:S(2)}, u32[]{:S(2)}) collective-permute-start(bf16[240,128]{1,0:T(8,128)(2,1)S(1)} %get-tuple-element.57), channel_id=1, source_target_pairs={{0,36},{4,32},{8,44},{12,40},{16,52},{20,48},{24,60},{28,56},{32,4... | collective-permute-start | bytes 184328 | tf_op jit(solution)/shard_map/ppermute | solution.py:361
  6.5 25.3 %collective-permute-start = (bf16[768,128]{1,0:T(8,128)(2,1)S(1)}, bf16[768,128]{1,0:T(8,128)(2,1)S(1)}, u32[]{:S(2)}, u32[]{:S(2)}) collective-permute-start(bf16[768,128]{1,0:T(8,128)(2,1)S(1)} %get-tuple-element.45), channel_id=1, source_target_pairs={{0,4},{4,0},{8,12},{12,8},{16,20},{20,16},{24,28},{28,24},{32,36},... | collective-permute-start | bytes 589832 | tf_op jit(solution)/shard_map/ppermute | solution.py:361
  8.2 23.9 %collective-permute-start.1 = (bf16[768,128]{1,0:T(8,128)(2,1)S(1)}, bf16[768,128]{1,0:T(8,128)(2,1)S(1)}, u32[]{:S(2)}, u32[]{:S(2)}) collective-permute-start(bf16[768,128]{1,0:T(8,128)(2,1)S(1)} %get-tuple-element.46), channel_id=1, source_target_pairs={{0,8},{4,12},{8,0},{12,4},{16,24},{20,28},{24,16},{28,20},{32,40},... | collective-permute-start | bytes 589832 | tf_op jit(solution)/shard_map/ppermute | solution.py:361
  17.0 15.1 %collective-permute-start.2 = (bf16[768,128]{1,0:T(8,128)(2,1)S(1)}, bf16[768,128]{1,0:T(8,128)(2,1)S(1)}, u32[]{:S(2)}, u32[]{:S(2)}) collective-permute-start(bf16[768,128]{1,0:T(8,128)(2,1)S(1)} %get-tuple-element.47), channel_id=1, source_target_pairs={{0,12},{4,8},{8,4},{12,0},{16,28},{20,24},{24,20},{28,16},{32,44},... | collective-permute-start | bytes 589832 | tf_op jit(solution)/shard_map/ppermute | solution.py:361
  17.2 9.9 %collective-permute-start.9 = (bf16[128,128]{1,0:T(8,128)(2,1)S(1)}, bf16[128,128]{1,0:T(8,128)(2,1)S(1)}, u32[]{:S(2)}, u32[]{:S(2)}) collective-permute-start(bf16[128,128]{1,0:T(8,128)(2,1)S(1)} %pad_maximum_fusion), channel_id=1, source_target_pairs={{0,64},{4,68},{8,72},{12,76},{16,80},{20,84},{24,88},{28,92},{32,9... | collective-permute-start | bytes 98312 | tf_op jit(solution)/shard_map/ppermute | solution.py:361
  27.2 19.4 %collective-permute-start.12 = (bf16[768,128]{1,0:T(8,128)(2,1)S(1)}, bf16[768,128]{1,0:T(8,128)(2,1)S(1)}, u32[]{:S(2)}, u32[]{:S(2)}) collective-permute-start(bf16[768,128]{1,0:T(8,128)(2,1)S(1)} %constant_dynamic-update-slice_fusion.refs_4_), channel_id=1, source_target_pairs={{0,16},{4,20},{8,24},{12,28},{16,0},{20,4},{24,8},{28,12},{32,48},... | collective-permute-start | bytes 589832 | tf_op jit(solution)/shard_map/ppermute | solution.py:361
  31.1 15.7 %collective-permute-start.11 = (bf16[768,128]{1,0:T(8,128)(2,1)S(1)}, bf16[768,128]{1,0:T(8,128)(2,1)S(1)}, u32[]{:S(2)}, u32[]{:S(2)}) collective-permute-start(bf16[768,128]{1,0:T(8,128)(2,1)S(1)} %constant_dynamic-update-slice_fusion.refs_4_), channel_id=1, source_target_pairs={{0,24},{4,28},{8,16},{12,20},{16,8},{20,12},{24,0},{28,4},{32,56},... | collective-permute-start | bytes 589832 | tf_op jit(solution)/shard_map/ppermute | solution.py:361
  31.8 15.0 %collective-permute-start.10 = (bf16[768,128]{1,0:T(8,128)(2,1)S(1)}, bf16[768,128]{1,0:T(8,128)(2,1)S(1)}, u32[]{:S(2)}, u32[]{:S(2)}) collective-permute-start(bf16[768,128]{1,0:T(8,128)(2,1)S(1)} %constant_dynamic-update-slice_fusion.refs_4_), channel_id=1, source_target_pairs={{0,8},{4,12},{8,0},{12,4},{16,24},{20,28},{24,16},{28,20},{32,40},... | collective-permute-start | bytes 589832 | tf_op jit(solution)/shard_map/ppermute | solution.py:361
  43.2 9.8 %collective-permute-start.3 = (bf16[512,128]{1,0:T(8,128)(2,1)S(1)}, bf16[512,128]{1,0:T(8,128)(2,1)S(1)}, u32[]{:S(2)}, u32[]{:S(2)}) collective-permute-start(bf16[512,128]{1,0:T(8,128)(2,1)S(1)} %get-tuple-element.49), channel_id=1, source_target_pairs={{0,4},{4,0},{8,12},{12,8},{16,20},{20,16},{24,28},{28,24},{32,36},... | collective-permute-start | bytes 393224 | tf_op jit(solution)/shard_map/ppermute | solution.py:361
  44.9 9.4 %collective-permute-start.4 = (bf16[512,128]{1,0:T(8,128)(2,1)S(1)}, bf16[512,128]{1,0:T(8,128)(2,1)S(1)}, u32[]{:S(2)}, u32[]{:S(2)}) collective-permute-start(bf16[512,128]{1,0:T(8,128)(2,1)S(1)} %get-tuple-element.50), channel_id=1, source_target_pairs={{0,8},{4,12},{8,0},{12,4},{16,24},{20,28},{24,16},{28,20},{32,40},... | collective-permute-start | bytes 393224 | tf_op jit(solution)/shard_map/ppermute | solution.py:361
  46.6 7.7 %copy-start = (s32[5,4]{0,1:T(4,128)S(1)}, s32[5,4]{0,1:T(4,128)}, u32[]{:S(2)}) copy-start(s32[5,4]{0,1:T(4,128)} %param.7) | copy-start | bytes 244
  46.6 7.7 %collective-permute-start.5 = (bf16[512,128]{1,0:T(8,128)(2,1)S(1)}, bf16[512,128]{1,0:T(8,128)(2,1)S(1)}, u32[]{:S(2)}, u32[]{:S(2)}) collective-permute-start(bf16[512,128]{1,0:T(8,128)(2,1)S(1)} %get-tuple-element.51), channel_id=1, source_target_pairs={{0,12},{4,8},{8,4},{12,0},{16,28},{20,24},{24,20},{28,16},{32,44},... | collective-permute-start | bytes 393224 | tf_op jit(solution)/shard_map/ppermute | solution.py:361
  50.7 7.3 %collective-permute-start.13 = (bf16[160,128]{1,0:T(8,128)(2,1)S(1)}, bf16[160,128]{1,0:T(8,128)(2,1)S(1)}, u32[]{:S(2)}, u32[]{:S(2)}) collective-permute-start(bf16[160,128]{1,0:T(8,128)(2,1)S(1)} %get-tuple-element.59), channel_id=1, source_target_pairs={{0,4},{4,0},{8,12},{12,8},{16,20},{20,16},{24,28},{28,24},{32,36},... | collective-permute-start | bytes 122888 | tf_op jit(solution)/shard_map/ppermute | solution.py:361
  52.4 5.7 %collective-permute-start.14 = (bf16[160,128]{1,0:T(8,128)(2,1)S(1)}, bf16[160,128]{1,0:T(8,128)(2,1)S(1)}, u32[]{:S(2)}, u32[]{:S(2)}) collective-permute-start(bf16[160,128]{1,0:T(8,128)(2,1)S(1)} %get-tuple-element.60), channel_id=1, source_target_pairs={{0,32},{4,36},{8,40},{12,44},{16,48},{20,52},{24,56},{28,60},{32,0... | collective-permute-start | bytes 122888 | tf_op jit(solution)/shard_map/ppermute | solution.py:361
  53.0 5.1 %collective-permute-start.15 = (bf16[160,128]{1,0:T(8,128)(2,1)S(1)}, bf16[160,128]{1,0:T(8,128)(2,1)S(1)}, u32[]{:S(2)}, u32[]{:S(2)}) collective-permute-start(bf16[160,128]{1,0:T(8,128)(2,1)S(1)} %get-tuple-element.61), channel_id=1, source_target_pairs={{0,36},{4,32},{8,44},{12,40},{16,52},{20,48},{24,60},{28,56},{32,4... | collective-permute-start | bytes 122888 | tf_op jit(solution)/shard_map/ppermute | solution.py:361
